TPU v7x, 32 devices: a whole 2x2x4 slice. The times are simulated.
32 devices in a mesh: seq: 16 (over z, y, x), batch: 2 (over core).
Axes of the slice: x: 2, y: 2, z: 4, core: 2. Of those that a mesh axis runs over, the one named last changes fastest.
Arguments:
- inputs: bfloat16 [16, 2048, 1024], P('batch', 'seq'), may hold values from -6 to 6
- segments: int32 [16, 2048], P('batch', 'seq'), may hold values from 0 to 2, as said below
- groups: int32 [16, 2048], P('batch', 'seq'), may hold values from 0 to 7
- group_loss_weight: float32 [8], replicated, may hold values from 0.5 to 2
- attention_norm_gain: bfloat16 [1024], replicated, may hold values from 0.5 to 1.5
- attention_norm_bias: bfloat16 [1024], replicated, may hold values from -1.75 to 1.75
- query_key_value_weight: bfloat16 [1024, 3072], replicated, may hold values from -0.1875 to 0.1875
- query_value_bias: bfloat16 [2, 1024], replicated, may hold values from -1.75 to 1.75
- attention_out_weight: bfloat16 [1024, 1024], replicated, may hold values from -0.75 to 0.75
- attention_out_bias: bfloat16 [1024], replicated, may hold values from -1.75 to 1.75
- feedforward_norm_gain: bfloat16 [1024], replicated, may hold values from 0.099609375 to 1.8984375
- feedforward_norm_bias: bfloat16 [1024], replicated, may hold values from -1.75 to 1.75
- expand_weight: bfloat16 [1024, 4096], replicated, may hold values from -0.1875 to 0.1875
- expand_bias: bfloat16 [4096], replicated, may hold values from -1.75 to 1.75
- contract_weight: bfloat16 [4096, 1024], replicated, may hold values from -0.09375 to 0.09375
- contract_bias: bfloat16 [1024], replicated, may hold values from -1.75 to 1.75
- adapter_down_maps: float32 [2, 1024, 4], replicated, may hold values from -0.1875 to 0.1875
- adapter_up_maps: float32 [2, 4, 1024], replicated, may hold values from -0.375 to 0.375
- down_velocity: float32 [2, 1024, 4], replicated, may hold values from -6144 to 6144
- up_velocity: float32 [2, 4, 1024], replicated, may hold values from -3072 to 3072
- running_down_mean: float32 [2, 1024, 4], replicated, may hold values from -0.1875 to 0.1875
- running_up_mean: float32 [2, 4, 1024], replicated, may hold values from -0.375 to 0.375
- cotangent: bfloat16 [16, 2048, 1024], P('batch', 'seq'), may hold values from -6 to 6
Outputs:
- layer_output: bfloat16 [16, 2048, 1024], P('batch', 'seq')
- input_grad: bfloat16 [16, 2048, 1024], P('batch', 'seq')
- lora_a_grad: float32 [2, 1024, 4], replicated
- lora_b_grad: float32 [2, 4, 1024], replicated
- adapter_down_updated: float32 [2, 1024, 4], replicated
- adapter_up_updated: float32 [2, 4, 1024], replicated
- down_velocity_next: float32 [2, 1024, 4], replicated
- up_velocity_next: float32 [2, 4, 1024], replicated
- updated_down_mean: float32 [2, 1024, 4], replicated
- updated_up_mean: float32 [2, 4, 1024], replicated
- lora_a_copy: bfloat16 [2, 1024, 4], replicated
- lora_b_copy: bfloat16 [2, 4, 1024], replicated
Inputs may be any that keep to these rules, and one draw needn't show every extreme that they name: `segments`: in each row the segment numbers start at 0, never fall and rise by one from one example to the next; every example has 1 to 1024 tokens, the second example of each row has exactly 1024 tokens, and every row holds the same number of examples.
All inputs are finite; a program needn't handle non-finite values.
Results may differ from a plain program's by a relative error of at most 0.019.
Values may be sent and summed in bfloat16 or wider, within the bound.
No kernel may reach another device: no remote copies, remote signals or barrier semaphores. Data moves between devices by JAX's collectives and lax.ppermute only.
A program may use at most 576 MiB of HBM per device.

v0:
```python
import functools

import jax
import jax.numpy as jnp
from jax import lax
from jax.experimental import pallas as pl
from jax.experimental.pallas import tpu as pltpu
from jax.sharding import PartitionSpec as P

HEADS = 16
EXAMPLE_MAX = 1024
SEGMENT_SLOTS = 8
LANES = 128
QUERY_BLOCK = 256
TOKEN_BLOCK = 256
HIDDEN_BLOCK = 1024
AHEAD = 3
VMEM_BYTES = 60 * 1024 * 1024

norm_eps = 1e-05
adapter_scale = 8.0
learning_step_size = 3e-05
velocity_factor = 0.5
mean_decay_factor = 0.5
masked_score = -1e30
score_scale = 0.125


def matmul_rows(left_side, right_side):
    return lax.dot_general(
        left_side, right_side, (((1,), (0,)), ((), ())), preferred_element_type=jnp.float32
    )


def matmul_back(left_side, right_side):
    return lax.dot_general(
        left_side, right_side, (((1,), (1,)), ((), ())), preferred_element_type=jnp.float32
    )


def matmul_over(left_side, right_side):
    return lax.dot_general(
        left_side, right_side, (((0,), (0,)), ((), ())), preferred_element_type=jnp.float32
    )


def gather_kernel(cores, with_codes, core_ref, *refs):
    stripes, codes, out_ref = refs[:cores], refs[cores:-1], refs[-1]
    came_from = lax.rem(core_ref[0] - pl.program_id(0) + cores, cores)
    stripe, width = stripes[0].shape[1:]
    for by in range(cores):

        @pl.when(came_from == by)
        def _(by=by):
            for group in range(width // LANES):
                rows = pl.ds(group * stripe, stripe)
                out_ref[:, rows, :] = stripes[by][:, :, group * LANES : (group + 1) * LANES]
            if with_codes:
                out_ref[:, width // LANES * stripe :, :] = codes[by][...]


def gather_stripes(x, codes=None):
    cores = lax.axis_size("batch")
    core = lax.axis_index("batch")
    rows, tokens, width = x.shape
    stripe = tokens // cores
    parts, extra = [x], [] if codes is None else [codes]
    for by in range(1, cores):
        goes = lax.rem(core + by, cores)
        parts.append(from_core(lax.dynamic_slice_in_dim(x, goes * stripe, stripe, 1), by))
        extra += [] if codes is None else [from_core(codes, by)]
    deep = width // LANES * stripe + sum(c.shape[1] for c in extra[:1])
    whole = pl.BlockSpec((rows, stripe, width), lambda c, core: (0, 0, 0))
    return pl.pallas_call(
        functools.partial(gather_kernel, cores, bool(extra)),
        grid_spec=pltpu.PrefetchScalarGridSpec(
            num_scalar_prefetch=1,
            grid=(cores,),
            in_specs=[pl.BlockSpec((rows, stripe, width), lambda c, core: (0, core[0], 0))]
            + [whole] * (cores - 1)
            + [pl.BlockSpec(c.shape, lambda c, core: (0, 0, 0)) for c in extra],
            out_specs=pl.BlockSpec((rows, deep, LANES), lambda c, core: (c, 0, 0)),
        ),
        out_shape=jax.ShapeDtypeStruct((rows * cores, deep, LANES), x.dtype),
        compiler_params=pltpu.CompilerParams(vmem_limit_bytes=32 * 1024 * 1024),
        name="gather_stripes",
    )(core[None], *parts, *extra)


def spread_kernel(cores, core_ref, *refs):
    came_from = lax.rem(core_ref[0] - pl.program_id(0) + cores, cores)
    for by in range(cores):

        @pl.when(came_from == by)
        def _(by=by):
            refs[-1][...] = refs[by][...]


def spread_stripes(y):
    cores = lax.axis_size("batch")
    core = lax.axis_index("batch")
    rows, stripe, width = y.shape[0] // cores, *y.shape[1:]
    parts = [y]
    for by in range(1, cores):
        goes = lax.rem(core + by, cores)
        parts.append(from_core(lax.dynamic_slice_in_dim(y, goes * rows, rows, 0), by))
    block = (rows, stripe, width)
    return pl.pallas_call(
        functools.partial(spread_kernel, cores),
        grid_spec=pltpu.PrefetchScalarGridSpec(
            num_scalar_prefetch=1,
            grid=(cores,),
            in_specs=[pl.BlockSpec(block, lambda c, core: (core[0], 0, 0))]
            + [pl.BlockSpec(block, lambda c, core: (0, 0, 0))] * (cores - 1),
            out_specs=pl.BlockSpec(block, lambda c, core: (0, c, 0)),
        ),
        out_shape=jax.ShapeDtypeStruct((rows, stripe * cores, width), y.dtype),
        compiler_params=pltpu.CompilerParams(vmem_limit_bytes=32 * 1024 * 1024),
        name="spread_stripes",
    )(core[None], *parts)


def rows_home(y):
    return lax.all_to_all(y, "seq", 0, 0, tiled=True)


def rows_back(y):
    ring = lax.axis_size("seq")
    y = y.reshape(ring, y.shape[0] // ring, y.shape[1])
    return lax.all_to_all(y, "seq", 0, 0, tiled=True)


def tokens_of(ref, stripe, width):
    groups = []
    for group in range(width // LANES):
        rows = slice(group * stripe, (group + 1) * stripe)
        groups.append(jnp.concatenate([ref[c, rows, :] for c in range(ref.shape[0])], axis=0))
    return jnp.concatenate(groups, axis=1)


def from_core(x, by):
    cores = lax.axis_size("batch")
    return lax.ppermute(x, "batch", [(i, (i + by) % cores) for i in range(cores)])


def sum_over(x, axis, low, high):
    size = lax.axis_size(axis)
    terms = [x]
    for by in range(1, 1 << (high - low)):
        terms.append(lax.ppermute(x, axis, [(i, i ^ (by << low)) for i in range(size)]))
    while len(terms) > 1:
        terms = [terms[i] + terms[i + 1] for i in range(0, len(terms), 2)]
    return terms[0]


def lane_masks(dtype):
    lane = lax.broadcasted_iota(jnp.int32, (1, LANES), 1)
    first = (lane < LANES // 2).astype(jnp.float32).astype(dtype)
    second = (lane >= LANES // 2).astype(jnp.float32).astype(dtype)
    return first, second


def slot_row():
    lane = lax.broadcasted_iota(jnp.int32, (1, LANES), 1)
    return (lax.rem(lane, LANES // 2) < SEGMENT_SLOTS).astype(jnp.float32).astype(jnp.bfloat16)


def block_of(ref, index):
    return ref[pl.ds(index * QUERY_BLOCK, QUERY_BLOCK), :]


def attend_kernel(cores, reach, *refs):
    far_ref, query_ref = refs[:2]
    key_refs = refs[2 : 2 + cores]
    value_refs = refs[2 + cores : 2 + 2 * cores]
    mark_ref, causal_ref, out_ref, log_ref, key_heads, turned_values = refs[2 + 2 * cores :]
    slots = slot_row()
    heads = lane_masks(jnp.bfloat16)
    half = LANES // 2
    blocks = query_ref.shape[0] // QUERY_BLOCK
    tile = cores * QUERY_BLOCK
    scale = jnp.asarray(score_scale, jnp.bfloat16)
    excluded = jnp.asarray(masked_score, jnp.bfloat16)
    for h in range(2):
        turned_values[h, half:, :] = jnp.ones_like(turned_values[h, half:, :])
    for j in range(blocks):
        for k in range(cores):
            key = block_of(key_refs[k], j)
            key_mark = slots - block_of(mark_ref, k * blocks + j)
            turned = block_of(value_refs[k], j).T
            at = pl.ds(j * tile + k * QUERY_BLOCK, QUERY_BLOCK)
            for h, own in enumerate(heads):
                key_heads[h, at, :] = key * own + key_mark * heads[1 - h]
                turned_values[h, :half, at] = turned[h * half : (h + 1) * half]

    def scores_of(n, h, start):
        query_head = block_of(query_ref, n) * scale * heads[h] + block_of(mark_ref, n) * excluded * heads[1 - h]
        scores = []
        for j in range(start, n + 1):
            score = matmul_back(key_heads[h, pl.ds(j * tile, tile), :], query_head)
            scores.append(score + causal_ref[...] if j == n else score)
        return scores

    def finish(n, h, start, scores):
        rows = pl.ds(n * QUERY_BLOCK, QUERY_BLOCK)
        top = scores[0]
        for score in scores[1:]:
            top = jnp.maximum(top, score)
        top = jnp.max(top, axis=0, keepdims=True)
        weights = [jnp.exp(score - top).astype(jnp.bfloat16) for score in scores]
        keys = pl.ds(start * tile, (n + 1 - start) * tile)
        out = matmul_rows(turned_values[h, :, keys], jnp.concatenate(weights))
        total = out[half : half + 1]
        log_ref[h : h + 1, rows] = top + jnp.log(total)
        return out[:half] / total

    def every(skipped):
        waiting, outs = [], []
        units = []
        for n in range(blocks):
            start = max(0, n - reach) + (skipped and n == blocks - 1)
            units += [(n, h, start) for h in range(2)]
        for unit in units + [None] * AHEAD:
            if unit is not None:
                waiting.append((unit, scores_of(*unit)))
            if len(waiting) > AHEAD or unit is None:
                done, scores = waiting.pop(0)
                outs.append(finish(*done, scores))
                if len(outs) == 2:
                    rows = pl.ds(done[0] * QUERY_BLOCK, QUERY_BLOCK)
                    out_ref[rows, :] = jnp.concatenate(outs).T.astype(out_ref.dtype)
                    outs = []

    either_way(every, far_ref, blocks > reach)


def either_way(every, far_ref, can_skip):
    if not can_skip:
        every(False)
        return
    pl.when(far_ref[0] == 1)(functools.partial(every, False))
    pl.when(far_ref[0] != 1)(functools.partial(every, True))


def spread(wide):
    high = wide.astype(jnp.bfloat16)
    return high, (wide - high.astype(jnp.float32)).astype(jnp.bfloat16)


def pull_kernel(cores, reach, *refs):
    far_ref, query_ref, grad_ref, out_ref, log_ref = refs[:5]
    key_refs = refs[5 : 5 + cores]
    value_refs = refs[5 + cores : 5 + 2 * cores]
    mark_ref, causal_ref = refs[5 + 2 * cores : 7 + 2 * cores]
    outs = refs[7 + 2 * cores :]
    slots = slot_row()
    excluded = jnp.asarray(masked_score, jnp.bfloat16)
    grad_query_ref = outs[0]
    grad_key_refs = outs[1 : 1 + cores]
    grad_value_refs = outs[1 + cores : 1 + 2 * cores]
    (
        query_heads, key_heads, value_heads, turned_queries, turned_keys, turned_grads,
        turned_sums, dots,
    ) = outs[1 + 2 * cores :]
    heads = lane_masks(jnp.bfloat16)
    half = LANES // 2
    blocks = query_ref.shape[0] // QUERY_BLOCK
    tile = cores * QUERY_BLOCK
    scale = jnp.asarray(score_scale, jnp.bfloat16)
    lane = lax.broadcasted_iota(jnp.int32, (8, LANES), 1)
    row = lax.broadcasted_iota(jnp.int32, (8, LANES), 0)
    chooser = (lane // half == row).astype(jnp.float32).astype(jnp.bfloat16)
    for n in range(blocks):
        rows = pl.ds(n * QUERY_BLOCK, QUERY_BLOCK)
        query = query_ref[rows, :] * scale
        grad = grad_ref[rows, :]
        high, rest = spread(grad.astype(jnp.float32) * out_ref[rows, :].astype(jnp.float32))
        dots[:, rows] = matmul_back(chooser, high) + matmul_back(chooser, rest)
        turned_queries[:, rows] = query.T
        turned_grads[:, rows] = grad.T
        for h, own in enumerate(heads):
            query_heads[h, rows, :] = query * own + mark_ref[rows, :] * excluded * heads[1 - h]
        for k in range(cores):
            key = block_of(key_refs[k], n)
            key_mark = slots - block_of(mark_ref, k * blocks + n)
            value = block_of(value_refs[k], n)
            at = pl.ds(n * tile + k * QUERY_BLOCK, QUERY_BLOCK)
            turned_keys[:, at] = key.T
            for h, own in enumerate(heads):
                key_heads[h, at, :] = key * own + key_mark * heads[1 - h]
                value_heads[h, at, :] = value * own
    turned_sums[...] = jnp.zeros_like(turned_sums)

    def products(j, n, h):
        keys = pl.ds(j * tile, tile)
        rows = pl.ds(n * QUERY_BLOCK, QUERY_BLOCK)
        score = matmul_back(key_heads[h, keys, :], query_heads[h, rows, :])
        change = matmul_back(value_heads[h, keys, :], grad_ref[rows, :])
        return score, change

    def weigh(j, n, h, score, change):
        rows = pl.ds(n * QUERY_BLOCK, QUERY_BLOCK)
        if n == j:
            score = score + causal_ref[...]
        weight = jnp.exp(score - log_ref[h : h + 1, rows])
        change = (weight * (change - dots[h : h + 1, rows])).astype(jnp.bfloat16)
        return weight.astype(jnp.bfloat16), change

    def finish(j, h, members):
        part = pl.ds(h * half, half)
        keys = pl.ds(j * tile, tile)
        rows = pl.ds(members[0][0] * QUERY_BLOCK, len(members) * QUERY_BLOCK)
        weights = jnp.concatenate([m[1] for m in members], axis=1)
        changes = jnp.concatenate([m[2] for m in members], axis=1)
        turned_sums[part, rows] += matmul_rows(turned_keys[part, keys], changes)
        return (
            matmul_back(turned_queries[part, rows], changes),
            matmul_back(turned_grads[part, rows], weights),
        )

    def every(skipped):
        units = []
        for j in range(blocks):
            last = min(blocks - 1, j + reach)
            if skipped and j + reach == blocks - 1:
                last -= 1
            units += [(j, n, h, n == last) for h in range(2) for n in range(j, last + 1)]
        waiting, members, sums = [], [], []
        for unit in units + [None] * AHEAD:
            if unit is not None:
                waiting.append((unit, products(*unit[:3])))
            if len(waiting) > AHEAD or unit is None:
                (j, n, h, closing), pair = waiting.pop(0)
                members.append((n, *weigh(j, n, h, *pair)))
                if closing:
                    sums.append(finish(j, h, members))
                    members = []
                if len(sums) == 2:
                    for out_refs, which in ((grad_key_refs, 0), (grad_value_refs, 1)):
                        both = jnp.concatenate([s[which] for s in sums]).T.astype(jnp.bfloat16)
                        for k in range(cores):
                            out_refs[k][pl.ds(j * QUERY_BLOCK, QUERY_BLOCK), :] = both[
                                k * QUERY_BLOCK : (k + 1) * QUERY_BLOCK
                            ]
                    sums = []

    either_way(every, far_ref, blocks > reach)
    grad_query_ref[...] = (turned_sums[...] * score_scale).T.astype(jnp.bfloat16)


def standardized(values):
    average = jnp.mean(values, axis=-1, keepdims=True)
    centred = values - average
    spread_inverse = lax.rsqrt(jnp.mean(centred * centred, axis=-1, keepdims=True) + norm_eps)
    return centred * spread_inverse, spread_inverse


def norm_pull(grad, shaped, spread_inverse):
    mean_grad = jnp.mean(grad, axis=-1, keepdims=True)
    mean_product = jnp.mean(grad * shaped, axis=-1, keepdims=True)
    return spread_inverse * (grad - mean_grad - shaped * mean_product)


def enter_kernel(
    stripe, kinds, x_ref, gain_ref, shift_ref, bias_ref, down_ref, up_ref, *refs
):
    weight_refs, out_refs = refs[: len(kinds)], refs[len(kinds) :]
    width = out_refs[0].shape[1]
    shaped, _ = standardized(tokens_of(x_ref, stripe, width).astype(jnp.float32))
    normed = (shaped * gain_ref[...] + shift_ref[...]).astype(jnp.bfloat16)
    lora = matmul_rows(normed, down_ref[...]).astype(jnp.bfloat16)
    if len(out_refs) > len(kinds):
        out_refs[-1][...] = lora
    for kind, weight_ref, out_ref in zip(kinds, weight_refs, out_refs):
        out = matmul_rows(normed, weight_ref[...])
        if kind != 1:
            j = kind // 2
            out = out + matmul_rows(lora, up_ref[:, j * width : (j + 1) * width])
            out = out + bias_ref[j : j + 1, :]
        out_ref[...] = out.astype(jnp.bfloat16)


root_two_over_pi = 0.7978845608028654
cubic = 0.044715


def middle_kernel(
    stripe, x_ref, attended_ref, cotangent_ref,
    out_bias_ref, gain_ref, shift_ref, expand_bias_ref, contract_bias_ref,
    out_weight_from, expand_from, contract_from,
    result_ref, grad_middle_ref, grad_attended_ref,
    out_weight_ref, expand_ref, contract_ref, arrivals,
):
    width, hidden = expand_ref.shape
    parts = [slice(at, at + HIDDEN_BLOCK) for at in range(0, hidden, HIDDEN_BLOCK)]
    copies = [pltpu.make_async_copy(out_weight_from, out_weight_ref, arrivals.at[0])]
    for i, part in enumerate(parts):
        for which, source, to in (
            (1, expand_from.at[:, part], expand_ref.at[:, part]),
            (2, contract_from.at[part, :], contract_ref.at[part, :]),
        ):
            copies.append(pltpu.make_async_copy(source, to, arrivals.at[2 * i + which]))

    def block(first):
        if first:
            for copy in copies:
                copy.start()
            copies[0].wait()
        middle = (
            tokens_of(x_ref, stripe, width).astype(jnp.float32)
            + matmul_rows(attended_ref[...], out_weight_ref[...])
            + out_bias_ref[...]
        )
        shaped, spread_inverse = standardized(middle)
        normed = (shaped * gain_ref[...] + shift_ref[...]).astype(jnp.bfloat16)
        grad_low = tokens_of(cotangent_ref, stripe, width)
        grad_out = grad_low.astype(jnp.float32)
        result = middle + contract_bias_ref[...]
        grad_normed = jnp.zeros_like(middle)
        for i, part in enumerate(parts):
            if first:
                copies[2 * i + 1].wait()
                copies[2 * i + 2].wait()
            pre = matmul_rows(normed, expand_ref[:, part]) + expand_bias_ref[:, part]
            grad_act = matmul_back(grad_low, contract_ref[part, :])
            square = pre * pre
            bent = jnp.tanh(root_two_over_pi * pre * (1.0 + cubic * square))
            upper = 0.5 + 0.5 * bent
            act = (pre * upper).astype(jnp.bfloat16)
            slope = upper + (0.5 * root_two_over_pi) * pre * (1.0 - bent * bent) * (
                1.0 + (3.0 * cubic) * square
            )
            grad_pre = (grad_act * slope).astype(jnp.bfloat16)
            result = result + matmul_rows(act, contract_ref[part, :])
            grad_normed = grad_normed + matmul_back(grad_pre, expand_ref[:, part])
        result_ref[...] = result.astype(jnp.bfloat16)
        grad_middle = grad_out + norm_pull(grad_normed * gain_ref[...], shaped, spread_inverse)
        grad_middle_low = grad_middle.astype(jnp.bfloat16)
        grad_middle_ref[...] = grad_middle_low
        grad_attended = matmul_back(grad_middle_low, out_weight_ref[...])
        grad_attended_ref[...] = grad_attended.astype(jnp.bfloat16)

    pl.when(pl.program_id(0) == 0)(functools.partial(block, True))
    pl.when(pl.program_id(0) != 0)(functools.partial(block, False))


def total(parts):
    out = parts[0][...].astype(jnp.float32)
    for part in parts[1:]:
        out = out + part[...].astype(jnp.float32)
    return out.astype(jnp.bfloat16)


def adapt_kernel(
    stripe, cores, x_ref, gain_ref, shift_ref, up_ref, lora_ref, grad_query_ref, *refs
):
    value_refs = refs[:cores]
    grad_lora_ref, down_sum_ref, up_sum_ref = refs[cores:]
    slots = down_sum_ref.shape[0]

    @pl.when(pl.program_id(0) == 0)
    def _():
        down_sum_ref[...] = jnp.zeros_like(down_sum_ref)
        up_sum_ref[...] = jnp.zeros_like(up_sum_ref)

    width = grad_query_ref.shape[1]
    grad_query = grad_query_ref[...]
    grad_value = total(value_refs)
    shaped, _ = standardized(tokens_of(x_ref, stripe, width).astype(jnp.float32))
    normed = (shaped * gain_ref[...] + shift_ref[...]).astype(jnp.bfloat16)
    grad_lora = matmul_back(grad_query, up_ref[:, :width]) + matmul_back(
        grad_value, up_ref[:, width:]
    )
    grad_lora = grad_lora.astype(jnp.bfloat16)
    grad_lora_ref[...] = grad_lora
    lora = lora_ref[...]
    down_sum_ref[...] += matmul_over(grad_lora, normed)[:slots]
    up_sum_ref[:, :width] += matmul_over(lora, grad_query)[:slots]
    up_sum_ref[:, width:] += matmul_over(lora, grad_value)[:slots]


def leave_kernel(
    stripe, cores, x_ref, gain_ref, weight_ref, down_ref, grad_lora_ref, grad_middle_ref,
    grad_query_ref, *refs,
):
    key_refs, value_refs, grad_ref = refs[:cores], refs[cores : 2 * cores], refs[-1]
    width = grad_query_ref.shape[1]
    shaped, spread_inverse = standardized(tokens_of(x_ref, stripe, width).astype(jnp.float32))
    grad_normed = (
        matmul_back(grad_query_ref[...], weight_ref[:, :width])
        + matmul_back(total(key_refs), weight_ref[:, width : 2 * width])
        + matmul_back(total(value_refs), weight_ref[:, 2 * width :])
        + matmul_back(grad_lora_ref[...], down_ref[...])
    )
    grad = norm_pull(grad_normed * gain_ref[...], shaped, spread_inverse)
    grad_ref[...] = (grad_middle_ref[...].astype(jnp.float32) + grad).astype(jnp.bfloat16)


def tile(x):
    def spec(tokens):
        share = x.shape[0] * min(TOKEN_BLOCK, tokens) // tokens
        return pl.BlockSpec((share, *x.shape[1:]), lambda i: (i,) + (0,) * (len(x.shape) - 1))

    return x, spec


def whole(x):
    def spec(tokens):
        kept = pl.Buffered(1)
        return pl.BlockSpec(x.shape, lambda i: (0,) * len(x.shape), pipeline_mode=kept)

    return x, spec


def columns(x, which, width):
    def spec(tokens):
        kept = pl.Buffered(1)
        return pl.BlockSpec((x.shape[0], width), lambda i: (0, which), pipeline_mode=kept)

    return x, spec


def in_place(x):
    return x, lambda tokens: pl.BlockSpec(memory_space=pl.ANY)


def over_tokens(kernel, name, tokens, operands, outs, sums, flops, scratch=()):
    moved = sum(x.size * x.dtype.itemsize for x in [*(x for x, _ in operands), *outs, *sums])
    return pl.pallas_call(
        kernel,
        grid=(tokens // min(TOKEN_BLOCK, tokens),),
        in_specs=[spec(tokens) for _, spec in operands],
        out_specs=[tile(x)[1](tokens) for x in outs]
        + [pl.BlockSpec(x.shape, lambda i: (0, 0)) for x in sums],
        out_shape=[*outs, *sums],
        scratch_shapes=list(scratch),
        compiler_params=pltpu.CompilerParams(
            dimension_semantics=("arbitrary",), vmem_limit_bytes=VMEM_BYTES
        ),
        cost_estimate=pl.CostEstimate(flops=flops, bytes_accessed=moved, transcendentals=0),
        name=name,
    )(*(x for x, _ in operands))


def attention_calls(tokens, width, cores, reach):
    pair = pl.BlockSpec((tokens, LANES), lambda p, far: (0, p))
    marks = pl.BlockSpec((cores * tokens, LANES), lambda p, far: (0, 0))
    causal = pl.BlockSpec((cores * QUERY_BLOCK, QUERY_BLOCK), lambda p, far: (0, 0))
    logs = pl.BlockSpec((8, tokens), lambda p, far: (p, 0))
    grid = (width // LANES,)
    blocks = tokens // QUERY_BLOCK
    pairs = sum(min(n, reach) + 1 for n in range(blocks)) * cores * QUERY_BLOCK**2 * HEADS
    head_width = width // HEADS
    low = jax.ShapeDtypeStruct((tokens, width), jnp.bfloat16)
    log_rows = jax.ShapeDtypeStruct((8 * grid[0], tokens), jnp.float32)
    params = pltpu.CompilerParams(
        dimension_semantics=("arbitrary",), vmem_limit_bytes=VMEM_BYTES
    )
    low_scratch = functools.partial(pltpu.VMEM, dtype=jnp.bfloat16)
    forward = pl.pallas_call(
        functools.partial(attend_kernel, cores, reach),
        grid_spec=pltpu.PrefetchScalarGridSpec(
            num_scalar_prefetch=1,
            grid=grid,
            in_specs=[pair] * (1 + 2 * cores) + [marks, causal],
            out_specs=[pair, logs],
            scratch_shapes=[
                low_scratch((2, cores * tokens, LANES)),
                low_scratch((2, LANES // 2 + 16, cores * tokens)),
            ],
        ),
        out_shape=[low, log_rows],
        compiler_params=params,
        cost_estimate=pl.CostEstimate(
            flops=4 * pairs * head_width,
            bytes_accessed=2 * tokens * width * (2 + 2 * cores),
            transcendentals=pairs,
        ),
        name="attend",
    )
    backward = pl.pallas_call(
        functools.partial(pull_kernel, cores, reach),
        grid_spec=pltpu.PrefetchScalarGridSpec(
            num_scalar_prefetch=1,
            grid=grid,
            in_specs=[pair, pair, pair, logs] + [pair] * (2 * cores) + [marks, causal],
            out_specs=[pair] * (1 + 2 * cores),
            scratch_shapes=[
                low_scratch((2, tokens, LANES)),
                low_scratch((2, cores * tokens, LANES)),
                low_scratch((2, cores * tokens, LANES)),
                low_scratch((LANES, tokens)),
                low_scratch((LANES, cores * tokens)),
                low_scratch((LANES, tokens)),
                pltpu.VMEM((LANES, tokens), jnp.float32),
                pltpu.VMEM((8, tokens), jnp.float32),
            ],
        ),
        out_shape=[low] * (1 + 2 * cores),
        compiler_params=params,
        cost_estimate=pl.CostEstimate(
            flops=10 * pairs * head_width,
            bytes_accessed=2 * tokens * width * (4 + 4 * cores),
            transcendentals=pairs,
        ),
        name="pull",
    )
    return forward, backward


def body(
    inputs,
    segments,
    groups,
    group_loss_weight,
    attention_norm_gain,
    attention_norm_bias,
    query_key_value_weight,
    query_value_bias,
    attention_out_weight,
    attention_out_bias,
    feedforward_norm_gain,
    feedforward_norm_bias,
    expand_weight,
    expand_bias,
    contract_weight,
    contract_bias,
    adapter_down_maps,
    adapter_up_maps,
    down_velocity,
    up_velocity,
    running_down_mean,
    running_up_mean,
    cotangent,
):
    rows_here, tokens_here, width = inputs.shape
    cores = lax.axis_size("batch")
    ring = lax.axis_size("seq")
    assert rows_here * cores == ring
    stripe = tokens_here // cores
    tokens = ring * stripe
    span = QUERY_BLOCK * cores
    reach = -(-(EXAMPLE_MAX - 1) // span)
    rank = adapter_down_maps.shape[-1]
    core = lax.axis_index("batch")
    attend, pull = attention_calls(tokens, width, cores, reach)

    assert tokens_here == LANES
    marks = jnp.broadcast_to(segments[:, None, :], (rows_here, 8, tokens_here))
    x = rows_home(gather_stripes(inputs, marks.astype(jnp.bfloat16)))
    chooser = groups[..., None] == jnp.arange(group_loss_weight.shape[0], dtype=jnp.int32)
    token_weight = jnp.sum(jnp.where(chooser, group_loss_weight, 0.0), axis=-1, keepdims=True)
    weighted = (cotangent.astype(jnp.float32) * token_weight).astype(jnp.bfloat16)
    stripes = gather_stripes(weighted)
    place = jnp.arange(QUERY_BLOCK, dtype=jnp.int32)
    place = tokens_here * (place // stripe) + place % stripe
    after = []
    for by in range(cores):
        key_place = place + stripe * lax.rem(core - by + cores, cores)
        after.append(key_place[:, None] > (place + stripe * core)[None, :])
    causal = jnp.where(jnp.concatenate(after), masked_score, 0.0).astype(jnp.float32)

    def row_of(vector):
        return vector.astype(jnp.float32).reshape(1, -1)

    first_gain, first_shift = row_of(attention_norm_gain), row_of(attention_norm_bias)
    second_gain, second_shift = row_of(feedforward_norm_gain), row_of(feedforward_norm_bias)
    pad = LANES - 2 * rank
    down_packed = jnp.concatenate([adapter_down_maps[0], adapter_down_maps[1]], axis=1)
    down_packed = jnp.pad(down_packed, ((0, 0), (0, pad))).astype(jnp.bfloat16)
    up_packed = jnp.concatenate(
        [
            jnp.pad(adapter_up_maps[0], ((0, rank + pad), (0, 0))),
            jnp.pad(adapter_up_maps[1], ((rank, pad), (0, 0))),
        ],
        axis=1,
    )
    up_packed = (adapter_scale * up_packed).astype(jnp.bfloat16)
    value_bias = query_value_bias.astype(jnp.float32)
    out_bias, up_bias, down_bias = map(row_of, (attention_out_bias, expand_bias, contract_bias))
    (
        x, stripes, causal, first_gain, first_shift, second_gain, second_shift,
        value_bias, out_bias, up_bias, down_bias, down_packed, up_packed,
    ) = lax.optimization_barrier(
        (
            x, stripes, causal, first_gain, first_shift, second_gain, second_shift,
            value_bias, out_bias, up_bias, down_bias, down_packed, up_packed,
        )
    )
    cotangent_home = rows_home(stripes)
    row_segments = x[:, width // LANES * stripe, :].astype(jnp.int32)
    parts = row_segments.reshape(ring, cores, stripe)
    turns = [lax.rem(core - by + cores, cores) for by in range(cores)]
    parts = [lax.dynamic_index_in_dim(parts, turn, 1, keepdims=False) for turn in turns]
    slot = jnp.arange(LANES, dtype=jnp.int32) % (LANES // 2)
    marks = jnp.concatenate(parts).reshape(cores * tokens, 1) == slot[None, :]
    marks = marks.astype(jnp.bfloat16)
    row_segments = row_segments.reshape(ring * tokens_here)
    blocks = tokens // QUERY_BLOCK
    last = max(0, blocks - 1 - reach)
    far = row_segments[span * (last + 1) - 1] >= row_segments[span * (blocks - 1)]
    far = far.astype(jnp.int32)[None]

    low = jax.ShapeDtypeStruct((tokens, width), jnp.bfloat16)

    def enter(kinds, extra):
        return over_tokens(
            functools.partial(enter_kernel, stripe, kinds),
            "enter",
            tokens,
            [tile(x), whole(first_gain), whole(first_shift), whole(value_bias)]
            + [whole(down_packed), whole(up_packed)]
            + [columns(query_key_value_weight, kind, width) for kind in kinds],
            [low] * len(kinds) + extra,
            [],
            2 * len(kinds) * tokens * width * width,
        )

    keys, values = enter((1, 2), [])
    all_keys = [keys] + [from_core(keys, by) for by in range(1, cores)]
    all_values = [values] + [from_core(values, by) for by in range(1, cores)]
    queries, lora = enter((0,), [jax.ShapeDtypeStruct((tokens, LANES), jnp.bfloat16)])
    attended, log_total = attend(far, queries, *all_keys, *all_values, marks, causal)

    hidden = expand_weight.shape[1]
    layer_result, grad_middle, grad_attended = over_tokens(
        functools.partial(middle_kernel, stripe),
        "middle",
        tokens,
        [tile(x), tile(attended), tile(cotangent_home)]
        + [whole(v) for v in (out_bias, second_gain, second_shift, up_bias, down_bias)]
        + [in_place(w) for w in (attention_out_weight, expand_weight, contract_weight)],
        [low, low, low],
        [],
        4 * tokens * width * (width + 2 * hidden),
        [pltpu.VMEM(w.shape, w.dtype) for w in (attention_out_weight, expand_weight, contract_weight)]
        + [pltpu.SemaphoreType.DMA((1 + 2 * (hidden // HIDDEN_BLOCK),))],
    )
    layer_out = rows_back(layer_result)

    pulled = pull(
        far,
        queries,
        grad_attended,
        attended,
        log_total,
        *all_keys,
        *all_values,
        marks,
        causal,
    )

    layer_out, pulled = lax.optimization_barrier((layer_out, pulled))
    layer_out = spread_stripes(layer_out)

    def owned(parts):
        return [parts[0]] + [from_core(parts[by], -by) for by in range(1, cores)]

    sums = [
        jax.ShapeDtypeStruct((2 * rank, width), jnp.float32),
        jax.ShapeDtypeStruct((2 * rank, 2 * width), jnp.float32),
    ]
    owned_values = owned(pulled[1 + cores :])
    owned_keys = owned(pulled[1 : 1 + cores])
    grad_lora, down_sum, up_sum = over_tokens(
        functools.partial(adapt_kernel, stripe, cores),
        "adapt",
        tokens,
        [tile(x), whole(first_gain), whole(first_shift), whole(up_packed), tile(lora)]
        + [tile(part) for part in (pulled[0], *owned_values)],
        [jax.ShapeDtypeStruct((tokens, LANES), jnp.bfloat16)],
        sums,
        1024 * tokens * width,
    )
    up_parts = [
        adapter_scale * up_sum[j * rank : (j + 1) * rank, j * width : (j + 1) * width]
        for j in range(2)
    ]
    adapter_sums = jnp.concatenate([*up_parts, down_sum], axis=0)
    bits = ring.bit_length() - 1
    adapter_sums = sum_over(adapter_sums, "seq", max(0, bits - 2), bits)
    (input_grad,) = over_tokens(
        functools.partial(leave_kernel, stripe, cores),
        "leave",
        tokens,
        [tile(x), whole(first_gain), whole(query_key_value_weight), whole(down_packed)]
        + [tile(part) for part in (grad_lora, grad_middle, pulled[0], *owned_keys, *owned_values)],
        [low],
        [],
        6 * tokens * width * width,
    )
    input_grad, adapter_sums = lax.optimization_barrier((input_grad, adapter_sums))
    input_grad = spread_stripes(rows_back(input_grad))
    for low in range(max(0, bits - 4), -1, -2) if bits > 2 else ():
        adapter_sums = sum_over(adapter_sums, "seq", low, min(low + 2, bits - 2))
    adapter_sums = sum_over(adapter_sums, "batch", 0, cores.bit_length() - 1)
    adapter_sums = adapter_sums.reshape(2, 2, rank, width)
    up_map_gradient = adapter_sums[0]
    down_map_gradient = jnp.transpose(adapter_sums[1], (0, 2, 1))

    down_velocity_next = velocity_factor * down_velocity + down_map_gradient
    up_velocity_next = velocity_factor * up_velocity + up_map_gradient
    adapter_down_updated = adapter_down_maps - learning_step_size * (
        down_map_gradient + velocity_factor * down_velocity_next
    )
    adapter_up_updated = adapter_up_maps - learning_step_size * (
        up_map_gradient + velocity_factor * up_velocity_next
    )
    updated_down_mean = (
        mean_decay_factor * running_down_mean + (1.0 - mean_decay_factor) * adapter_down_updated
    )
    updated_up_mean = (
        mean_decay_factor * running_up_mean + (1.0 - mean_decay_factor) * adapter_up_updated
    )
    return (
        layer_out,
        input_grad,
        down_map_gradient,
        up_map_gradient,
        adapter_down_updated,
        adapter_up_updated,
        down_velocity_next,
        up_velocity_next,
        updated_down_mean,
        updated_up_mean,
        adapter_down_updated.astype(jnp.bfloat16),
        adapter_up_updated.astype(jnp.bfloat16),
    )


def solution(mesh):
    tokens = P("batch", "seq", None)
    codes = P("batch", "seq")
    return jax.shard_map(
        body,
        mesh=mesh,
        in_specs=(tokens, codes, codes) + (P(),) * 19 + (tokens,),
        out_specs=(tokens, tokens) + (P(),) * 10,
        check_vma=False,
    )
```

profile of v0, /device:TPU:0, one launch (start us, length us, event | category | flops | bytes accessed | tf_op | source)
XLA Modules:
  0.0 347.3 jit_solution(4074885360370395960)
XLA Ops:
  0.7 1.5 constant_dynamic-slice_fusion.5
  2.8 2.2 collective-permute-done.1.refs_3_
  5.0 1.6 gather_stripes.2
  6.7 8.4 %all-to-all-start = ((bf16[16,520,128]{2,1,0:T(8,128)(2,1)}), bf16[16,520,128]{2,1,0:T(8,128)(2,1)}, u32[]{:S(2)}, u32[]{:S(2)}) async-start(bf16[16,520,128]{2,1,0:T(8,128)(2,1)} %gather_stripes.2), calls=%async_computation | async-start | bytes 4259840 | tf_op jit(solution)/shard_map/all_to_all | solution.py:124
  15.2 2.0 multiply_convert_fusion.refs_0_
  28.0 31.0 %all-to-all-done.x_ref = bf16[16,520,128]{2,1,0:T(8,128)(2,1)} async-done(((bf16[16,520,128]{2,1,0:T(8,128)(2,1)}), bf16[16,520,128]{2,1,0:T(8,128)(2,1)}, u32[]{:S(2)}, u32[]{:S(2)}) %all-to-all-start) | async-done | bytes 2129952 | tf_op jit(solution)/shard_map/all_to_all | solution.py:124
  58.9 10.7 %all-to-all-start.1 = ((bf16[16,512,128]{2,1,0:T(8,128)(2,1)}), bf16[16,512,128]{2,1,0:T(8,128)(2,1)S(1)}, u32[]{:S(2)}, u32[]{:S(2)}) async-start(bf16[16,512,128]{2,1,0:T(8,128)(2,1)} %copy-done), calls=%async_computation.1 | async-start | bytes 4194304 | tf_op jit(solution)/shard_map/all_to_all | solution.py:124
  69.6 10.8 %enter.3 = (bf16[1024,1024]{1,0:T(8,128)(2,1)}, bf16[1024,1024]{1,0:T(8,128)(2,1)}) custom-call(bf16[16,520,128]{2,1,0:T(8,128)(2,1)} %all-to-all-done.x_ref, f32[1,1024]{1,0:T(1,128)} %bitcast.26, f32[1,1024]{1,0:T(1,128)} %bitcast.30, f32[2,1024]{1,0:T(2,128)} %convert_element_type.58.bias_ref, bf16[1024,128]{1,0:T(8,128)(2,1)} %pad.13.down_ref, ...), custom_call_target="tpu_custom_call" | custom-call | flops 4294967296 | bytes 19709952 | tf_op jit(solution)/shard_map/enter/pallas_call | solution.py:529
  84.6 8.3 %enter.2 = (bf16[1024,1024]{1,0:T(8,128)(2,1)}, bf16[1024,128]{1,0:T(8,128)(2,1)}) custom-call(bf16[16,520,128]{2,1,0:T(8,128)(2,1)} %all-to-all-done.x_ref, f32[1,1024]{1,0:T(1,128)} %bitcast.27, f32[1,1024]{1,0:T(1,128)} %bitcast.31, f32[2,1024]{1,0:T(2,128)} %convert_element_type.58.bias_ref, bf16[1024,128]{1,0:T(8,128)(2,1)} %pad.13.down_ref, ...), custom_call_target="tpu_custom_call" | custom-call | flops 2147483648 | bytes 11583488 | tf_op jit(solution)/shard_map/enter/pallas_call | solution.py:529
  94.1 30.1 %attend.1 = (bf16[1024,1024]{1,0:T(8,128)(2,1)}, f32[64,1024]{1,0:T(8,128)}) custom-call(s32[1]{0:T(128)S(6)} %convert_element_type.62.refs_0_, bf16[1024,1024]{1,0:T(8,128)(2,1)} %get-tuple-element.56.refs_1_, bf16[1024,1024]{1,0:T(8,128)(2,1)} %get-tuple-element.57.refs_2_.refs_5_, bf16[1024,1024]{1,0:T(8,128)(2,1)} %collective-permute-done.3.refs_3_.refs_6_, ...), custom_call_target="tpu_custom_call" | custom-call | flops 4831838208 | bytes 12582912 | tf_op jit(solution)/shard_map/attend/pallas_call | solution.py:723
  125.5 64.5 %middle.1 = (bf16[1024,1024]{1,0:T(8,128)(2,1)}, bf16[1024,1024]{1,0:T(8,128)(2,1)}, bf16[1024,1024]{1,0:T(8,128)(2,1)}) custom-call(bf16[16,520,128]{2,1,0:T(8,128)(2,1)} %all-to-all-done.x_ref, bf16[1024,1024]{1,0:T(8,128)(2,1)} %get-tuple-element.60.attended_ref.refs_3_, bf16[16,512,128]{2,1,0:T(8,128)(2,1)} %copy-done.2, f32[1,1024]{1,0:T(1,128)} %bitcast.37, ...), custom_call_target="tpu_custom_call" | custom-call | flops 38654705664 | bytes 31522816 | tf_op jit(solution)/shard_map/middle/pallas_call | solution.py:529
  190.0 7.0 %all-to-all-start.2 = ((bf16[16,64,1024]{2,1,0:T(8,128)(2,1)}), bf16[16,64,1024]{2,1,0:T(8,128)(2,1)S(1)}, u32[]{:S(2)}, u32[]{:S(2)}) async-start(bf16[16,64,1024]{2,1,0:T(8,128)(2,1)} %bitcast.24), calls=%async_computation.2 | async-start | bytes 4194304 | tf_op jit(solution)/shard_map/all_to_all | solution.py:130
  197.1 61.2 %pull.1 = (bf16[1024,1024]{1,0:T(8,128)(2,1)}, bf16[1024,1024]{1,0:T(8,128)(2,1)}, bf16[1024,1024]{1,0:T(8,128)(2,1)}, bf16[1024,1024]{1,0:T(8,128)(2,1)}, bf16[1024,1024]{1,0:T(8,128)(2,1)}) custom-call(s32[1]{0:T(128)S(6)} %convert_element_type.62.refs_0_, bf16[1024,1024]{1,0:T(8,128)(2,1)} %get-tuple-element.56.refs_1_, ...), custom_call_target="tpu_custom_call" | custom-call | flops 12079595520 | bytes 25165824 | tf_op jit(solution)/shard_map/pull/pallas_call | solution.py:741
  258.8 4.0 %collective-permute-done.6.refs_1_.refs_3_ = bf16[1024,1024]{1,0:T(8,128)(2,1)} collective-permute-done((bf16[1024,1024]{1,0:T(8,128)(2,1)}, bf16[1024,1024]{1,0:T(8,128)(2,1)}, u32[]{:S(2)}, u32[]{:S(2)}) %collective-permute-start.6) | collective-permute-done | bytes 2097184 | tf_op jit(solution)/shard_map/ppermute | solution.py:143
  262.8 8.1 %adapt.1 = (bf16[1024,128]{1,0:T(8,128)(2,1)}, f32[8,1024]{1,0:T(8,128)}, f32[8,2048]{1,0:T(8,128)}) custom-call(bf16[16,520,128]{2,1,0:T(8,128)(2,1)} %all-to-all-done.x_ref, f32[1,1024]{1,0:T(1,128)} %bitcast.28, f32[1,1024]{1,0:T(1,128)} %bitcast.32, bf16[128,2048]{1,0:T(8,128)(2,1)} %fusion.1.up_ref, bf16[1024,128]{1,0:T(8,128)(2,1)} %get-tuple-element.76.lora_ref, ...), custom_call_target="tpu_custom_call" | custom-call | flops 1073741824 | bytes 9576448 | tf_op jit(solution)/shard_map/adapt/pallas_call | solution.py:529
  272.5 2.9 collective-permute-start.9
  275.4 1.5 collective-permute-start.10
  276.9 14.4 %leave.1 = bf16[1024,1024]{1,0:T(8,128)(2,1)} custom-call(bf16[16,520,128]{2,1,0:T(8,128)(2,1)} %all-to-all-done.x_ref, f32[1,1024]{1,0:T(1,128)} %bitcast.29, bf16[1024,3072]{1,0:T(8,128)(2,1)} %weight_ref.1, bf16[1024,128]{1,0:T(8,128)(2,1)} %pad.13.down_ref, bf16[1024,128]{1,0:T(8,128)(2,1)} %get-tuple-element.80.grad_lora_ref, ...), custom_call_target="tpu_custom_call" | custom-call | flops 6442450944 | bytes 23629824 | tf_op jit(solution)/shard_map/leave/pallas_call | solution.py:529
  291.3 6.2 %all-to-all-start.3 = ((bf16[16,64,1024]{2,1,0:T(8,128)(2,1)}), bf16[16,64,1024]{2,1,0:T(8,128)(2,1)}, u32[]{:S(2)}, u32[]{:S(2)}) async-start(bf16[16,64,1024]{2,1,0:T(8,128)(2,1)} %bitcast.23), calls=%async_computation.3 | async-start | bytes 4194304 | tf_op jit(solution)/shard_map/all_to_all | solution.py:130
  297.7 2.8 collective-permute-start.14
  301.3 7.6 %collective-permute-done.14 = f32[16,1024]{1,0:T(8,128)S(1)} collective-permute-done((f32[16,1024]{1,0:T(8,128)S(1)}, f32[16,1024]{1,0:T(8,128)S(1)}, u32[]{:S(2)}, u32[]{:S(2)}) %collective-permute-start.14) | collective-permute-done | bytes 65568 | tf_op jit(solution)/shard_map/ppermute | solution.py:150
  308.9 5.2 %collective-permute-done.13 = f32[16,1024]{1,0:T(8,128)S(1)} collective-permute-done((f32[16,1024]{1,0:T(8,128)S(1)}, f32[16,1024]{1,0:T(8,128)S(1)}, u32[]{:S(2)}, u32[]{:S(2)}) %collective-permute-start.13) | collective-permute-done | bytes 65568 | tf_op jit(solution)/shard_map/ppermute | solution.py:150
  315.7 24.7 %all-to-all-done.3.refs_0_ = bf16[16,64,1024]{2,1,0:T(8,128)(2,1)} async-done(((bf16[16,64,1024]{2,1,0:T(8,128)(2,1)}), bf16[16,64,1024]{2,1,0:T(8,128)(2,1)}, u32[]{:S(2)}, u32[]{:S(2)}) %all-to-all-start.3) | async-done | bytes 2097184 | tf_op jit(solution)/shard_map/all_to_all | solution.py:130
  344.5 2.6 spread_stripes.3
  (125 shorter events, 25.3 us)
Async XLA Ops:
  2.2 2.8 collective-permute-start
  2.7 2.3 collective-permute-start.1
  6.7 52.3 %all-to-all-start = ((bf16[16,520,128]{2,1,0:T(8,128)(2,1)}), bf16[16,520,128]{2,1,0:T(8,128)(2,1)}, u32[]{:S(2)}, u32[]{:S(2)}) async-start(bf16[16,520,128]{2,1,0:T(8,128)(2,1)} %gather_stripes.2), calls=%async_computation | async-start | bytes 4259840 | tf_op jit(solution)/shard_map/all_to_all | solution.py:124
  18.4 7.7 %collective-permute-start.2 = (bf16[8,64,1024]{2,1,0:T(8,128)(2,1)}, bf16[8,64,1024]{2,1,0:T(8,128)(2,1)S(1)}, u32[]{:S(2)}, u32[]{:S(2)}) collective-permute-start(bf16[8,64,1024]{2,1,0:T(8,128)(2,1)} %constant_dynamic-slice_fusion.4), channel_id=1, source_target_pairs={{0,1},{1,0},{2,3},{3,2},{4,5},{5,4},{6,7},{7,6},{8,9},{9,8},{10,11... | collective-permute-start | bytes 3145736 | tf_op jit(solution)/shard_map/ppermute | solution.py:143
  58.9 65.2 %all-to-all-start.1 = ((bf16[16,512,128]{2,1,0:T(8,128)(2,1)}), bf16[16,512,128]{2,1,0:T(8,128)(2,1)S(1)}, u32[]{:S(2)}, u32[]{:S(2)}) async-start(bf16[16,512,128]{2,1,0:T(8,128)(2,1)} %copy-done), calls=%async_computation.1 | async-start | bytes 4194304 | tf_op jit(solution)/shard_map/all_to_all | solution.py:124
  80.5 13.6 %collective-permute-start.3 = (bf16[1024,1024]{1,0:T(8,128)(2,1)}, bf16[1024,1024]{1,0:T(8,128)(2,1)}, u32[]{:S(2)}, u32[]{:S(2)}) collective-permute-start(bf16[1024,1024]{1,0:T(8,128)(2,1)} %get-tuple-element.57.refs_2_.refs_5_), channel_id=1, source_target_pairs={{0,1},{1,0},{2,3},{3,2},{4,5},{5,4},{6,7},{7,6},{8,9},{9,8},{10,11... | collective-permute-start | bytes 6291464 | tf_op jit(solution)/shard_map/ppermute | solution.py:143
  80.5 13.6 %collective-permute-start.4 = (bf16[1024,1024]{1,0:T(8,128)(2,1)}, bf16[1024,1024]{1,0:T(8,128)(2,1)}, u32[]{:S(2)}, u32[]{:S(2)}) collective-permute-start(bf16[1024,1024]{1,0:T(8,128)(2,1)} %get-tuple-element.58.refs_4_.refs_7_), channel_id=1, source_target_pairs={{0,1},{1,0},{2,3},{3,2},{4,5},{5,4},{6,7},{7,6},{8,9},{9,8},{10,11... | collective-permute-start | bytes 6291464 | tf_op jit(solution)/shard_map/ppermute | solution.py:143
  190.0 68.2 %all-to-all-start.2 = ((bf16[16,64,1024]{2,1,0:T(8,128)(2,1)}), bf16[16,64,1024]{2,1,0:T(8,128)(2,1)S(1)}, u32[]{:S(2)}, u32[]{:S(2)}) async-start(bf16[16,64,1024]{2,1,0:T(8,128)(2,1)} %bitcast.24), calls=%async_computation.2 | async-start | bytes 4194304 | tf_op jit(solution)/shard_map/all_to_all | solution.py:130
  258.3 4.6 %collective-permute-start.6 = (bf16[1024,1024]{1,0:T(8,128)(2,1)}, bf16[1024,1024]{1,0:T(8,128)(2,1)}, u32[]{:S(2)}, u32[]{:S(2)}) collective-permute-start(bf16[1024,1024]{1,0:T(8,128)(2,1)} %get-tuple-element.79), channel_id=1, source_target_pairs={{0,1},{1,0},{2,3},{3,2},{4,5},{5,4},{6,7},{7,6},{8,9},{9,8},{10,11... | collective-permute-start | bytes 6291464 | tf_op jit(solution)/shard_map/ppermute | solution.py:143
  258.3 18.5 %collective-permute-start.7 = (bf16[1024,1024]{1,0:T(8,128)(2,1)}, bf16[1024,1024]{1,0:T(8,128)(2,1)}, u32[]{:S(2)}, u32[]{:S(2)}) collective-permute-start(bf16[1024,1024]{1,0:T(8,128)(2,1)} %get-tuple-element.83), channel_id=1, source_target_pairs={{0,1},{1,0},{2,3},{3,2},{4,5},{5,4},{6,7},{7,6},{8,9},{9,8},{10,11... | collective-permute-start | bytes 6291464 | tf_op jit(solution)/shard_map/ppermute | solution.py:143
  272.5 18.7 %collective-permute-start.9 = (f32[16,1024]{1,0:T(8,128)S(1)}, f32[16,1024]{1,0:T(8,128)S(1)}, u32[]{:S(2)}, u32[]{:S(2)}) collective-permute-start(f32[16,1024]{1,0:T(8,128)S(1)} %pad_maximum_fusion), channel_id=1, source_target_pairs={{0,16},{2,18},{4,20},{6,22},{8,24},{10,26},{12,28},{14,30},{16,0},... | collective-permute-start | bytes 196616 | tf_op jit(solution)/shard_map/ppermute | solution.py:150
  275.4 15.8 %collective-permute-start.10 = (f32[16,1024]{1,0:T(8,128)S(1)}, f32[16,1024]{1,0:T(8,128)S(1)}, u32[]{:S(2)}, u32[]{:S(2)}) collective-permute-start(f32[16,1024]{1,0:T(8,128)S(1)} %pad_maximum_fusion), channel_id=1, source_target_pairs={{0,24},{2,26},{4,28},{6,30},{8,16},{10,18},{12,20},{14,22},{16,8},... | collective-permute-start | bytes 196616 | tf_op jit(solution)/shard_map/ppermute | solution.py:150
  276.9 14.4 %collective-permute-start.8 = (f32[16,1024]{1,0:T(8,128)S(1)}, f32[16,1024]{1,0:T(8,128)S(1)}, u32[]{:S(2)}, u32[]{:S(2)}) collective-permute-start(f32[16,1024]{1,0:T(8,128)S(1)} %pad_maximum_fusion), channel_id=1, source_target_pairs={{0,8},{2,10},{4,12},{6,14},{8,0},{10,2},{12,4},{14,6},{16,24},{18,... | collective-permute-start | bytes 196616 | tf_op jit(solution)/shard_map/ppermute | solution.py:150
  291.3 49.1 %all-to-all-start.3 = ((bf16[16,64,1024]{2,1,0:T(8,128)(2,1)}), bf16[16,64,1024]{2,1,0:T(8,128)(2,1)}, u32[]{:S(2)}, u32[]{:S(2)}) async-start(bf16[16,64,1024]{2,1,0:T(8,128)(2,1)} %bitcast.23), calls=%async_computation.3 | async-start | bytes 4194304 | tf_op jit(solution)/shard_map/all_to_all | solution.py:130
  297.6 16.6 %collective-permute-start.5 = (bf16[8,64,1024]{2,1,0:T(8,128)(2,1)S(1)}, bf16[8,64,1024]{2,1,0:T(8,128)(2,1)S(1)}, u32[]{:S(2)}, u32[]{:S(2)}) collective-permute-start(bf16[8,64,1024]{2,1,0:T(8,128)(2,1)S(1)} %constant_dynamic-slice_fusion.1), channel_id=1, source_target_pairs={{0,1},{1,0},{2,3},{3,2},{4,5},{5,4},{6,7},{7,6},{8,9},{9,8},{10,11... | collective-permute-start | bytes 3145736 | tf_op jit(solution)/shard_map/ppermute | solution.py:143
  297.7 11.2 %collective-permute-start.14 = (f32[16,1024]{1,0:T(8,128)S(1)}, f32[16,1024]{1,0:T(8,128)S(1)}, u32[]{:S(2)}, u32[]{:S(2)}) collective-permute-start(f32[16,1024]{1,0:T(8,128)S(1)} %add_add_fusion.1), channel_id=1, source_target_pairs={{0,6},{2,4},{4,2},{6,0},{8,14},{10,12},{12,10},{14,8},{16,22},{18,... | collective-permute-start | bytes 196616 | tf_op jit(solution)/shard_map/ppermute | solution.py:150
  300.5 13.6 %collective-permute-start.13 = (f32[16,1024]{1,0:T(8,128)S(1)}, f32[16,1024]{1,0:T(8,128)S(1)}, u32[]{:S(2)}, u32[]{:S(2)}) collective-permute-start(f32[16,1024]{1,0:T(8,128)S(1)} %add_add_fusion.1), channel_id=1, source_target_pairs={{0,4},{2,6},{4,0},{6,2},{8,12},{10,14},{12,8},{14,10},{16,20},{18,... | collective-permute-start | bytes 196616 | tf_op jit(solution)/shard_map/ppermute | solution.py:150
  301.1 13.0 %collective-permute-start.12 = (f32[16,1024]{1,0:T(8,128)S(1)}, f32[16,1024]{1,0:T(8,128)S(1)}, u32[]{:S(2)}, u32[]{:S(2)}) collective-permute-start(f32[16,1024]{1,0:T(8,128)S(1)} %add_add_fusion.1), channel_id=1, source_target_pairs={{0,2},{2,0},{4,6},{6,4},{8,10},{10,8},{12,14},{14,12},{16,18},{18,... | collective-permute-start | bytes 196616 | tf_op jit(solution)/shard_map/ppermute | solution.py:150
  314.1 1.5 collective-permute-start.15
  315.6 26.2 %copy-start.12 = (f32[2,1024,4]{1,2,0:T(4,128)S(1)}, f32[2,1024,4]{1,2,0:T(4,128)}, u32[]{:S(2)}) copy-start(f32[2,1024,4]{1,2,0:T(4,128)} %param.41) | copy-start | bytes 98308
  315.6 26.9 %copy-start.10 = (f32[2,1024,4]{1,2,0:T(4,128)S(1)}, f32[2,1024,4]{1,2,0:T(4,128)}, u32[]{:S(2)}) copy-start(f32[2,1024,4]{1,2,0:T(4,128)} %param.43) | copy-start | bytes 98308
  315.6 27.5 %copy-start.13 = (f32[2,4,1024]{2,1,0:T(4,128)S(1)}, f32[2,4,1024]{2,1,0:T(4,128)}, u32[]{:S(2)}) copy-start(f32[2,4,1024]{2,1,0:T(4,128)} %param.42) | copy-start | bytes 98308
  315.7 28.2 %copy-start.11 = (f32[2,4,1024]{2,1,0:T(4,128)S(1)}, f32[2,4,1024]{2,1,0:T(4,128)}, u32[]{:S(2)}) copy-start(f32[2,4,1024]{2,1,0:T(4,128)} %param.44) | copy-start | bytes 98308
  341.7 2.7 collective-permute-start.11
  (21 other events, 94.3 us)
where the time goes:
time: 349 us; the launch traced here: 347 us
  Pallas kernels  204 us (58%)
  waiting for transfers between devices  74.7 us (21%)
  starting transfers between devices  42.1 us (12%)
  other arithmetic  15.6 us (4%)
  local copies, waits for them, and re-layouts  8.56 us (2%)
    pallas_call x5, Pallas kernels, over_tokens(): pl.pallas_call(kernel, grid=(tokens // min(TOKEN_BLOCK, tokens),), in_spe...  106 us
    pallas_call x1, Pallas kernels, body(): pull(far, queries, grad_attended, attended, log_total, *all_keys, *all_va...  61.2 us
    all_to_all x2, waiting for transfers between devices, rows_home(): return lax.all_to_all(y, 'seq', 0, 0, tiled=True)  31 us
    pallas_call x1, Pallas kernels, body(): attend(far, queries, *all_keys, *all_values, marks, causal)  30.1 us
    all_to_all x2, waiting for transfers between devices, rows_back(): return lax.all_to_all(y, 'seq', 0, 0, tiled=True)  24.7 us
    all_to_all x2, starting transfers between devices, rows_home(): return lax.all_to_all(y, 'seq', 0, 0, tiled=True)  19.1 us
    all_to_all x2, starting transfers between devices, rows_back(): return lax.all_to_all(y, 'seq', 0, 0, tiled=True)  13.2 us
    ppermute x7, waiting for transfers between devices, sum_over(): lax.ppermute(x, axis, [(i, i ^ by << low) for i in range(size)])  12.9 us
  transfers between devices with their start and end apart: 20, of which 6 were waited for; matrix products, arithmetic and copies ran while one was open for 5% of the time, Pallas kernels for 39%

commit v1 on v0

--- a/solution.py
+++ b/solution.py
@@ -14,8 +14,11 @@
 QUERY_BLOCK = 256
 TOKEN_BLOCK = 256
 HIDDEN_BLOCK = 1024
-AHEAD = 3
-VMEM_BYTES = 60 * 1024 * 1024
+AHEAD = 2
+PER = 2
+SCORES_AHEAD = 2
+DELAY = 0
+VMEM_BYTES = 63 * 1024 * 1024
 
 norm_eps = 1e-05
 adapter_scale = 8.0
@@ -143,14 +146,44 @@
     return lax.ppermute(x, "batch", [(i, (i + by) % cores) for i in range(cores)])
 
 
-def sum_over(x, axis, low, high):
-    size = lax.axis_size(axis)
-    terms = [x]
-    for by in range(1, 1 << (high - low)):
-        terms.append(lax.ppermute(x, axis, [(i, i ^ (by << low)) for i in range(size)]))
+def paired_sum(terms):
     while len(terms) > 1:
         terms = [terms[i] + terms[i + 1] for i in range(0, len(terms), 2)]
     return terms[0]
+
+
+def sum_everywhere(x):
+    ring, cores = lax.axis_size("seq"), lax.axis_size("batch")
+    assert ring & (ring - 1) == 0 and cores & (cores - 1) == 0
+
+    def exchanged(x, axis, size, by):
+        return lax.ppermute(x, axis, [(i, i ^ by) for i in range(size)])
+
+    step = 1
+    while step < cores:
+        x = x + exchanged(x, "batch", cores, step)
+        step *= 2
+    near = min(4, ring)
+    share = x.shape[0] // near
+    me = lax.rem(lax.axis_index("seq"), near)
+
+    def shares_of(x, which):
+        return lax.dynamic_slice_in_dim(x, which * share, share, 0)
+
+    terms = [shares_of(x, me)]
+    for by in range(1, near):
+        terms.append(exchanged(shares_of(x, me ^ by), "seq", ring, by))
+    mine = paired_sum(terms)
+    step = near
+    while step < ring:
+        width = min(4, ring // step)
+        mine = paired_sum(
+            [mine] + [exchanged(mine, "seq", ring, by * step) for by in range(1, width)]
+        )
+        step *= width
+    held = [mine] + [exchanged(mine, "seq", ring, by) for by in range(1, near)]
+    held = jnp.concatenate(held)
+    return jnp.concatenate([shares_of(held, me ^ at) for at in range(near)])
 
 
 def lane_masks(dtype):
@@ -169,7 +202,7 @@
     return ref[pl.ds(index * QUERY_BLOCK, QUERY_BLOCK), :]
 
 
-def attend_kernel(cores, reach, *refs):
+def attend_block(cores, reach, skipped, *refs):
     far_ref, query_ref = refs[:2]
     key_refs = refs[2 : 2 + cores]
     value_refs = refs[2 + cores : 2 + 2 * cores]
@@ -201,45 +234,50 @@
             scores.append(score + causal_ref[...] if j == n else score)
         return scores
 
-    def finish(n, h, start, scores):
-        rows = pl.ds(n * QUERY_BLOCK, QUERY_BLOCK)
+    def soften(scores):
         top = scores[0]
         for score in scores[1:]:
             top = jnp.maximum(top, score)
         top = jnp.max(top, axis=0, keepdims=True)
-        weights = [jnp.exp(score - top).astype(jnp.bfloat16) for score in scores]
+        return top, [jnp.exp(score - top).astype(jnp.bfloat16) for score in scores]
+
+    def finish(n, h, start, top, weights, outs):
+        rows = pl.ds(n * QUERY_BLOCK, QUERY_BLOCK)
         keys = pl.ds(start * tile, (n + 1 - start) * tile)
         out = matmul_rows(turned_values[h, :, keys], jnp.concatenate(weights))
         total = out[half : half + 1]
         log_ref[h : h + 1, rows] = top + jnp.log(total)
-        return out[:half] / total
+        outs.append(out[:half] / total)
+        if h:
+            out_ref[rows, :] = jnp.concatenate(outs[-2:]).T.astype(out_ref.dtype)
 
     def every(skipped):
-        waiting, outs = [], []
+        waiting, left, outs = [], [], []
         units = []
         for n in range(blocks):
             start = max(0, n - reach) + (skipped and n == blocks - 1)
             units += [(n, h, start) for h in range(2)]
-        for unit in units + [None] * AHEAD:
+        for unit in units + [None] * SCORES_AHEAD:
             if unit is not None:
                 waiting.append((unit, scores_of(*unit)))
-            if len(waiting) > AHEAD or unit is None:
+            if len(waiting) > SCORES_AHEAD or unit is None:
                 done, scores = waiting.pop(0)
-                outs.append(finish(*done, scores))
-                if len(outs) == 2:
-                    rows = pl.ds(done[0] * QUERY_BLOCK, QUERY_BLOCK)
-                    out_ref[rows, :] = jnp.concatenate(outs).T.astype(out_ref.dtype)
-                    outs = []
-
-    either_way(every, far_ref, blocks > reach)
-
-
-def either_way(every, far_ref, can_skip):
-    if not can_skip:
-        every(False)
+                left.append((*done, *soften(scores)))
+                if len(left) > DELAY:
+                    finish(*left.pop(0), outs)
+        for one in left:
+            finish(*one, outs)
+
+    every(skipped)
+
+
+def either_way(block, cores, reach, *refs):
+    far_ref, query_ref = refs[:2]
+    if query_ref.shape[0] // QUERY_BLOCK <= reach:
+        block(cores, reach, False, *refs)
         return
-    pl.when(far_ref[0] == 1)(functools.partial(every, False))
-    pl.when(far_ref[0] != 1)(functools.partial(every, True))
+    pl.when(far_ref[0] == 1)(functools.partial(block, cores, reach, False, *refs))
+    pl.when(far_ref[0] != 1)(functools.partial(block, cores, reach, True, *refs))
 
 
 def spread(wide):
@@ -247,7 +285,7 @@
     return high, (wide - high.astype(jnp.float32)).astype(jnp.bfloat16)
 
 
-def pull_kernel(cores, reach, *refs):
+def pull_block(cores, reach, skipped, *refs):
     far_ref, query_ref, grad_ref, out_ref, log_ref = refs[:5]
     key_refs = refs[5 : 5 + cores]
     value_refs = refs[5 + cores : 5 + 2 * cores]
@@ -259,8 +297,8 @@
     grad_key_refs = outs[1 : 1 + cores]
     grad_value_refs = outs[1 + cores : 1 + 2 * cores]
     (
-        query_heads, key_heads, value_heads, turned_queries, turned_keys, turned_grads,
-        turned_sums, dots,
+        query_marked, query_heads, key_heads, all_values, grad_heads, turned_keys, turned_sums,
+        dots,
     ) = outs[1 + 2 * cores :]
     heads = lane_masks(jnp.bfloat16)
     half = LANES // 2
@@ -276,26 +314,26 @@
         grad = grad_ref[rows, :]
         high, rest = spread(grad.astype(jnp.float32) * out_ref[rows, :].astype(jnp.float32))
         dots[:, rows] = matmul_back(chooser, high) + matmul_back(chooser, rest)
-        turned_queries[:, rows] = query.T
-        turned_grads[:, rows] = grad.T
         for h, own in enumerate(heads):
-            query_heads[h, rows, :] = query * own + mark_ref[rows, :] * excluded * heads[1 - h]
+            mine = query * own
+            query_heads[h, rows, :] = mine
+            query_marked[h, rows, :] = mine + mark_ref[rows, :] * excluded * heads[1 - h]
+            grad_heads[h, rows, :] = grad * own
         for k in range(cores):
             key = block_of(key_refs[k], n)
             key_mark = slots - block_of(mark_ref, k * blocks + n)
-            value = block_of(value_refs[k], n)
             at = pl.ds(n * tile + k * QUERY_BLOCK, QUERY_BLOCK)
             turned_keys[:, at] = key.T
+            all_values[at, :] = block_of(value_refs[k], n)
             for h, own in enumerate(heads):
                 key_heads[h, at, :] = key * own + key_mark * heads[1 - h]
-                value_heads[h, at, :] = value * own
     turned_sums[...] = jnp.zeros_like(turned_sums)
 
     def products(j, n, h):
         keys = pl.ds(j * tile, tile)
         rows = pl.ds(n * QUERY_BLOCK, QUERY_BLOCK)
-        score = matmul_back(key_heads[h, keys, :], query_heads[h, rows, :])
-        change = matmul_back(value_heads[h, keys, :], grad_ref[rows, :])
+        score = matmul_back(key_heads[h, keys, :], query_marked[h, rows, :])
+        change = matmul_back(all_values[keys, :], grad_heads[h, rows, :])
         return score, change
 
     def weigh(j, n, h, score, change):
@@ -306,17 +344,30 @@
         change = (weight * (change - dots[h : h + 1, rows])).astype(jnp.bfloat16)
         return weight.astype(jnp.bfloat16), change
 
-    def finish(j, h, members):
-        part = pl.ds(h * half, half)
+    def finishing(j, members):
+        count = len(members) // 2
         keys = pl.ds(j * tile, tile)
-        rows = pl.ds(members[0][0] * QUERY_BLOCK, len(members) * QUERY_BLOCK)
-        weights = jnp.concatenate([m[1] for m in members], axis=1)
-        changes = jnp.concatenate([m[2] for m in members], axis=1)
-        turned_sums[part, rows] += matmul_rows(turned_keys[part, keys], changes)
-        return (
-            matmul_back(turned_queries[part, rows], changes),
-            matmul_back(turned_grads[part, rows], weights),
-        )
+        rows = pl.ds(j * QUERY_BLOCK, count * QUERY_BLOCK)
+
+        def query_side(h):
+            part = pl.ds(h * half, half)
+            mine = jnp.concatenate([m[1] for m in members[h * count : (h + 1) * count]], axis=1)
+            turned_sums[part, rows] += matmul_rows(turned_keys[part, keys], mine)
+
+        def key_side(out_refs, which, right):
+            left = jnp.concatenate([m[which] for m in members], axis=1)
+            right = jnp.concatenate([right[0, rows, :], right[1, rows, :]])
+            both = matmul_rows(left, right).astype(jnp.bfloat16)
+            for k in range(cores):
+                mine = both[k * QUERY_BLOCK : (k + 1) * QUERY_BLOCK]
+                out_refs[k][pl.ds(j * QUERY_BLOCK, QUERY_BLOCK), :] = mine
+
+        return [
+            functools.partial(key_side, grad_value_refs, 0, grad_heads),
+            functools.partial(query_side, 0),
+            functools.partial(key_side, grad_key_refs, 1, query_heads),
+            functools.partial(query_side, 1),
+        ]
 
     def every(skipped):
         units = []
@@ -324,27 +375,24 @@
             last = min(blocks - 1, j + reach)
             if skipped and j + reach == blocks - 1:
                 last -= 1
-            units += [(j, n, h, n == last) for h in range(2) for n in range(j, last + 1)]
-        waiting, members, sums = [], [], []
+            units += [(j, n, h, n == last and h) for h in range(2) for n in range(j, last + 1)]
+        waiting, members, left = [], [], []
         for unit in units + [None] * AHEAD:
             if unit is not None:
                 waiting.append((unit, products(*unit[:3])))
             if len(waiting) > AHEAD or unit is None:
                 (j, n, h, closing), pair = waiting.pop(0)
-                members.append((n, *weigh(j, n, h, *pair)))
+                members.append(weigh(j, n, h, *pair))
+                for task in left[:PER]:
+                    task()
+                left = left[PER:]
                 if closing:
-                    sums.append(finish(j, h, members))
+                    left += finishing(j, members)
                     members = []
-                if len(sums) == 2:
-                    for out_refs, which in ((grad_key_refs, 0), (grad_value_refs, 1)):
-                        both = jnp.concatenate([s[which] for s in sums]).T.astype(jnp.bfloat16)
-                        for k in range(cores):
-                            out_refs[k][pl.ds(j * QUERY_BLOCK, QUERY_BLOCK), :] = both[
-                                k * QUERY_BLOCK : (k + 1) * QUERY_BLOCK
-                            ]
-                    sums = []
-
-    either_way(every, far_ref, blocks > reach)
+        for task in left:
+            task()
+
+    every(skipped)
     grad_query_ref[...] = (turned_sums[...] * score_scale).T.astype(jnp.bfloat16)
 
 
@@ -362,22 +410,22 @@
 
 
 def enter_kernel(
-    stripe, kinds, x_ref, gain_ref, shift_ref, bias_ref, down_ref, up_ref, *refs
+    stripe, x_ref, gain_ref, shift_ref, bias_ref, down_ref, up_ref, key_weight_ref,
+    value_weight_ref, key_ref, value_ref, normed_ref, lora_ref,
 ):
-    weight_refs, out_refs = refs[: len(kinds)], refs[len(kinds) :]
-    width = out_refs[0].shape[1]
-    shaped, _ = standardized(tokens_of(x_ref, stripe, width).astype(jnp.float32))
+    shaped, _ = standardized(tokens_of(x_ref, stripe, key_ref.shape[1]).astype(jnp.float32))
     normed = (shaped * gain_ref[...] + shift_ref[...]).astype(jnp.bfloat16)
+    normed_ref[...] = normed
+    key_ref[...] = matmul_rows(normed, key_weight_ref[...]).astype(jnp.bfloat16)
     lora = matmul_rows(normed, down_ref[...]).astype(jnp.bfloat16)
-    if len(out_refs) > len(kinds):
-        out_refs[-1][...] = lora
-    for kind, weight_ref, out_ref in zip(kinds, weight_refs, out_refs):
-        out = matmul_rows(normed, weight_ref[...])
-        if kind != 1:
-            j = kind // 2
-            out = out + matmul_rows(lora, up_ref[:, j * width : (j + 1) * width])
-            out = out + bias_ref[j : j + 1, :]
-        out_ref[...] = out.astype(jnp.bfloat16)
+    lora_ref[...] = lora
+    value = matmul_rows(normed, value_weight_ref[...]) + matmul_rows(lora, up_ref[...])
+    value_ref[...] = (value + bias_ref[...]).astype(jnp.bfloat16)
+
+
+def ask_kernel(normed_ref, lora_ref, bias_ref, up_ref, weight_ref, query_ref):
+    query = matmul_rows(normed_ref[...], weight_ref[...]) + matmul_rows(lora_ref[...], up_ref[...])
+    query_ref[...] = (query + bias_ref[...]).astype(jnp.bfloat16)
 
 
 root_two_over_pi = 0.7978845608028654
@@ -452,10 +500,9 @@
 
 
 def adapt_kernel(
-    stripe, cores, x_ref, gain_ref, shift_ref, up_ref, lora_ref, grad_query_ref, *refs
+    cores, normed_ref, lora_ref, grad_lora_ref, grad_query_ref, *refs
 ):
-    value_refs = refs[:cores]
-    grad_lora_ref, down_sum_ref, up_sum_ref = refs[cores:]
+    down_sum_ref, up_sum_ref = refs[cores:]
     slots = down_sum_ref.shape[0]
 
     @pl.when(pl.program_id(0) == 0)
@@ -464,33 +511,32 @@
         up_sum_ref[...] = jnp.zeros_like(up_sum_ref)
 
     width = grad_query_ref.shape[1]
+    lora = lora_ref[...]
+    down_sum_ref[...] += matmul_over(grad_lora_ref[...], normed_ref[...])[:slots]
+    up_sum_ref[:, :width] += matmul_over(lora, grad_query_ref[...])[:slots]
+    up_sum_ref[:, width:] += matmul_over(lora, total(refs[:cores]))[:slots]
+
+
+def leave_kernel(
+    stripe, cores, x_ref, gain_ref, weight_ref, down_ref, up_ref, grad_middle_ref,
+    grad_query_ref, *refs,
+):
+    key_refs, value_refs = refs[:cores], refs[cores : 2 * cores]
+    grad_ref, grad_lora_ref = refs[2 * cores :]
+    width = grad_query_ref.shape[1]
     grad_query = grad_query_ref[...]
     grad_value = total(value_refs)
-    shaped, _ = standardized(tokens_of(x_ref, stripe, width).astype(jnp.float32))
-    normed = (shaped * gain_ref[...] + shift_ref[...]).astype(jnp.bfloat16)
     grad_lora = matmul_back(grad_query, up_ref[:, :width]) + matmul_back(
         grad_value, up_ref[:, width:]
     )
     grad_lora = grad_lora.astype(jnp.bfloat16)
     grad_lora_ref[...] = grad_lora
-    lora = lora_ref[...]
-    down_sum_ref[...] += matmul_over(grad_lora, normed)[:slots]
-    up_sum_ref[:, :width] += matmul_over(lora, grad_query)[:slots]
-    up_sum_ref[:, width:] += matmul_over(lora, grad_value)[:slots]
-
-
-def leave_kernel(
-    stripe, cores, x_ref, gain_ref, weight_ref, down_ref, grad_lora_ref, grad_middle_ref,
-    grad_query_ref, *refs,
-):
-    key_refs, value_refs, grad_ref = refs[:cores], refs[cores : 2 * cores], refs[-1]
-    width = grad_query_ref.shape[1]
     shaped, spread_inverse = standardized(tokens_of(x_ref, stripe, width).astype(jnp.float32))
     grad_normed = (
-        matmul_back(grad_query_ref[...], weight_ref[:, :width])
+        matmul_back(grad_query, weight_ref[:, :width])
         + matmul_back(total(key_refs), weight_ref[:, width : 2 * width])
-        + matmul_back(total(value_refs), weight_ref[:, 2 * width :])
-        + matmul_back(grad_lora_ref[...], down_ref[...])
+        + matmul_back(grad_value, weight_ref[:, 2 * width :])
+        + matmul_back(grad_lora, down_ref[...])
     )
     grad = norm_pull(grad_normed * gain_ref[...], shaped, spread_inverse)
     grad_ref[...] = (grad_middle_ref[...].astype(jnp.float32) + grad).astype(jnp.bfloat16)
@@ -558,7 +604,7 @@
     )
     low_scratch = functools.partial(pltpu.VMEM, dtype=jnp.bfloat16)
     forward = pl.pallas_call(
-        functools.partial(attend_kernel, cores, reach),
+        functools.partial(either_way, attend_block, cores, reach),
         grid_spec=pltpu.PrefetchScalarGridSpec(
             num_scalar_prefetch=1,
             grid=grid,
@@ -579,7 +625,7 @@
         name="attend",
     )
     backward = pl.pallas_call(
-        functools.partial(pull_kernel, cores, reach),
+        functools.partial(either_way, pull_block, cores, reach),
         grid_spec=pltpu.PrefetchScalarGridSpec(
             num_scalar_prefetch=1,
             grid=grid,
@@ -587,11 +633,11 @@
             out_specs=[pair] * (1 + 2 * cores),
             scratch_shapes=[
                 low_scratch((2, tokens, LANES)),
+                low_scratch((2, tokens, LANES)),
                 low_scratch((2, cores * tokens, LANES)),
-                low_scratch((2, cores * tokens, LANES)),
-                low_scratch((LANES, tokens)),
+                low_scratch((cores * tokens, LANES)),
+                low_scratch((2, tokens, LANES)),
                 low_scratch((LANES, cores * tokens)),
-                low_scratch((LANES, tokens)),
                 pltpu.VMEM((LANES, tokens), jnp.float32),
                 pltpu.VMEM((8, tokens), jnp.float32),
             ],
@@ -703,23 +749,29 @@
 
     low = jax.ShapeDtypeStruct((tokens, width), jnp.bfloat16)
 
-    def enter(kinds, extra):
-        return over_tokens(
-            functools.partial(enter_kernel, stripe, kinds),
-            "enter",
-            tokens,
-            [tile(x), whole(first_gain), whole(first_shift), whole(value_bias)]
-            + [whole(down_packed), whole(up_packed)]
-            + [columns(query_key_value_weight, kind, width) for kind in kinds],
-            [low] * len(kinds) + extra,
-            [],
-            2 * len(kinds) * tokens * width * width,
-        )
-
-    keys, values = enter((1, 2), [])
+    keys, values, normed, lora = over_tokens(
+        functools.partial(enter_kernel, stripe),
+        "enter",
+        tokens,
+        [tile(x), whole(first_gain), whole(first_shift), whole(value_bias[1:])]
+        + [whole(down_packed), columns(up_packed, 1, width)]
+        + [columns(query_key_value_weight, kind, width) for kind in (1, 2)],
+        [low, low, low, jax.ShapeDtypeStruct((tokens, LANES), jnp.bfloat16)],
+        [],
+        4 * tokens * width * width,
+    )
     all_keys = [keys] + [from_core(keys, by) for by in range(1, cores)]
     all_values = [values] + [from_core(values, by) for by in range(1, cores)]
-    queries, lora = enter((0,), [jax.ShapeDtypeStruct((tokens, LANES), jnp.bfloat16)])
+    (queries,) = over_tokens(
+        ask_kernel,
+        "ask",
+        tokens,
+        [tile(normed), tile(lora), whole(value_bias[:1]), columns(up_packed, 0, width)]
+        + [columns(query_key_value_weight, 0, width)],
+        [low],
+        [],
+        2 * tokens * width * width,
+    )
     attended, log_total = attend(far, queries, *all_keys, *all_values, marks, causal)
 
     hidden = expand_weight.shape[1]
@@ -762,38 +814,33 @@
     ]
     owned_values = owned(pulled[1 + cores :])
     owned_keys = owned(pulled[1 : 1 + cores])
-    grad_lora, down_sum, up_sum = over_tokens(
-        functools.partial(adapt_kernel, stripe, cores),
+    input_grad, grad_lora = over_tokens(
+        functools.partial(leave_kernel, stripe, cores),
+        "leave",
+        tokens,
+        [tile(x), whole(first_gain), whole(query_key_value_weight), whole(down_packed)]
+        + [whole(up_packed), tile(grad_middle), tile(pulled[0])]
+        + [tile(part) for part in (*owned_keys, *owned_values)],
+        [low, jax.ShapeDtypeStruct((tokens, LANES), jnp.bfloat16)],
+        [],
+        6 * tokens * width * width,
+    )
+    down_sum, up_sum = over_tokens(
+        functools.partial(adapt_kernel, cores),
         "adapt",
         tokens,
-        [tile(x), whole(first_gain), whole(first_shift), whole(up_packed), tile(lora)]
-        + [tile(part) for part in (pulled[0], *owned_values)],
-        [jax.ShapeDtypeStruct((tokens, LANES), jnp.bfloat16)],
+        [tile(part) for part in (normed, lora, grad_lora, pulled[0], *owned_values)],
+        [],
         sums,
-        1024 * tokens * width,
-    )
+        512 * tokens * width,
+    )
+    layer_out, down_sum = lax.optimization_barrier((layer_out, down_sum))
     up_parts = [
         adapter_scale * up_sum[j * rank : (j + 1) * rank, j * width : (j + 1) * width]
         for j in range(2)
     ]
-    adapter_sums = jnp.concatenate([*up_parts, down_sum], axis=0)
-    bits = ring.bit_length() - 1
-    adapter_sums = sum_over(adapter_sums, "seq", max(0, bits - 2), bits)
-    (input_grad,) = over_tokens(
-        functools.partial(leave_kernel, stripe, cores),
-        "leave",
-        tokens,
-        [tile(x), whole(first_gain), whole(query_key_value_weight), whole(down_packed)]
-        + [tile(part) for part in (grad_lora, grad_middle, pulled[0], *owned_keys, *owned_values)],
-        [low],
-        [],
-        6 * tokens * width * width,
-    )
-    input_grad, adapter_sums = lax.optimization_barrier((input_grad, adapter_sums))
     input_grad = spread_stripes(rows_back(input_grad))
-    for low in range(max(0, bits - 4), -1, -2) if bits > 2 else ():
-        adapter_sums = sum_over(adapter_sums, "seq", low, min(low + 2, bits - 2))
-    adapter_sums = sum_over(adapter_sums, "batch", 0, cores.bit_length() - 1)
+    adapter_sums = sum_everywhere(jnp.concatenate([*up_parts, down_sum], axis=0))
     adapter_sums = adapter_sums.reshape(2, 2, rank, width)
     up_map_gradient = adapter_sums[0]
     down_map_gradient = jnp.transpose(adapter_sums[1], (0, 2, 1))

time: 349 us -> 336 us (0.963); the launches traced: 347 us -> 339 us
  Pallas kernels: 204 us -> 190 us
  starting transfers between devices: 42.1 us -> 47.2 us
    all_to_all x2, waiting for transfers between devices: 24.7 us -> 0.01 us  [rows_back(): return lax.all_to_all(y, 'seq', 0, 0, tiled=True)]
    ppermute x7 -> x10, waiting for transfers between devices: 12.9 us -> 30.7 us  [exchanged(): return lax.ppermute(x, axis, [(i, i ^ by) for i in range(size)])]
    pallas_call x1, Pallas kernels: 61.2 us -> 50.3 us  [body(): pull(far, queries, grad_attended, attended, log_total, *all_keys, *all_va...]
    ppermute x9, waiting for transfers between devices: 6.19 us -> 11.8 us  [from_core(): lax.ppermute(x, 'batch', [(i, (i + by) % cores) for i in range(cores)])]
    ppermute x7 -> x10, starting transfers between devices: 7.96 us -> 12.2 us  [exchanged(): return lax.ppermute(x, axis, [(i, i ^ by) for i in range(size)])]
  transfers between devices with their start and end apart: 20 -> 23, of which waited for: 6 -> 13; matrix products, arithmetic and copies ran while one was open for 5% -> 6% of each run, Pallas kernels for 39% -> 31%
where the time goes in v1:
time: 336 us; the launch traced here: 339 us
  Pallas kernels  190 us (57%)
  waiting for transfers between devices  74.1 us (22%)
  starting transfers between devices  47.2 us (14%)
  other arithmetic  15.8 us (5%)
  local copies, waits for them, and re-layouts  9.1 us (3%)
    pallas_call x5, Pallas kernels, over_tokens(): pl.pallas_call(kernel, grid=(tokens // min(TOKEN_BLOCK, tokens),), in_spe...  104 us
    pallas_call x1, Pallas kernels, body(): pull(far, queries, grad_attended, attended, log_total, *all_keys, *all_va...  50.3 us
    all_to_all x2, waiting for transfers between devices, rows_home(): return lax.all_to_all(y, 'seq', 0, 0, tiled=True)  31.6 us
    ppermute x10, waiting for transfers between devices, exchanged(): return lax.ppermute(x, axis, [(i, i ^ by) for i in range(size)])  30.7 us
    pallas_call x1, Pallas kernels, body(): attend(far, queries, *all_keys, *all_values, marks, causal)  27.9 us
    all_to_all x2, starting transfers between devices, rows_home(): return lax.all_to_all(y, 'seq', 0, 0, tiled=True)  19.2 us
    all_to_all x2, starting transfers between devices, rows_back(): return lax.all_to_all(y, 'seq', 0, 0, tiled=True)  13.9 us
    ppermute x10, starting transfers between devices, exchanged(): return lax.ppermute(x, axis, [(i, i ^ by) for i in range(size)])  12.2 us
  transfers between devices with their start and end apart: 23, of which 13 were waited for; matrix products, arithmetic and copies ran while one was open for 6% of the time, Pallas kernels for 31%

profile of v1, /device:TPU:0, one launch (start us, length us, event | category | flops | bytes accessed | tf_op | source)
XLA Modules:
  0.0 338.6 jit_solution(4816894605307192706)
XLA Ops:
  2.8 2.2 collective-permute-done.1.refs_3_
  6.6 8.4 %all-to-all-start = ((bf16[16,520,128]{2,1,0:T(8,128)(2,1)}), bf16[16,520,128]{2,1,0:T(8,128)(2,1)}, u32[]{:S(2)}, u32[]{:S(2)}) async-start(bf16[16,520,128]{2,1,0:T(8,128)(2,1)} %gather_stripes.2), calls=%async_computation | async-start | bytes 4259840 | tf_op jit(solution)/shard_map/all_to_all | solution.py:127
  15.2 2.0 multiply_convert_fusion.refs_0_
  27.4 31.6 %all-to-all-done.x_ref = bf16[16,520,128]{2,1,0:T(8,128)(2,1)} async-done(((bf16[16,520,128]{2,1,0:T(8,128)(2,1)}), bf16[16,520,128]{2,1,0:T(8,128)(2,1)}, u32[]{:S(2)}, u32[]{:S(2)}) %all-to-all-start) | async-done | bytes 2129952 | tf_op jit(solution)/shard_map/all_to_all | solution.py:127
  58.9 10.8 %all-to-all-start.1 = ((bf16[16,512,128]{2,1,0:T(8,128)(2,1)}), bf16[16,512,128]{2,1,0:T(8,128)(2,1)}, u32[]{:S(2)}, u32[]{:S(2)}) async-start(bf16[16,512,128]{2,1,0:T(8,128)(2,1)} %copy-done), calls=%async_computation.1 | async-start | bytes 4194304 | tf_op jit(solution)/shard_map/all_to_all | solution.py:127
  70.3 11.4 %enter.1 = (bf16[1024,1024]{1,0:T(8,128)(2,1)}, bf16[1024,1024]{1,0:T(8,128)(2,1)}, bf16[1024,1024]{1,0:T(8,128)(2,1)}, bf16[1024,128]{1,0:T(8,128)(2,1)}) custom-call(bf16[16,520,128]{2,1,0:T(8,128)(2,1)} %all-to-all-done.x_ref, f32[1,1024]{1,0:T(1,128)} %bitcast.30, f32[1,1024]{1,0:T(1,128)} %bitcast.36, f32[1,1024]{1,0:T(1,128)} %get-tuple-element.112.bias_ref, ...), custom_call_target="tpu_custom_call" | custom-call | flops 4294967296 | bytes 22065152 | tf_op jit(solution)/shard_map/enter/pallas_call | solution.py:575
  85.8 6.5 %ask.1.refs_1_ = bf16[1024,1024]{1,0:T(8,128)(2,1)} custom-call(bf16[1024,1024]{1,0:T(8,128)(2,1)} %get-tuple-element.57.normed_ref, bf16[1024,128]{1,0:T(8,128)(2,1)} %get-tuple-element.58.lora_ref, f32[1,1024]{1,0:T(1,128)} %get-tuple-element.111.bias_ref, bf16[128,2048]{1,0:T(8,128)(2,1)} %fusion.1.up_ref, bf16[1024,3072]{1,0:T(8,128)(2,1)} %weight_ref.3), custom_call_target="tpu_custom_call" | custom-call | flops 2147483648 | bytes 11276288 | tf_op jit(solution)/shard_map/ask/pallas_call | solution.py:575
  93.5 27.9 %attend.1 = (bf16[1024,1024]{1,0:T(8,128)(2,1)}, f32[64,1024]{1,0:T(8,128)}) custom-call(s32[1]{0:T(128)S(6)} %convert_element_type.62.refs_0_, bf16[1024,1024]{1,0:T(8,128)(2,1)} %ask.1.refs_1_, bf16[1024,1024]{1,0:T(8,128)(2,1)} %get-tuple-element.59.refs_2_.refs_5_, bf16[1024,1024]{1,0:T(8,128)(2,1)} %collective-permute-done.3.refs_3_.refs_6_, ...), custom_call_target="tpu_custom_call" | custom-call | flops 4831838208 | bytes 12582912 | tf_op jit(solution)/shard_map/attend/pallas_call | solution.py:775
  121.4 64.8 %middle.1 = (bf16[1024,1024]{1,0:T(8,128)(2,1)}, bf16[1024,1024]{1,0:T(8,128)(2,1)}, bf16[1024,1024]{1,0:T(8,128)(2,1)}) custom-call(bf16[16,520,128]{2,1,0:T(8,128)(2,1)} %all-to-all-done.x_ref, bf16[1024,1024]{1,0:T(8,128)(2,1)} %get-tuple-element.62.attended_ref.refs_3_, bf16[16,512,128]{2,1,0:T(8,128)(2,1)} %all-to-all-done.1.cotangent_ref, ...), custom_call_target="tpu_custom_call" | custom-call | flops 38654705664 | bytes 31522816 | tf_op jit(solution)/shard_map/middle/pallas_call | solution.py:575
  186.2 7.1 %all-to-all-start.2 = ((bf16[16,64,1024]{2,1,0:T(8,128)(2,1)}), bf16[16,64,1024]{2,1,0:T(8,128)(2,1)}, u32[]{:S(2)}, u32[]{:S(2)}) async-start(bf16[16,64,1024]{2,1,0:T(8,128)(2,1)} %bitcast.24), calls=%async_computation.2 | async-start | bytes 4194304 | tf_op jit(solution)/shard_map/all_to_all | solution.py:133
  193.3 50.3 %pull.1 = (bf16[1024,1024]{1,0:T(8,128)(2,1)}, bf16[1024,1024]{1,0:T(8,128)(2,1)}, bf16[1024,1024]{1,0:T(8,128)(2,1)}, bf16[1024,1024]{1,0:T(8,128)(2,1)}, bf16[1024,1024]{1,0:T(8,128)(2,1)}) custom-call(s32[1]{0:T(128)S(6)} %convert_element_type.62.refs_0_, bf16[1024,1024]{1,0:T(8,128)(2,1)} %ask.1.refs_1_, bf16[1024,1024]{1,0:T(8,128)(2,1)} %get-tuple-element.70.refs_2_, ...), custom_call_target="tpu_custom_call" | custom-call | flops 12079595520 | bytes 25165824 | tf_op jit(solution)/shard_map/pull/pallas_call | solution.py:793
  244.3 4.0 %collective-permute-done.6.refs_1_ = bf16[1024,1024]{1,0:T(8,128)(2,1)} collective-permute-done((bf16[1024,1024]{1,0:T(8,128)(2,1)}, bf16[1024,1024]{1,0:T(8,128)(2,1)}, u32[]{:S(2)}, u32[]{:S(2)}) %collective-permute-start.6) | collective-permute-done | bytes 2097184 | tf_op jit(solution)/shard_map/ppermute | solution.py:146
  248.2 3.0 collective-permute-done.7.refs_3_.refs_1_
  251.2 16.0 %leave.1 = (bf16[1024,1024]{1,0:T(8,128)(2,1)}, bf16[1024,128]{1,0:T(8,128)(2,1)}) custom-call(bf16[16,520,128]{2,1,0:T(8,128)(2,1)} %all-to-all-done.x_ref, f32[1,1024]{1,0:T(1,128)} %bitcast.31, bf16[1024,3072]{1,0:T(8,128)(2,1)} %weight_ref.3, bf16[1024,128]{1,0:T(8,128)(2,1)} %pad.13.down_ref, bf16[128,2048]{1,0:T(8,128)(2,1)} %fusion.1.up_ref, ...), custom_call_target="tpu_custom_call" | custom-call | flops 6442450944 | bytes 24154112 | tf_op jit(solution)/shard_map/leave/pallas_call | solution.py:575
  267.2 6.9 %all-to-all-start.3 = ((bf16[16,64,1024]{2,1,0:T(8,128)(2,1)}), bf16[16,64,1024]{2,1,0:T(8,128)(2,1)}, u32[]{:S(2)}, u32[]{:S(2)}) async-start(bf16[16,64,1024]{2,1,0:T(8,128)(2,1)} %bitcast.23), calls=%async_computation.3 | async-start | bytes 4194304 | tf_op jit(solution)/shard_map/all_to_all | solution.py:133
  275.5 2.6 collective-permute-done.5.refs_1_
  278.2 2.6 spread_stripes.2
  280.8 5.4 %adapt.1 = (f32[8,1024]{1,0:T(8,128)}, f32[8,2048]{1,0:T(8,128)}) custom-call(bf16[1024,1024]{1,0:T(8,128)(2,1)} %get-tuple-element.57.normed_ref, bf16[1024,128]{1,0:T(8,128)(2,1)} %get-tuple-element.58.lora_ref, bf16[1024,128]{1,0:T(8,128)(2,1)} %get-tuple-element.84.grad_lora_ref, bf16[1024,1024]{1,0:T(8,128)(2,1)} %get-tuple-element.79.grad_query_ref, ...), custom_call_target="tpu_custom_call" | custom-call | flops 536870912 | bytes 9011200 | tf_op jit(solution)/shard_map/adapt/pallas_call | solution.py:575
  293.7 2.2 collective-permute-done.11
  296.0 8.3 %collective-permute-done.12 = f32[4,1024]{1,0:T(4,128)S(1)} collective-permute-done((f32[4,1024]{1,0:T(4,128)S(1)}, f32[4,1024]{1,0:T(4,128)S(1)}, u32[]{:S(2)}, u32[]{:S(2)}) %collective-permute-start.12) | collective-permute-done | bytes 16416 | tf_op jit(solution)/shard_map/ppermute | solution.py:160
  304.4 4.3 %collective-permute-start.15 = (f32[4,1024]{1,0:T(4,128)S(1)}, f32[4,1024]{1,0:T(4,128)S(1)}, u32[]{:S(2)}, u32[]{:S(2)}) collective-permute-start(f32[4,1024]{1,0:T(4,128)S(1)} %add_add_fusion.1), channel_id=1, source_target_pairs={{0,24},{2,26},{4,28},{6,30},{8,16},{10,18},{12,20},{14,22},{16,8},... | collective-permute-start | bytes 49160 | tf_op jit(solution)/shard_map/ppermute | solution.py:160
  309.5 14.2 %collective-permute-done.14 = f32[4,1024]{1,0:T(4,128)S(1)} collective-permute-done((f32[4,1024]{1,0:T(4,128)S(1)}, f32[4,1024]{1,0:T(4,128)S(1)}, u32[]{:S(2)}, u32[]{:S(2)}) %collective-permute-start.14) | collective-permute-done | bytes 16416 | tf_op jit(solution)/shard_map/ppermute | solution.py:160
  329.0 2.6 collective-permute-done.18
  335.7 2.6 spread_stripes.3
  (132 shorter events, 38.3 us)
Async XLA Ops:
  2.2 2.8 collective-permute-start
  2.7 2.3 collective-permute-start.1
  6.6 52.3 %all-to-all-start = ((bf16[16,520,128]{2,1,0:T(8,128)(2,1)}), bf16[16,520,128]{2,1,0:T(8,128)(2,1)}, u32[]{:S(2)}, u32[]{:S(2)}) async-start(bf16[16,520,128]{2,1,0:T(8,128)(2,1)} %gather_stripes.2), calls=%async_computation | async-start | bytes 4259840 | tf_op jit(solution)/shard_map/all_to_all | solution.py:127
  18.4 7.1 %collective-permute-start.2 = (bf16[8,64,1024]{2,1,0:T(8,128)(2,1)}, bf16[8,64,1024]{2,1,0:T(8,128)(2,1)S(1)}, u32[]{:S(2)}, u32[]{:S(2)}) collective-permute-start(bf16[8,64,1024]{2,1,0:T(8,128)(2,1)} %constant_dynamic-slice_fusion.11), channel_id=1, source_target_pairs={{0,1},{1,0},{2,3},{3,2},{4,5},{5,4},{6,7},{7,6},{8,9},{9,8},{10,11... | collective-permute-start | bytes 3145736 | tf_op jit(solution)/shard_map/ppermute | solution.py:146
  58.9 62.5 %all-to-all-start.1 = ((bf16[16,512,128]{2,1,0:T(8,128)(2,1)}), bf16[16,512,128]{2,1,0:T(8,128)(2,1)}, u32[]{:S(2)}, u32[]{:S(2)}) async-start(bf16[16,512,128]{2,1,0:T(8,128)(2,1)} %copy-done), calls=%async_computation.1 | async-start | bytes 4194304 | tf_op jit(solution)/shard_map/all_to_all | solution.py:127
  81.7 11.8 %collective-permute-start.3 = (bf16[1024,1024]{1,0:T(8,128)(2,1)}, bf16[1024,1024]{1,0:T(8,128)(2,1)}, u32[]{:S(2)}, u32[]{:S(2)}) collective-permute-start(bf16[1024,1024]{1,0:T(8,128)(2,1)} %get-tuple-element.59.refs_2_.refs_5_), channel_id=1, source_target_pairs={{0,1},{1,0},{2,3},{3,2},{4,5},{5,4},{6,7},{7,6},{8,9},{9,8},{10,11... | collective-permute-start | bytes 6291464 | tf_op jit(solution)/shard_map/ppermute | solution.py:146
  81.7 11.8 %collective-permute-start.4 = (bf16[1024,1024]{1,0:T(8,128)(2,1)}, bf16[1024,1024]{1,0:T(8,128)(2,1)}, u32[]{:S(2)}, u32[]{:S(2)}) collective-permute-start(bf16[1024,1024]{1,0:T(8,128)(2,1)} %get-tuple-element.60.refs_4_.refs_7_), channel_id=1, source_target_pairs={{0,1},{1,0},{2,3},{3,2},{4,5},{5,4},{6,7},{7,6},{8,9},{9,8},{10,11... | collective-permute-start | bytes 6291464 | tf_op jit(solution)/shard_map/ppermute | solution.py:146
  186.2 57.4 %all-to-all-start.2 = ((bf16[16,64,1024]{2,1,0:T(8,128)(2,1)}), bf16[16,64,1024]{2,1,0:T(8,128)(2,1)}, u32[]{:S(2)}, u32[]{:S(2)}) async-start(bf16[16,64,1024]{2,1,0:T(8,128)(2,1)} %bitcast.24), calls=%async_computation.2 | async-start | bytes 4194304 | tf_op jit(solution)/shard_map/all_to_all | solution.py:133
  243.7 4.6 %collective-permute-start.6 = (bf16[1024,1024]{1,0:T(8,128)(2,1)}, bf16[1024,1024]{1,0:T(8,128)(2,1)}, u32[]{:S(2)}, u32[]{:S(2)}) collective-permute-start(bf16[1024,1024]{1,0:T(8,128)(2,1)} %get-tuple-element.81), channel_id=1, source_target_pairs={{0,1},{1,0},{2,3},{3,2},{4,5},{5,4},{6,7},{7,6},{8,9},{9,8},{10,11... | collective-permute-start | bytes 6291464 | tf_op jit(solution)/shard_map/ppermute | solution.py:146
  243.8 7.5 %collective-permute-start.7 = (bf16[1024,1024]{1,0:T(8,128)(2,1)}, bf16[1024,1024]{1,0:T(8,128)(2,1)}, u32[]{:S(2)}, u32[]{:S(2)}) collective-permute-start(bf16[1024,1024]{1,0:T(8,128)(2,1)} %get-tuple-element.83), channel_id=1, source_target_pairs={{0,1},{1,0},{2,3},{3,2},{4,5},{5,4},{6,7},{7,6},{8,9},{9,8},{10,11... | collective-permute-start | bytes 6291464 | tf_op jit(solution)/shard_map/ppermute | solution.py:146
  267.2 64.4 %all-to-all-start.3 = ((bf16[16,64,1024]{2,1,0:T(8,128)(2,1)}), bf16[16,64,1024]{2,1,0:T(8,128)(2,1)}, u32[]{:S(2)}, u32[]{:S(2)}) async-start(bf16[16,64,1024]{2,1,0:T(8,128)(2,1)} %bitcast.23), calls=%async_computation.3 | async-start | bytes 4194304 | tf_op jit(solution)/shard_map/all_to_all | solution.py:133
  275.4 2.7 collective-permute-start.5
  286.2 48.9 %copy-start.9 = (f32[2,1024,4]{1,2,0:T(4,128)S(1)}, f32[2,1024,4]{1,2,0:T(4,128)}, u32[]{:S(2)}) copy-start(f32[2,1024,4]{1,2,0:T(4,128)} %param.43) | copy-start | bytes 98308
  287.8 1.3 collective-permute-start.9
  289.9 3.8 %collective-permute-start.10 = (f32[4,1024]{1,0:T(4,128)S(1)}, f32[4,1024]{1,0:T(4,128)S(1)}, u32[]{:S(2)}, u32[]{:S(2)}) collective-permute-start(f32[4,1024]{1,0:T(4,128)S(1)} %get-tuple-element.100), channel_id=1, source_target_pairs={{0,2},{2,0},{4,6},{6,4},{8,10},{10,8},{12,14},{14,12},{16,18},{18,... | collective-permute-start | bytes 49160 | tf_op jit(solution)/shard_map/ppermute | solution.py:160
  291.9 4.1 %collective-permute-start.11 = (f32[4,1024]{1,0:T(4,128)S(1)}, f32[4,1024]{1,0:T(4,128)S(1)}, u32[]{:S(2)}, u32[]{:S(2)}) collective-permute-start(f32[4,1024]{1,0:T(4,128)S(1)} %get-tuple-element.102), channel_id=1, source_target_pairs={{0,4},{2,6},{4,0},{6,2},{8,12},{10,14},{12,8},{14,10},{16,20},{18,... | collective-permute-start | bytes 49160 | tf_op jit(solution)/shard_map/ppermute | solution.py:160
  293.3 10.9 %collective-permute-start.12 = (f32[4,1024]{1,0:T(4,128)S(1)}, f32[4,1024]{1,0:T(4,128)S(1)}, u32[]{:S(2)}, u32[]{:S(2)}) collective-permute-start(f32[4,1024]{1,0:T(4,128)S(1)} %get-tuple-element.101), channel_id=1, source_target_pairs={{0,6},{2,4},{4,2},{6,0},{8,14},{10,12},{12,10},{14,8},{16,22},{18,... | collective-permute-start | bytes 49160 | tf_op jit(solution)/shard_map/ppermute | solution.py:160
  304.3 5.2 %collective-permute-start.13 = (f32[4,1024]{1,0:T(4,128)S(1)}, f32[4,1024]{1,0:T(4,128)S(1)}, u32[]{:S(2)}, u32[]{:S(2)}) collective-permute-start(f32[4,1024]{1,0:T(4,128)S(1)} %add_add_fusion.1), channel_id=1, source_target_pairs={{0,8},{2,10},{4,12},{6,14},{8,0},{10,2},{12,4},{14,6},{16,24},{18,... | collective-permute-start | bytes 49160 | tf_op jit(solution)/shard_map/ppermute | solution.py:160
  304.3 19.4 %collective-permute-start.14 = (f32[4,1024]{1,0:T(4,128)S(1)}, f32[4,1024]{1,0:T(4,128)S(1)}, u32[]{:S(2)}, u32[]{:S(2)}) collective-permute-start(f32[4,1024]{1,0:T(4,128)S(1)} %add_add_fusion.1), channel_id=1, source_target_pairs={{0,16},{2,18},{4,20},{6,22},{8,24},{10,26},{12,28},{14,30},{16,0},... | collective-permute-start | bytes 49160 | tf_op jit(solution)/shard_map/ppermute | solution.py:160
  304.4 19.3 %collective-permute-start.15 = (f32[4,1024]{1,0:T(4,128)S(1)}, f32[4,1024]{1,0:T(4,128)S(1)}, u32[]{:S(2)}, u32[]{:S(2)}) collective-permute-start(f32[4,1024]{1,0:T(4,128)S(1)} %add_add_fusion.1), channel_id=1, source_target_pairs={{0,24},{2,26},{4,28},{6,30},{8,16},{10,18},{12,20},{14,22},{16,8},... | collective-permute-start | bytes 49160 | tf_op jit(solution)/shard_map/ppermute | solution.py:160
  323.7 4.0 %collective-permute-start.16 = (f32[4,1024]{1,0:T(4,128)S(1)}, f32[4,1024]{1,0:T(4,128)S(1)}, u32[]{:S(2)}, u32[]{:S(2)}) collective-permute-start(f32[4,1024]{1,0:T(4,128)S(1)} %add_add_fusion), channel_id=1, source_target_pairs={{0,2},{2,0},{4,6},{6,4},{8,10},{10,8},{12,14},{14,12},{16,18},{18,... | collective-permute-start | bytes 49160 | tf_op jit(solution)/shard_map/ppermute | solution.py:160
  325.3 3.7 %collective-permute-start.17 = (f32[4,1024]{1,0:T(4,128)S(1)}, f32[4,1024]{1,0:T(4,128)S(1)}, u32[]{:S(2)}, u32[]{:S(2)}) collective-permute-start(f32[4,1024]{1,0:T(4,128)S(1)} %add_add_fusion), channel_id=1, source_target_pairs={{0,4},{2,6},{4,0},{6,2},{8,12},{10,14},{12,8},{14,10},{16,20},{18,... | collective-permute-start | bytes 49160 | tf_op jit(solution)/shard_map/ppermute | solution.py:160
  326.9 4.6 %collective-permute-start.18 = (f32[4,1024]{1,0:T(4,128)S(1)}, f32[4,1024]{1,0:T(4,128)S(1)}, u32[]{:S(2)}, u32[]{:S(2)}) collective-permute-start(f32[4,1024]{1,0:T(4,128)S(1)} %add_add_fusion), channel_id=1, source_target_pairs={{0,6},{2,4},{4,2},{6,0},{8,14},{10,12},{12,10},{14,8},{16,22},{18,... | collective-permute-start | bytes 49160 | tf_op jit(solution)/shard_map/ppermute | solution.py:160
  333.0 2.7 collective-permute-start.8
  (22 other events, 218.8 us)

commit v2 on v1

--- a/solution.py
+++ b/solution.py
@@ -152,7 +152,7 @@
     return terms[0]
 
 
-def sum_everywhere(x):
+def sum_everywhere(x, before_last):
     ring, cores = lax.axis_size("seq"), lax.axis_size("batch")
     assert ring & (ring - 1) == 0 and cores & (cores - 1) == 0
 
@@ -181,9 +181,10 @@
             [mine] + [exchanged(mine, "seq", ring, by * step) for by in range(1, width)]
         )
         step *= width
+    mine, before_last = lax.optimization_barrier((mine, before_last))
     held = [mine] + [exchanged(mine, "seq", ring, by) for by in range(1, near)]
     held = jnp.concatenate(held)
-    return jnp.concatenate([shares_of(held, me ^ at) for at in range(near)])
+    return jnp.concatenate([shares_of(held, me ^ at) for at in range(near)]), before_last
 
 
 def lane_masks(dtype):
@@ -203,10 +204,10 @@
 
 
 def attend_block(cores, reach, skipped, *refs):
-    far_ref, query_ref = refs[:2]
-    key_refs = refs[2 : 2 + cores]
-    value_refs = refs[2 + cores : 2 + 2 * cores]
-    mark_ref, causal_ref, out_ref, log_ref, key_heads, turned_values = refs[2 + 2 * cores :]
+    query_ref = refs[0]
+    key_refs = refs[1 : 1 + cores]
+    value_refs = refs[1 + cores : 1 + 2 * cores]
+    mark_ref, causal_ref, out_ref, log_ref, key_heads, turned_values = refs[1 + 2 * cores :]
     slots = slot_row()
     heads = lane_masks(jnp.bfloat16)
     half = LANES // 2
@@ -271,13 +272,25 @@
     every(skipped)
 
 
-def either_way(block, cores, reach, *refs):
-    far_ref, query_ref = refs[:2]
-    if query_ref.shape[0] // QUERY_BLOCK <= reach:
+def either_way(block, cores, reach, mark_at, *refs):
+    refs, flag_ref = refs[:-1], refs[-1]
+    mark_ref = refs[mark_at]
+    blocks = refs[0].shape[0] // QUERY_BLOCK
+    if blocks <= reach:
         block(cores, reach, False, *refs)
         return
-    pl.when(far_ref[0] == 1)(functools.partial(block, cores, reach, False, *refs))
-    pl.when(far_ref[0] != 1)(functools.partial(block, cores, reach, True, *refs))
+
+    @pl.when(pl.program_id(0) == 0)
+    def _():
+        asking = mark_ref[pl.ds((blocks - 1) * QUERY_BLOCK, 16), :].astype(jnp.float32)[:1]
+        shared = jnp.zeros_like(asking)
+        for k in range(cores):
+            last = (k * blocks + blocks - reach) * QUERY_BLOCK - 16
+            shared = shared + asking * mark_ref[pl.ds(last, 16), :].astype(jnp.float32)[15:]
+        flag_ref[0] = (jnp.sum(shared) > 0.0).astype(jnp.int32)
+
+    pl.when(flag_ref[0] == 1)(functools.partial(block, cores, reach, False, *refs))
+    pl.when(flag_ref[0] != 1)(functools.partial(block, cores, reach, True, *refs))
 
 
 def spread(wide):
@@ -286,11 +299,11 @@
 
 
 def pull_block(cores, reach, skipped, *refs):
-    far_ref, query_ref, grad_ref, out_ref, log_ref = refs[:5]
-    key_refs = refs[5 : 5 + cores]
-    value_refs = refs[5 + cores : 5 + 2 * cores]
-    mark_ref, causal_ref = refs[5 + 2 * cores : 7 + 2 * cores]
-    outs = refs[7 + 2 * cores :]
+    query_ref, grad_ref, out_ref, log_ref = refs[:4]
+    key_refs = refs[4 : 4 + cores]
+    value_refs = refs[4 + cores : 4 + 2 * cores]
+    mark_ref, causal_ref = refs[4 + 2 * cores : 6 + 2 * cores]
+    outs = refs[6 + 2 * cores :]
     slots = slot_row()
     excluded = jnp.asarray(masked_score, jnp.bfloat16)
     grad_query_ref = outs[0]
@@ -410,21 +423,19 @@
 
 
 def enter_kernel(
-    stripe, x_ref, gain_ref, shift_ref, bias_ref, down_ref, up_ref, key_weight_ref,
-    value_weight_ref, key_ref, value_ref, normed_ref, lora_ref,
+    stripe, x_ref, gain_ref, shift_ref, bias_ref, key_weight_ref, value_weight_ref,
+    key_ref, value_ref, normed_ref,
 ):
     shaped, _ = standardized(tokens_of(x_ref, stripe, key_ref.shape[1]).astype(jnp.float32))
     normed = (shaped * gain_ref[...] + shift_ref[...]).astype(jnp.bfloat16)
     normed_ref[...] = normed
     key_ref[...] = matmul_rows(normed, key_weight_ref[...]).astype(jnp.bfloat16)
-    lora = matmul_rows(normed, down_ref[...]).astype(jnp.bfloat16)
-    lora_ref[...] = lora
-    value = matmul_rows(normed, value_weight_ref[...]) + matmul_rows(lora, up_ref[...])
+    value = matmul_rows(normed, value_weight_ref[...])
     value_ref[...] = (value + bias_ref[...]).astype(jnp.bfloat16)
 
 
-def ask_kernel(normed_ref, lora_ref, bias_ref, up_ref, weight_ref, query_ref):
-    query = matmul_rows(normed_ref[...], weight_ref[...]) + matmul_rows(lora_ref[...], up_ref[...])
+def ask_kernel(normed_ref, bias_ref, weight_ref, query_ref):
+    query = matmul_rows(normed_ref[...], weight_ref[...])
     query_ref[...] = (query + bias_ref[...]).astype(jnp.bfloat16)
 
 
@@ -499,9 +510,7 @@
     return out.astype(jnp.bfloat16)
 
 
-def adapt_kernel(
-    cores, normed_ref, lora_ref, grad_lora_ref, grad_query_ref, *refs
-):
+def adapt_kernel(cores, down_ref, up_ref, normed_ref, grad_query_ref, *refs):
     down_sum_ref, up_sum_ref = refs[cores:]
     slots = down_sum_ref.shape[0]
 
@@ -511,32 +520,29 @@
         up_sum_ref[...] = jnp.zeros_like(up_sum_ref)
 
     width = grad_query_ref.shape[1]
-    lora = lora_ref[...]
-    down_sum_ref[...] += matmul_over(grad_lora_ref[...], normed_ref[...])[:slots]
-    up_sum_ref[:, :width] += matmul_over(lora, grad_query_ref[...])[:slots]
-    up_sum_ref[:, width:] += matmul_over(lora, total(refs[:cores]))[:slots]
-
-
-def leave_kernel(
-    stripe, cores, x_ref, gain_ref, weight_ref, down_ref, up_ref, grad_middle_ref,
-    grad_query_ref, *refs,
-):
-    key_refs, value_refs = refs[:cores], refs[cores : 2 * cores]
-    grad_ref, grad_lora_ref = refs[2 * cores :]
-    width = grad_query_ref.shape[1]
+    normed = normed_ref[...]
     grad_query = grad_query_ref[...]
-    grad_value = total(value_refs)
+    grad_value = total(refs[:cores])
+    lora = matmul_rows(normed, down_ref[...]).astype(jnp.bfloat16)
     grad_lora = matmul_back(grad_query, up_ref[:, :width]) + matmul_back(
         grad_value, up_ref[:, width:]
     )
-    grad_lora = grad_lora.astype(jnp.bfloat16)
-    grad_lora_ref[...] = grad_lora
+    down_sum_ref[...] += matmul_over(grad_lora.astype(jnp.bfloat16), normed)[:slots]
+    up_sum_ref[:, :width] += matmul_over(lora, grad_query)[:slots]
+    up_sum_ref[:, width:] += matmul_over(lora, grad_value)[:slots]
+
+
+def leave_kernel(
+    stripe, cores, x_ref, gain_ref, query_weight_ref, key_weight_ref, value_weight_ref,
+    grad_middle_ref, grad_query_ref, *refs,
+):
+    key_refs, value_refs, grad_ref = refs[:cores], refs[cores : 2 * cores], refs[-1]
+    width = grad_query_ref.shape[1]
     shaped, spread_inverse = standardized(tokens_of(x_ref, stripe, width).astype(jnp.float32))
     grad_normed = (
-        matmul_back(grad_query, weight_ref[:, :width])
-        + matmul_back(total(key_refs), weight_ref[:, width : 2 * width])
-        + matmul_back(grad_value, weight_ref[:, 2 * width :])
-        + matmul_back(grad_lora, down_ref[...])
+        matmul_back(grad_query_ref[...], query_weight_ref[...])
+        + matmul_back(total(key_refs), key_weight_ref[...])
+        + matmul_back(total(value_refs), value_weight_ref[...])
     )
     grad = norm_pull(grad_normed * gain_ref[...], shaped, spread_inverse)
     grad_ref[...] = (grad_middle_ref[...].astype(jnp.float32) + grad).astype(jnp.bfloat16)
@@ -589,10 +595,10 @@
 
 
 def attention_calls(tokens, width, cores, reach):
-    pair = pl.BlockSpec((tokens, LANES), lambda p, far: (0, p))
-    marks = pl.BlockSpec((cores * tokens, LANES), lambda p, far: (0, 0))
-    causal = pl.BlockSpec((cores * QUERY_BLOCK, QUERY_BLOCK), lambda p, far: (0, 0))
-    logs = pl.BlockSpec((8, tokens), lambda p, far: (p, 0))
+    pair = pl.BlockSpec((tokens, LANES), lambda p: (0, p))
+    marks = pl.BlockSpec((cores * tokens, LANES), lambda p: (0, 0))
+    causal = pl.BlockSpec((cores * QUERY_BLOCK, QUERY_BLOCK), lambda p: (0, 0))
+    logs = pl.BlockSpec((8, tokens), lambda p: (p, 0))
     grid = (width // LANES,)
     blocks = tokens // QUERY_BLOCK
     pairs = sum(min(n, reach) + 1 for n in range(blocks)) * cores * QUERY_BLOCK**2 * HEADS
@@ -604,15 +610,15 @@
     )
     low_scratch = functools.partial(pltpu.VMEM, dtype=jnp.bfloat16)
     forward = pl.pallas_call(
-        functools.partial(either_way, attend_block, cores, reach),
-        grid_spec=pltpu.PrefetchScalarGridSpec(
-            num_scalar_prefetch=1,
+        functools.partial(either_way, attend_block, cores, reach, 1 + 2 * cores),
+        grid_spec=pl.GridSpec(
             grid=grid,
             in_specs=[pair] * (1 + 2 * cores) + [marks, causal],
             out_specs=[pair, logs],
             scratch_shapes=[
                 low_scratch((2, cores * tokens, LANES)),
                 low_scratch((2, LANES // 2 + 16, cores * tokens)),
+                pltpu.SMEM((1,), jnp.int32),
             ],
         ),
         out_shape=[low, log_rows],
@@ -625,9 +631,8 @@
         name="attend",
     )
     backward = pl.pallas_call(
-        functools.partial(either_way, pull_block, cores, reach),
-        grid_spec=pltpu.PrefetchScalarGridSpec(
-            num_scalar_prefetch=1,
+        functools.partial(either_way, pull_block, cores, reach, 4 + 2 * cores),
+        grid_spec=pl.GridSpec(
             grid=grid,
             in_specs=[pair, pair, pair, logs] + [pair] * (2 * cores) + [marks, causal],
             out_specs=[pair] * (1 + 2 * cores),
@@ -640,6 +645,7 @@
                 low_scratch((LANES, cores * tokens)),
                 pltpu.VMEM((LANES, tokens), jnp.float32),
                 pltpu.VMEM((8, tokens), jnp.float32),
+                pltpu.SMEM((1,), jnp.int32),
             ],
         ),
         out_shape=[low] * (1 + 2 * cores),
@@ -722,41 +728,45 @@
         axis=1,
     )
     up_packed = (adapter_scale * up_packed).astype(jnp.bfloat16)
+
+    def folded(which, j):
+        added = matmul_rows(
+            adapter_down_maps[j].astype(jnp.bfloat16), adapter_up_maps[j].astype(jnp.bfloat16)
+        )
+        frozen = query_key_value_weight[:, which * width : (which + 1) * width]
+        return (frozen.astype(jnp.float32) + adapter_scale * added).astype(jnp.bfloat16)
+
+    query_weight, value_weight = folded(0, 0), folded(2, 1)
     value_bias = query_value_bias.astype(jnp.float32)
     out_bias, up_bias, down_bias = map(row_of, (attention_out_bias, expand_bias, contract_bias))
     (
         x, stripes, causal, first_gain, first_shift, second_gain, second_shift,
-        value_bias, out_bias, up_bias, down_bias, down_packed, up_packed,
+        value_bias, out_bias, up_bias, down_bias, down_packed, up_packed, query_weight,
+        value_weight,
     ) = lax.optimization_barrier(
         (
             x, stripes, causal, first_gain, first_shift, second_gain, second_shift,
-            value_bias, out_bias, up_bias, down_bias, down_packed, up_packed,
+            value_bias, out_bias, up_bias, down_bias, down_packed, up_packed, query_weight,
+            value_weight,
         )
     )
     cotangent_home = rows_home(stripes)
-    row_segments = x[:, width // LANES * stripe, :].astype(jnp.int32)
-    parts = row_segments.reshape(ring, cores, stripe)
+    parts = x[:, width // LANES * stripe, :].reshape(ring, cores, stripe)
     turns = [lax.rem(core - by + cores, cores) for by in range(cores)]
     parts = [lax.dynamic_index_in_dim(parts, turn, 1, keepdims=False) for turn in turns]
-    slot = jnp.arange(LANES, dtype=jnp.int32) % (LANES // 2)
+    slot = (jnp.arange(LANES, dtype=jnp.int32) % (LANES // 2)).astype(jnp.bfloat16)
     marks = jnp.concatenate(parts).reshape(cores * tokens, 1) == slot[None, :]
     marks = marks.astype(jnp.bfloat16)
-    row_segments = row_segments.reshape(ring * tokens_here)
-    blocks = tokens // QUERY_BLOCK
-    last = max(0, blocks - 1 - reach)
-    far = row_segments[span * (last + 1) - 1] >= row_segments[span * (blocks - 1)]
-    far = far.astype(jnp.int32)[None]
 
     low = jax.ShapeDtypeStruct((tokens, width), jnp.bfloat16)
 
-    keys, values, normed, lora = over_tokens(
+    keys, values, normed = over_tokens(
         functools.partial(enter_kernel, stripe),
         "enter",
         tokens,
         [tile(x), whole(first_gain), whole(first_shift), whole(value_bias[1:])]
-        + [whole(down_packed), columns(up_packed, 1, width)]
-        + [columns(query_key_value_weight, kind, width) for kind in (1, 2)],
-        [low, low, low, jax.ShapeDtypeStruct((tokens, LANES), jnp.bfloat16)],
+        + [columns(query_key_value_weight, 1, width), whole(value_weight)],
+        [low, low, low],
         [],
         4 * tokens * width * width,
     )
@@ -766,13 +776,12 @@
         ask_kernel,
         "ask",
         tokens,
-        [tile(normed), tile(lora), whole(value_bias[:1]), columns(up_packed, 0, width)]
-        + [columns(query_key_value_weight, 0, width)],
+        [tile(normed), whole(value_bias[:1]), whole(query_weight)],
         [low],
         [],
         2 * tokens * width * width,
     )
-    attended, log_total = attend(far, queries, *all_keys, *all_values, marks, causal)
+    attended, log_total = attend(queries, *all_keys, *all_values, marks, causal)
 
     hidden = expand_weight.shape[1]
     layer_result, grad_middle, grad_attended = over_tokens(
@@ -791,7 +800,6 @@
     layer_out = rows_back(layer_result)
 
     pulled = pull(
-        far,
         queries,
         grad_attended,
         attended,
@@ -803,7 +811,6 @@
     )
 
     layer_out, pulled = lax.optimization_barrier((layer_out, pulled))
-    layer_out = spread_stripes(layer_out)
 
     def owned(parts):
         return [parts[0]] + [from_core(parts[by], -by) for by in range(1, cores)]
@@ -814,33 +821,36 @@
     ]
     owned_values = owned(pulled[1 + cores :])
     owned_keys = owned(pulled[1 : 1 + cores])
-    input_grad, grad_lora = over_tokens(
+    (input_grad,) = over_tokens(
         functools.partial(leave_kernel, stripe, cores),
         "leave",
         tokens,
-        [tile(x), whole(first_gain), whole(query_key_value_weight), whole(down_packed)]
-        + [whole(up_packed), tile(grad_middle), tile(pulled[0])]
-        + [tile(part) for part in (*owned_keys, *owned_values)],
-        [low, jax.ShapeDtypeStruct((tokens, LANES), jnp.bfloat16)],
+        [tile(x), whole(first_gain), whole(query_weight)]
+        + [columns(query_key_value_weight, 1, width), whole(value_weight)]
+        + [tile(part) for part in (grad_middle, pulled[0], *owned_keys, *owned_values)],
+        [low],
         [],
         6 * tokens * width * width,
     )
+    input_grad, normed = lax.optimization_barrier((input_grad, normed))
     down_sum, up_sum = over_tokens(
         functools.partial(adapt_kernel, cores),
         "adapt",
         tokens,
-        [tile(part) for part in (normed, lora, grad_lora, pulled[0], *owned_values)],
+        [whole(down_packed), whole(up_packed)]
+        + [tile(part) for part in (normed, pulled[0], *owned_values)],
         [],
         sums,
-        512 * tokens * width,
-    )
-    layer_out, down_sum = lax.optimization_barrier((layer_out, down_sum))
+        1024 * tokens * width,
+    )
+    layer_out, down_sum = lax.optimization_barrier((spread_stripes(layer_out), down_sum))
     up_parts = [
         adapter_scale * up_sum[j * rank : (j + 1) * rank, j * width : (j + 1) * width]
         for j in range(2)
     ]
-    input_grad = spread_stripes(rows_back(input_grad))
-    adapter_sums = sum_everywhere(jnp.concatenate([*up_parts, down_sum], axis=0))
+    adapter_sums = jnp.concatenate([*up_parts, down_sum], axis=0)
+    adapter_sums, input_grad = sum_everywhere(adapter_sums, rows_back(input_grad))
+    input_grad = spread_stripes(input_grad)
     adapter_sums = adapter_sums.reshape(2, 2, rank, width)
     up_map_gradient = adapter_sums[0]
     down_map_gradient = jnp.transpose(adapter_sums[1], (0, 2, 1))

time: 336 us -> 329 us (0.979)
  waiting for transfers between devices: 74.1 us -> 55.8 us
  matrix products: 0 us -> 7.45 us
  other arithmetic: 15.8 us -> 20.5 us
    all_to_all x2, waiting for transfers between devices: 31.6 us -> 17.4 us  [rows_home(): return lax.all_to_all(y, 'seq', 0, 0, tiled=True)]
    dot_general x0 -> x2, matrix products: none -> 7.45 us  [matmul_rows(): lax.dot_general(left_side, right_side, (((1,), (0,)), ((), ())), preferre...]
    reshape x7, other arithmetic: 4.18 us -> 8.95 us  [row_of(): return vector.astype(jnp.float32).reshape(1, -1)]
    ppermute x10, waiting for transfers between devices: 30.7 us -> 26.6 us  [exchanged(): return lax.ppermute(x, axis, [(i, i ^ by) for i in range(size)])]
  transfers between devices with their start and end apart: 23 -> 23, of which waited for: 13 -> 11; matrix products, arithmetic and copies ran while one was open for 6% -> 11% of each run, Pallas kernels for 31% -> 32%
where the time goes in v2:
time: 329 us; the launch traced here: 331 us
  Pallas kernels  189 us (57%)
  waiting for transfers between devices  55.8 us (17%)
  starting transfers between devices  47.2 us (14%)
  other arithmetic  20.5 us (6%)
  local copies, waits for them, and re-layouts  9.85 us (3%)
  matrix products  7.45 us (2%)
    pallas_call x5, Pallas kernels, over_tokens(): pl.pallas_call(kernel, grid=(tokens // min(TOKEN_BLOCK, tokens),), in_spe...  103 us
    pallas_call x1, Pallas kernels, body(): pull(queries, grad_attended, attended, log_total, *all_keys, *all_values,...  50.4 us
    pallas_call x1, Pallas kernels, body(): attended, log_total = attend(queries, *all_keys, *all_values, marks, causal)  28.1 us
    ppermute x10, waiting for transfers between devices, exchanged(): return lax.ppermute(x, axis, [(i, i ^ by) for i in range(size)])  26.6 us
    all_to_all x2, starting transfers between devices, rows_home(): return lax.all_to_all(y, 'seq', 0, 0, tiled=True)  19.2 us
    all_to_all x2, waiting for transfers between devices, rows_home(): return lax.all_to_all(y, 'seq', 0, 0, tiled=True)  17.4 us
    all_to_all x2, starting transfers between devices, rows_back(): return lax.all_to_all(y, 'seq', 0, 0, tiled=True)  14 us
    ppermute x10, starting transfers between devices, exchanged(): return lax.ppermute(x, axis, [(i, i ^ by) for i in range(size)])  12.2 us
  transfers between devices with their start and end apart: 23, of which 11 were waited for; matrix products, arithmetic and copies ran while one was open for 11% of the time, Pallas kernels for 32%

profile of v2, /device:TPU:0, one launch (start us, length us, event | category | flops | bytes accessed | tf_op | source)
XLA Modules:
  0.0 331.0 jit_solution(18315121277196372518)
XLA Ops:
  2.8 2.2 collective-permute-done.1.refs_3_
  6.6 8.4 %all-to-all-start = ((bf16[16,520,128]{2,1,0:T(8,128)(2,1)}), bf16[16,520,128]{2,1,0:T(8,128)(2,1)}, u32[]{:S(2)}, u32[]{:S(2)}) async-start(bf16[16,520,128]{2,1,0:T(8,128)(2,1)} %gather_stripes.2), calls=%async_computation | async-start | bytes 4259840 | tf_op jit(solution)/shard_map/all_to_all | solution.py:127
  32.2 3.7 %add_convert_fusion.value_weight_ref = bf16[1024,1024]{1,0:T(8,128)(2,1)} fusion(bf16[1024,4]{0,1:T(4,128)(2,1)} %copy-done.16, bf16[1024,3072]{1,0:T(8,128)(2,1)} %key_weight_ref.3, f32[2,4,1024]{2,1,0:T(4,128)} %param.40), kind=kOutput, calls=%fused_computation | convolution fusion | flops 12582912 | bytes 4210688 | tf_op jit(solution)/shard_map/dot_general | solution.py:33
  36.0 3.7 %add_convert_fusion.1.weight_ref.query_weight_ref = bf16[1024,1024]{1,0:T(8,128)(2,1)} fusion(bf16[1024,4]{0,1:T(4,128)(2,1)S(1)} %copy-done.15, bf16[1024,3072]{1,0:T(8,128)(2,1)} %key_weight_ref.3, f32[2,4,1024]{2,1,0:T(4,128)S(1)} %copy-done.5), kind=kOutput, calls=%fused_computation.1 | convolution fusion | flops 12582912 | bytes 4210688 | tf_op jit(solution)/shard_map/dot_general | solution.py:33
  41.5 17.4 %all-to-all-done.x_ref = bf16[16,520,128]{2,1,0:T(8,128)(2,1)} async-done(((bf16[16,520,128]{2,1,0:T(8,128)(2,1)}), bf16[16,520,128]{2,1,0:T(8,128)(2,1)}, u32[]{:S(2)}, u32[]{:S(2)}) %all-to-all-start) | async-done | bytes 2129952 | tf_op jit(solution)/shard_map/all_to_all | solution.py:127
  58.9 10.8 %all-to-all-start.1 = ((bf16[16,512,128]{2,1,0:T(8,128)(2,1)}), bf16[16,512,128]{2,1,0:T(8,128)(2,1)}, u32[]{:S(2)}, u32[]{:S(2)}) async-start(bf16[16,512,128]{2,1,0:T(8,128)(2,1)} %copy-done), calls=%async_computation.1 | async-start | bytes 4194304 | tf_op jit(solution)/shard_map/all_to_all | solution.py:127
  70.3 9.7 %enter.1 = (bf16[1024,1024]{1,0:T(8,128)(2,1)}, bf16[1024,1024]{1,0:T(8,128)(2,1)}, bf16[1024,1024]{1,0:T(8,128)(2,1)}) custom-call(bf16[16,520,128]{2,1,0:T(8,128)(2,1)} %all-to-all-done.x_ref, f32[1,1024]{1,0:T(1,128)} %bitcast.37, f32[1,1024]{1,0:T(1,128)} %bitcast.46, f32[1,1024]{1,0:T(1,128)} %get-tuple-element.118.bias_ref, ...), custom_call_target="tpu_custom_call" | custom-call | flops 4294967296 | bytes 16822272 | tf_op jit(solution)/shard_map/enter/pallas_call | solution.py:581
  81.6 6.0 %ask.1.refs_0_ = bf16[1024,1024]{1,0:T(8,128)(2,1)} custom-call(bf16[1024,1024]{1,0:T(8,128)(2,1)} %get-tuple-element.88.normed_ref, f32[1,1024]{1,0:T(1,128)} %get-tuple-element.117.bias_ref, bf16[1024,1024]{1,0:T(8,128)(2,1)} %add_convert_fusion.1.weight_ref.query_weight_ref), custom_call_target="tpu_custom_call" | custom-call | flops 2147483648 | bytes 6295552 | tf_op jit(solution)/shard_map/ask/pallas_call | solution.py:581
  88.7 28.1 %attend.1 = (bf16[1024,1024]{1,0:T(8,128)(2,1)}, f32[64,1024]{1,0:T(8,128)}) custom-call(bf16[1024,1024]{1,0:T(8,128)(2,1)} %ask.1.refs_0_, bf16[1024,1024]{1,0:T(8,128)(2,1)} %get-tuple-element.61.refs_1_.refs_4_, bf16[1024,1024]{1,0:T(8,128)(2,1)} %collective-permute-done.3.refs_2_.refs_5_, bf16[1024,1024]{1,0:T(8,128)(2,1)} %get-tuple-element.62.refs_3_.refs_6_, ...), custom_call_target="tpu_custom_call" | custom-call | flops 4831838208 | bytes 12582912 | tf_op jit(solution)/shard_map/attend/pallas_call | solution.py:784
  116.9 64.8 %middle.1 = (bf16[1024,1024]{1,0:T(8,128)(2,1)}, bf16[1024,1024]{1,0:T(8,128)(2,1)}, bf16[1024,1024]{1,0:T(8,128)(2,1)}) custom-call(bf16[16,520,128]{2,1,0:T(8,128)(2,1)} %all-to-all-done.x_ref, bf16[1024,1024]{1,0:T(8,128)(2,1)} %get-tuple-element.64.attended_ref.refs_2_, bf16[16,512,128]{2,1,0:T(8,128)(2,1)} %all-to-all-done.1.cotangent_ref, ...), custom_call_target="tpu_custom_call" | custom-call | flops 38654705664 | bytes 31522816 | tf_op jit(solution)/shard_map/middle/pallas_call | solution.py:581
  181.6 7.1 %all-to-all-start.2 = ((bf16[16,64,1024]{2,1,0:T(8,128)(2,1)}), bf16[16,64,1024]{2,1,0:T(8,128)(2,1)}, u32[]{:S(2)}, u32[]{:S(2)}) async-start(bf16[16,64,1024]{2,1,0:T(8,128)(2,1)} %bitcast.35), calls=%async_computation.2 | async-start | bytes 4194304 | tf_op jit(solution)/shard_map/all_to_all | solution.py:133
  188.7 50.4 %pull.1 = (bf16[1024,1024]{1,0:T(8,128)(2,1)}, bf16[1024,1024]{1,0:T(8,128)(2,1)}, bf16[1024,1024]{1,0:T(8,128)(2,1)}, bf16[1024,1024]{1,0:T(8,128)(2,1)}, bf16[1024,1024]{1,0:T(8,128)(2,1)}) custom-call(bf16[1024,1024]{1,0:T(8,128)(2,1)} %ask.1.refs_0_, bf16[1024,1024]{1,0:T(8,128)(2,1)} %get-tuple-element.72.refs_1_, ...), custom_call_target="tpu_custom_call" | custom-call | flops 12079595520 | bytes 25165824 | tf_op jit(solution)/shard_map/pull/pallas_call | solution.py:802
  239.7 4.0 %collective-permute-done.6.refs_1_ = bf16[1024,1024]{1,0:T(8,128)(2,1)} collective-permute-done((bf16[1024,1024]{1,0:T(8,128)(2,1)}, bf16[1024,1024]{1,0:T(8,128)(2,1)}, u32[]{:S(2)}, u32[]{:S(2)}) %collective-permute-start.6) | collective-permute-done | bytes 2097184 | tf_op jit(solution)/shard_map/ppermute | solution.py:146
  243.7 3.0 collective-permute-done.7.refs_3_.refs_1_
  246.7 14.4 %leave.1 = bf16[1024,1024]{1,0:T(8,128)(2,1)} custom-call(bf16[16,520,128]{2,1,0:T(8,128)(2,1)} %all-to-all-done.x_ref, f32[1,1024]{1,0:T(1,128)} %bitcast.38, bf16[1024,1024]{1,0:T(8,128)(2,1)} %add_convert_fusion.1.weight_ref.query_weight_ref, bf16[1024,3072]{1,0:T(8,128)(2,1)} %key_weight_ref.3, bf16[1024,1024]{1,0:T(8,128)(2,1)} %add_convert_fusion.value_weight_ref, ...), custom_call_target="tpu_custom_call" | custom-call | flops 6442450944 | bytes 27299840 | tf_op jit(solution)/shard_map/leave/pallas_call | solution.py:581
  261.0 6.9 %all-to-all-start.3 = ((bf16[16,64,1024]{2,1,0:T(8,128)(2,1)}), bf16[16,64,1024]{2,1,0:T(8,128)(2,1)}, u32[]{:S(2)}, u32[]{:S(2)}) async-start(bf16[16,64,1024]{2,1,0:T(8,128)(2,1)} %bitcast.34), calls=%async_computation.3 | async-start | bytes 4194304 | tf_op jit(solution)/shard_map/all_to_all | solution.py:133
  269.4 2.6 collective-permute-done.5.refs_1_
  272.0 2.6 spread_stripes.2
  274.6 8.1 %adapt.1 = (f32[8,1024]{1,0:T(8,128)}, f32[8,2048]{1,0:T(8,128)}) custom-call(bf16[1024,128]{1,0:T(8,128)(2,1)} %pad.13.down_ref, bf16[128,2048]{1,0:T(8,128)(2,1)} %fusion.1.up_ref, bf16[1024,1024]{1,0:T(8,128)(2,1)} %get-tuple-element.88.normed_ref, bf16[1024,1024]{1,0:T(8,128)(2,1)} %get-tuple-element.83.grad_query_ref, ...), custom_call_target="tpu_custom_call" | custom-call | flops 1073741824 | bytes 9273344 | tf_op jit(solution)/shard_map/adapt/pallas_call | solution.py:581
  291.2 7.0 %collective-permute-done.11 = f32[4,1024]{1,0:T(4,128)S(1)} collective-permute-done((f32[4,1024]{1,0:T(4,128)S(1)}, f32[4,1024]{1,0:T(4,128)S(1)}, u32[]{:S(2)}, u32[]{:S(2)}) %collective-permute-start.11) | collective-permute-done | bytes 16416 | tf_op jit(solution)/shard_map/ppermute | solution.py:160
  300.1 4.3 %collective-permute-start.14 = (f32[4,1024]{1,0:T(4,128)S(1)}, f32[4,1024]{1,0:T(4,128)S(1)}, u32[]{:S(2)}, u32[]{:S(2)}) collective-permute-start(f32[4,1024]{1,0:T(4,128)S(1)} %add_add_fusion.1), channel_id=1, source_target_pairs={{0,24},{2,26},{4,28},{6,30},{8,16},{10,18},{12,20},{14,22},{16,8},... | collective-permute-start | bytes 49160 | tf_op jit(solution)/shard_map/ppermute | solution.py:160
  304.4 13.2 %collective-permute-done.13 = f32[4,1024]{1,0:T(4,128)S(1)} collective-permute-done((f32[4,1024]{1,0:T(4,128)S(1)}, f32[4,1024]{1,0:T(4,128)S(1)}, u32[]{:S(2)}, u32[]{:S(2)}) %collective-permute-start.13) | collective-permute-done | bytes 16416 | tf_op jit(solution)/shard_map/ppermute | solution.py:160
  323.1 2.3 collective-permute-done.18
  328.2 2.6 spread_stripes.3
  (127 shorter events, 46.4 us)
Async XLA Ops:
  2.2 2.8 collective-permute-start
  2.7 2.3 collective-permute-start.1
  6.6 52.3 %all-to-all-start = ((bf16[16,520,128]{2,1,0:T(8,128)(2,1)}), bf16[16,520,128]{2,1,0:T(8,128)(2,1)}, u32[]{:S(2)}, u32[]{:S(2)}) async-start(bf16[16,520,128]{2,1,0:T(8,128)(2,1)} %gather_stripes.2), calls=%async_computation | async-start | bytes 4259840 | tf_op jit(solution)/shard_map/all_to_all | solution.py:127
  18.3 21.4 %collective-permute-start.2 = (bf16[8,64,1024]{2,1,0:T(8,128)(2,1)}, bf16[8,64,1024]{2,1,0:T(8,128)(2,1)S(1)}, u32[]{:S(2)}, u32[]{:S(2)}) collective-permute-start(bf16[8,64,1024]{2,1,0:T(8,128)(2,1)} %constant_dynamic-slice_fusion.11), channel_id=1, source_target_pairs={{0,1},{1,0},{2,3},{3,2},{4,5},{5,4},{6,7},{7,6},{8,9},{9,8},{10,11... | collective-permute-start | bytes 3145736 | tf_op jit(solution)/shard_map/ppermute | solution.py:146
  58.9 57.9 %all-to-all-start.1 = ((bf16[16,512,128]{2,1,0:T(8,128)(2,1)}), bf16[16,512,128]{2,1,0:T(8,128)(2,1)}, u32[]{:S(2)}, u32[]{:S(2)}) async-start(bf16[16,512,128]{2,1,0:T(8,128)(2,1)} %copy-done), calls=%async_computation.1 | async-start | bytes 4194304 | tf_op jit(solution)/shard_map/all_to_all | solution.py:127
  80.0 8.7 %collective-permute-start.3 = (bf16[1024,1024]{1,0:T(8,128)(2,1)}, bf16[1024,1024]{1,0:T(8,128)(2,1)}, u32[]{:S(2)}, u32[]{:S(2)}) collective-permute-start(bf16[1024,1024]{1,0:T(8,128)(2,1)} %get-tuple-element.61.refs_1_.refs_4_), channel_id=1, source_target_pairs={{0,1},{1,0},{2,3},{3,2},{4,5},{5,4},{6,7},{7,6},{8,9},{9,8},{10,11... | collective-permute-start | bytes 6291464 | tf_op jit(solution)/shard_map/ppermute | solution.py:146
  80.0 8.7 %collective-permute-start.4 = (bf16[1024,1024]{1,0:T(8,128)(2,1)}, bf16[1024,1024]{1,0:T(8,128)(2,1)}, u32[]{:S(2)}, u32[]{:S(2)}) collective-permute-start(bf16[1024,1024]{1,0:T(8,128)(2,1)} %get-tuple-element.62.refs_3_.refs_6_), channel_id=1, source_target_pairs={{0,1},{1,0},{2,3},{3,2},{4,5},{5,4},{6,7},{7,6},{8,9},{9,8},{10,11... | collective-permute-start | bytes 6291464 | tf_op jit(solution)/shard_map/ppermute | solution.py:146
  181.6 57.4 %all-to-all-start.2 = ((bf16[16,64,1024]{2,1,0:T(8,128)(2,1)}), bf16[16,64,1024]{2,1,0:T(8,128)(2,1)}, u32[]{:S(2)}, u32[]{:S(2)}) async-start(bf16[16,64,1024]{2,1,0:T(8,128)(2,1)} %bitcast.35), calls=%async_computation.2 | async-start | bytes 4194304 | tf_op jit(solution)/shard_map/all_to_all | solution.py:133
  239.1 4.6 %collective-permute-start.6 = (bf16[1024,1024]{1,0:T(8,128)(2,1)}, bf16[1024,1024]{1,0:T(8,128)(2,1)}, u32[]{:S(2)}, u32[]{:S(2)}) collective-permute-start(bf16[1024,1024]{1,0:T(8,128)(2,1)} %get-tuple-element.85), channel_id=1, source_target_pairs={{0,1},{1,0},{2,3},{3,2},{4,5},{5,4},{6,7},{7,6},{8,9},{9,8},{10,11... | collective-permute-start | bytes 6291464 | tf_op jit(solution)/shard_map/ppermute | solution.py:146
  239.2 7.5 %collective-permute-start.7 = (bf16[1024,1024]{1,0:T(8,128)(2,1)}, bf16[1024,1024]{1,0:T(8,128)(2,1)}, u32[]{:S(2)}, u32[]{:S(2)}) collective-permute-start(bf16[1024,1024]{1,0:T(8,128)(2,1)} %get-tuple-element.87), channel_id=1, source_target_pairs={{0,1},{1,0},{2,3},{3,2},{4,5},{5,4},{6,7},{7,6},{8,9},{9,8},{10,11... | collective-permute-start | bytes 6291464 | tf_op jit(solution)/shard_map/ppermute | solution.py:146
  261.0 56.6 %all-to-all-start.3 = ((bf16[16,64,1024]{2,1,0:T(8,128)(2,1)}), bf16[16,64,1024]{2,1,0:T(8,128)(2,1)}, u32[]{:S(2)}, u32[]{:S(2)}) async-start(bf16[16,64,1024]{2,1,0:T(8,128)(2,1)} %bitcast.34), calls=%async_computation.3 | async-start | bytes 4194304 | tf_op jit(solution)/shard_map/all_to_all | solution.py:133
  269.3 2.7 collective-permute-start.5
  282.7 44.8 %copy-start.11 = (f32[2,1024,4]{1,2,0:T(4,128)S(1)}, f32[2,1024,4]{1,2,0:T(4,128)}, u32[]{:S(2)}) copy-start(f32[2,1024,4]{1,2,0:T(4,128)} %param.43) | copy-start | bytes 98308
  284.3 1.3 collective-permute-start.8
  286.5 4.7 %collective-permute-start.10 = (f32[4,1024]{1,0:T(4,128)S(1)}, f32[4,1024]{1,0:T(4,128)S(1)}, u32[]{:S(2)}, u32[]{:S(2)}) collective-permute-start(f32[4,1024]{1,0:T(4,128)S(1)} %get-tuple-element.108), channel_id=1, source_target_pairs={{0,4},{2,6},{4,0},{6,2},{8,12},{10,14},{12,8},{14,10},{16,20},{18,... | collective-permute-start | bytes 49160 | tf_op jit(solution)/shard_map/ppermute | solution.py:160
  288.4 9.7 %collective-permute-start.11 = (f32[4,1024]{1,0:T(4,128)S(1)}, f32[4,1024]{1,0:T(4,128)S(1)}, u32[]{:S(2)}, u32[]{:S(2)}) collective-permute-start(f32[4,1024]{1,0:T(4,128)S(1)} %get-tuple-element.107), channel_id=1, source_target_pairs={{0,6},{2,4},{4,2},{6,0},{8,14},{10,12},{12,10},{14,8},{16,22},{18,... | collective-permute-start | bytes 49160 | tf_op jit(solution)/shard_map/ppermute | solution.py:160
  289.9 10.1 %collective-permute-start.9 = (f32[4,1024]{1,0:T(4,128)S(1)}, f32[4,1024]{1,0:T(4,128)S(1)}, u32[]{:S(2)}, u32[]{:S(2)}) collective-permute-start(f32[4,1024]{1,0:T(4,128)S(1)} %get-tuple-element.106), channel_id=1, source_target_pairs={{0,2},{2,0},{4,6},{6,4},{8,10},{10,8},{12,14},{14,12},{16,18},{18,... | collective-permute-start | bytes 49160 | tf_op jit(solution)/shard_map/ppermute | solution.py:160
  300.0 4.5 %collective-permute-start.12 = (f32[4,1024]{1,0:T(4,128)S(1)}, f32[4,1024]{1,0:T(4,128)S(1)}, u32[]{:S(2)}, u32[]{:S(2)}) collective-permute-start(f32[4,1024]{1,0:T(4,128)S(1)} %add_add_fusion.1), channel_id=1, source_target_pairs={{0,8},{2,10},{4,12},{6,14},{8,0},{10,2},{12,4},{14,6},{16,24},{18,... | collective-permute-start | bytes 49160 | tf_op jit(solution)/shard_map/ppermute | solution.py:160
  300.0 17.5 %collective-permute-start.13 = (f32[4,1024]{1,0:T(4,128)S(1)}, f32[4,1024]{1,0:T(4,128)S(1)}, u32[]{:S(2)}, u32[]{:S(2)}) collective-permute-start(f32[4,1024]{1,0:T(4,128)S(1)} %add_add_fusion.1), channel_id=1, source_target_pairs={{0,16},{2,18},{4,20},{6,22},{8,24},{10,26},{12,28},{14,30},{16,0},... | collective-permute-start | bytes 49160 | tf_op jit(solution)/shard_map/ppermute | solution.py:160
  300.1 17.5 %collective-permute-start.14 = (f32[4,1024]{1,0:T(4,128)S(1)}, f32[4,1024]{1,0:T(4,128)S(1)}, u32[]{:S(2)}, u32[]{:S(2)}) collective-permute-start(f32[4,1024]{1,0:T(4,128)S(1)} %add_add_fusion.1), channel_id=1, source_target_pairs={{0,24},{2,26},{4,28},{6,30},{8,16},{10,18},{12,20},{14,22},{16,8},... | collective-permute-start | bytes 49160 | tf_op jit(solution)/shard_map/ppermute | solution.py:160
  317.6 5.5 %collective-permute-start.16 = (f32[4,1024]{1,0:T(4,128)S(1)}, f32[4,1024]{1,0:T(4,128)S(1)}, u32[]{:S(2)}, u32[]{:S(2)}) collective-permute-start(f32[4,1024]{1,0:T(4,128)S(1)} %add_add_fusion), channel_id=1, source_target_pairs={{0,2},{2,0},{4,6},{6,4},{8,10},{10,8},{12,14},{14,12},{16,18},{18,... | collective-permute-start | bytes 49160 | tf_op jit(solution)/shard_map/ppermute | solution.py:160
  319.2 3.9 %collective-permute-start.17 = (f32[4,1024]{1,0:T(4,128)S(1)}, f32[4,1024]{1,0:T(4,128)S(1)}, u32[]{:S(2)}, u32[]{:S(2)}) collective-permute-start(f32[4,1024]{1,0:T(4,128)S(1)} %add_add_fusion), channel_id=1, source_target_pairs={{0,4},{2,6},{4,0},{6,2},{8,12},{10,14},{12,8},{14,10},{16,20},{18,... | collective-permute-start | bytes 49160 | tf_op jit(solution)/shard_map/ppermute | solution.py:160
  320.8 4.6 %collective-permute-start.18 = (f32[4,1024]{1,0:T(4,128)S(1)}, f32[4,1024]{1,0:T(4,128)S(1)}, u32[]{:S(2)}, u32[]{:S(2)}) collective-permute-start(f32[4,1024]{1,0:T(4,128)S(1)} %add_add_fusion), channel_id=1, source_target_pairs={{0,6},{2,4},{4,2},{6,0},{8,14},{10,12},{12,10},{14,8},{16,22},{18,... | collective-permute-start | bytes 49160 | tf_op jit(solution)/shard_map/ppermute | solution.py:160
  323.0 5.2 %collective-permute-start.15 = (bf16[8,64,1024]{2,1,0:T(8,128)(2,1)S(1)}, bf16[8,64,1024]{2,1,0:T(8,128)(2,1)S(1)}, u32[]{:S(2)}, u32[]{:S(2)}) collective-permute-start(bf16[8,64,1024]{2,1,0:T(8,128)(2,1)S(1)} %constant_dynamic-slice_fusion.4), channel_id=1, source_target_pairs={{0,1},{1,0},{2,3},{3,2},{4,5},{5,4},{6,7},{7,6},{8,9},{9,8},{10,11... | collective-permute-start | bytes 3145736 | tf_op jit(solution)/shard_map/ppermute | solution.py:146
  (19 other events, 228.9 us)

commit v3 on v2

--- a/solution.py
+++ b/solution.py
@@ -532,15 +532,19 @@
     up_sum_ref[:, width:] += matmul_over(lora, grad_value)[:slots]
 
 
+def return_kernel(grad_query_ref, query_weight_ref, grad_normed_ref):
+    grad_normed_ref[...] = matmul_back(grad_query_ref[...], query_weight_ref[...])
+
+
 def leave_kernel(
-    stripe, cores, x_ref, gain_ref, query_weight_ref, key_weight_ref, value_weight_ref,
-    grad_middle_ref, grad_query_ref, *refs,
+    stripe, cores, x_ref, gain_ref, key_weight_ref, value_weight_ref,
+    grad_middle_ref, from_queries_ref, *refs,
 ):
     key_refs, value_refs, grad_ref = refs[:cores], refs[cores : 2 * cores], refs[-1]
-    width = grad_query_ref.shape[1]
+    width = grad_middle_ref.shape[1]
     shaped, spread_inverse = standardized(tokens_of(x_ref, stripe, width).astype(jnp.float32))
     grad_normed = (
-        matmul_back(grad_query_ref[...], query_weight_ref[...])
+        from_queries_ref[...]
         + matmul_back(total(key_refs), key_weight_ref[...])
         + matmul_back(total(value_refs), value_weight_ref[...])
     )
@@ -821,16 +825,25 @@
     ]
     owned_values = owned(pulled[1 + cores :])
     owned_keys = owned(pulled[1 : 1 + cores])
+    (from_queries,) = over_tokens(
+        return_kernel,
+        "return",
+        tokens,
+        [tile(pulled[0]), whole(query_weight)],
+        [jax.ShapeDtypeStruct((tokens, width), jnp.float32)],
+        [],
+        2 * tokens * width * width,
+    )
     (input_grad,) = over_tokens(
         functools.partial(leave_kernel, stripe, cores),
         "leave",
         tokens,
-        [tile(x), whole(first_gain), whole(query_weight)]
+        [tile(x), whole(first_gain)]
         + [columns(query_key_value_weight, 1, width), whole(value_weight)]
-        + [tile(part) for part in (grad_middle, pulled[0], *owned_keys, *owned_values)],
+        + [tile(part) for part in (grad_middle, from_queries, *owned_keys, *owned_values)],
         [low],
         [],
-        6 * tokens * width * width,
+        4 * tokens * width * width,
     )
     input_grad, normed = lax.optimization_barrier((input_grad, normed))
     down_sum, up_sum = over_tokens(

time: 329 us -> 328 us (level)
  waiting for transfers between devices: 55.8 us -> 49.2 us
  Pallas kernels: 189 us -> 194 us
    ppermute x9, waiting for transfers between devices: 11.8 us -> 5.22 us  [from_core(): lax.ppermute(x, 'batch', [(i, (i + by) % cores) for i in range(cores)])]
    pallas_call x5 -> x6, Pallas kernels: 103 us -> 108 us  [over_tokens(): pl.pallas_call(kernel, grid=(tokens // min(TOKEN_BLOCK, tokens),), in_spe...]
  transfers between devices with their start and end apart: 23 -> 23, of which waited for: 11 -> 10; matrix products, arithmetic and copies ran while one was open for 11% -> 11% of each run, Pallas kernels for 32% -> 34%
where the time goes in v3:
time: 328 us; the launch traced here: 329 us
  Pallas kernels  194 us (59%)
  waiting for transfers between devices  49.2 us (15%)
  starting transfers between devices  47.2 us (14%)
  other arithmetic  20.5 us (6%)
  local copies, waits for them, and re-layouts  9.92 us (3%)
  matrix products  7.44 us (2%)
    pallas_call x6, Pallas kernels, over_tokens(): pl.pallas_call(kernel, grid=(tokens // min(TOKEN_BLOCK, tokens),), in_spe...  108 us
    pallas_call x1, Pallas kernels, body(): pull(queries, grad_attended, attended, log_total, *all_keys, *all_values,...  50.4 us
    pallas_call x1, Pallas kernels, body(): attended, log_total = attend(queries, *all_keys, *all_values, marks, causal)  28.1 us
    ppermute x10, waiting for transfers between devices, exchanged(): return lax.ppermute(x, axis, [(i, i ^ by) for i in range(size)])  26.6 us
    all_to_all x2, starting transfers between devices, rows_home(): return lax.all_to_all(y, 'seq', 0, 0, tiled=True)  19.2 us
    all_to_all x2, waiting for transfers between devices, rows_home(): return lax.all_to_all(y, 'seq', 0, 0, tiled=True)  17.4 us
    all_to_all x2, starting transfers between devices, rows_back(): return lax.all_to_all(y, 'seq', 0, 0, tiled=True)  14 us
    ppermute x10, starting transfers between devices, exchanged(): return lax.ppermute(x, axis, [(i, i ^ by) for i in range(size)])  12.2 us
  transfers between devices with their start and end apart: 23, of which 10 were waited for; matrix products, arithmetic and copies ran while one was open for 11% of the time, Pallas kernels for 34%

profile of v3, /device:TPU:0, one launch (start us, length us, event | category | flops | bytes accessed | tf_op | source)
XLA Modules:
  0.0 329.2 jit_solution(17542257578970573828)
XLA Ops:
  2.8 2.2 collective-permute-done.1.refs_3_
  6.6 8.4 %all-to-all-start = ((bf16[16,520,128]{2,1,0:T(8,128)(2,1)}), bf16[16,520,128]{2,1,0:T(8,128)(2,1)}, u32[]{:S(2)}, u32[]{:S(2)}) async-start(bf16[16,520,128]{2,1,0:T(8,128)(2,1)} %gather_stripes.2), calls=%async_computation | async-start | bytes 4259840 | tf_op jit(solution)/shard_map/all_to_all | solution.py:127
  15.2 2.0 multiply_convert_fusion.refs_0_
  32.2 3.7 %add_convert_fusion.value_weight_ref = bf16[1024,1024]{1,0:T(8,128)(2,1)} fusion(bf16[1024,4]{0,1:T(4,128)(2,1)} %copy-done.16, bf16[1024,3072]{1,0:T(8,128)(2,1)} %key_weight_ref.3, f32[2,4,1024]{2,1,0:T(4,128)} %param.40), kind=kOutput, calls=%fused_computation | convolution fusion | flops 12582912 | bytes 4210688 | tf_op jit(solution)/shard_map/dot_general | solution.py:33
  35.9 3.7 %add_convert_fusion.1.weight_ref.query_weight_ref = bf16[1024,1024]{1,0:T(8,128)(2,1)} fusion(bf16[1024,4]{0,1:T(4,128)(2,1)S(1)} %copy-done.15, bf16[1024,3072]{1,0:T(8,128)(2,1)} %key_weight_ref.3, f32[2,4,1024]{2,1,0:T(4,128)S(1)} %copy-done.5), kind=kOutput, calls=%fused_computation.1 | convolution fusion | flops 12582912 | bytes 4210688 | tf_op jit(solution)/shard_map/dot_general | solution.py:33
  41.6 17.4 %all-to-all-done.x_ref = bf16[16,520,128]{2,1,0:T(8,128)(2,1)} async-done(((bf16[16,520,128]{2,1,0:T(8,128)(2,1)}), bf16[16,520,128]{2,1,0:T(8,128)(2,1)}, u32[]{:S(2)}, u32[]{:S(2)}) %all-to-all-start) | async-done | bytes 2129952 | tf_op jit(solution)/shard_map/all_to_all | solution.py:127
  58.9 10.8 %all-to-all-start.1 = ((bf16[16,512,128]{2,1,0:T(8,128)(2,1)}), bf16[16,512,128]{2,1,0:T(8,128)(2,1)}, u32[]{:S(2)}, u32[]{:S(2)}) async-start(bf16[16,512,128]{2,1,0:T(8,128)(2,1)} %copy-done), calls=%async_computation.1 | async-start | bytes 4194304 | tf_op jit(solution)/shard_map/all_to_all | solution.py:127
  70.3 9.8 %enter.1 = (bf16[1024,1024]{1,0:T(8,128)(2,1)}, bf16[1024,1024]{1,0:T(8,128)(2,1)}, bf16[1024,1024]{1,0:T(8,128)(2,1)}) custom-call(bf16[16,520,128]{2,1,0:T(8,128)(2,1)} %all-to-all-done.x_ref, f32[1,1024]{1,0:T(1,128)} %bitcast.37, f32[1,1024]{1,0:T(1,128)} %bitcast.46, f32[1,1024]{1,0:T(1,128)} %get-tuple-element.118.bias_ref, ...), custom_call_target="tpu_custom_call" | custom-call | flops 4294967296 | bytes 16822272 | tf_op jit(solution)/shard_map/enter/pallas_call | solution.py:585
  81.6 6.0 %ask.1.refs_0_ = bf16[1024,1024]{1,0:T(8,128)(2,1)} custom-call(bf16[1024,1024]{1,0:T(8,128)(2,1)} %get-tuple-element.88.normed_ref, f32[1,1024]{1,0:T(1,128)} %get-tuple-element.117.bias_ref, bf16[1024,1024]{1,0:T(8,128)(2,1)} %add_convert_fusion.1.weight_ref.query_weight_ref), custom_call_target="tpu_custom_call" | custom-call | flops 2147483648 | bytes 6295552 | tf_op jit(solution)/shard_map/ask/pallas_call | solution.py:585
  88.8 28.1 %attend.1 = (bf16[1024,1024]{1,0:T(8,128)(2,1)}, f32[64,1024]{1,0:T(8,128)}) custom-call(bf16[1024,1024]{1,0:T(8,128)(2,1)} %ask.1.refs_0_, bf16[1024,1024]{1,0:T(8,128)(2,1)} %get-tuple-element.61.refs_1_.refs_4_, bf16[1024,1024]{1,0:T(8,128)(2,1)} %collective-permute-done.3.refs_2_.refs_5_, bf16[1024,1024]{1,0:T(8,128)(2,1)} %get-tuple-element.62.refs_3_.refs_6_, ...), custom_call_target="tpu_custom_call" | custom-call | flops 4831838208 | bytes 12582912 | tf_op jit(solution)/shard_map/attend/pallas_call | solution.py:788
  116.9 64.8 %middle.1 = (bf16[1024,1024]{1,0:T(8,128)(2,1)}, bf16[1024,1024]{1,0:T(8,128)(2,1)}, bf16[1024,1024]{1,0:T(8,128)(2,1)}) custom-call(bf16[16,520,128]{2,1,0:T(8,128)(2,1)} %all-to-all-done.x_ref, bf16[1024,1024]{1,0:T(8,128)(2,1)} %get-tuple-element.64.attended_ref.refs_2_, bf16[16,512,128]{2,1,0:T(8,128)(2,1)} %all-to-all-done.1.cotangent_ref, ...), custom_call_target="tpu_custom_call" | custom-call | flops 38654705664 | bytes 31522816 | tf_op jit(solution)/shard_map/middle/pallas_call | solution.py:585
  181.8 7.0 %all-to-all-start.2 = ((bf16[16,64,1024]{2,1,0:T(8,128)(2,1)}), bf16[16,64,1024]{2,1,0:T(8,128)(2,1)}, u32[]{:S(2)}, u32[]{:S(2)}) async-start(bf16[16,64,1024]{2,1,0:T(8,128)(2,1)} %bitcast.35), calls=%async_computation.2 | async-start | bytes 4194304 | tf_op jit(solution)/shard_map/all_to_all | solution.py:133
  188.8 50.4 %pull.1 = (bf16[1024,1024]{1,0:T(8,128)(2,1)}, bf16[1024,1024]{1,0:T(8,128)(2,1)}, bf16[1024,1024]{1,0:T(8,128)(2,1)}, bf16[1024,1024]{1,0:T(8,128)(2,1)}, bf16[1024,1024]{1,0:T(8,128)(2,1)}) custom-call(bf16[1024,1024]{1,0:T(8,128)(2,1)} %ask.1.refs_0_, bf16[1024,1024]{1,0:T(8,128)(2,1)} %get-tuple-element.72.refs_1_, ...), custom_call_target="tpu_custom_call" | custom-call | flops 12079595520 | bytes 25165824 | tf_op jit(solution)/shard_map/pull/pallas_call | solution.py:806
  239.8 6.6 %return.1.from_queries_ref = f32[1024,1024]{1,0:T(8,128)} custom-call(bf16[1024,1024]{1,0:T(8,128)(2,1)} %get-tuple-element.83.grad_query_ref, bf16[1024,1024]{1,0:T(8,128)(2,1)} %add_convert_fusion.1.weight_ref.query_weight_ref), custom_call_target="tpu_custom_call" | custom-call | flops 2147483648 | bytes 8388608 | tf_op jit(solution)/shard_map/return/pallas_call | solution.py:585
  246.8 12.5 %leave.1 = bf16[1024,1024]{1,0:T(8,128)(2,1)} custom-call(bf16[16,520,128]{2,1,0:T(8,128)(2,1)} %all-to-all-done.x_ref, f32[1,1024]{1,0:T(1,128)} %bitcast.38, bf16[1024,3072]{1,0:T(8,128)(2,1)} %key_weight_ref.3, bf16[1024,1024]{1,0:T(8,128)(2,1)} %add_convert_fusion.value_weight_ref, bf16[1024,1024]{1,0:T(8,128)(2,1)} %get-tuple-element.82.grad_middle_ref, ...), custom_call_target="tpu_custom_call" | custom-call | flops 4294967296 | bytes 27299840 | tf_op jit(solution)/shard_map/leave/pallas_call | solution.py:585
  259.2 6.9 %all-to-all-start.3 = ((bf16[16,64,1024]{2,1,0:T(8,128)(2,1)}), bf16[16,64,1024]{2,1,0:T(8,128)(2,1)}, u32[]{:S(2)}, u32[]{:S(2)}) async-start(bf16[16,64,1024]{2,1,0:T(8,128)(2,1)} %bitcast.34), calls=%async_computation.3 | async-start | bytes 4194304 | tf_op jit(solution)/shard_map/all_to_all | solution.py:133
  267.6 2.6 collective-permute-done.5.refs_1_
  270.2 2.6 spread_stripes.2
  272.8 8.1 %adapt.1 = (f32[8,1024]{1,0:T(8,128)}, f32[8,2048]{1,0:T(8,128)}) custom-call(bf16[1024,128]{1,0:T(8,128)(2,1)} %pad.13.down_ref, bf16[128,2048]{1,0:T(8,128)(2,1)} %fusion.1.up_ref, bf16[1024,1024]{1,0:T(8,128)(2,1)} %get-tuple-element.88.normed_ref, bf16[1024,1024]{1,0:T(8,128)(2,1)} %get-tuple-element.83.grad_query_ref, ...), custom_call_target="tpu_custom_call" | custom-call | flops 1073741824 | bytes 9273344 | tf_op jit(solution)/shard_map/adapt/pallas_call | solution.py:585
  289.4 7.0 %collective-permute-done.11 = f32[4,1024]{1,0:T(4,128)S(1)} collective-permute-done((f32[4,1024]{1,0:T(4,128)S(1)}, f32[4,1024]{1,0:T(4,128)S(1)}, u32[]{:S(2)}, u32[]{:S(2)}) %collective-permute-start.11) | collective-permute-done | bytes 16416 | tf_op jit(solution)/shard_map/ppermute | solution.py:160
  298.4 4.3 %collective-permute-start.14 = (f32[4,1024]{1,0:T(4,128)S(1)}, f32[4,1024]{1,0:T(4,128)S(1)}, u32[]{:S(2)}, u32[]{:S(2)}) collective-permute-start(f32[4,1024]{1,0:T(4,128)S(1)} %add_add_fusion.1), channel_id=1, source_target_pairs={{0,24},{2,26},{4,28},{6,30},{8,16},{10,18},{12,20},{14,22},{16,8},... | collective-permute-start | bytes 49160 | tf_op jit(solution)/shard_map/ppermute | solution.py:160
  302.7 13.2 %collective-permute-done.13 = f32[4,1024]{1,0:T(4,128)S(1)} collective-permute-done((f32[4,1024]{1,0:T(4,128)S(1)}, f32[4,1024]{1,0:T(4,128)S(1)}, u32[]{:S(2)}, u32[]{:S(2)}) %collective-permute-start.13) | collective-permute-done | bytes 16416 | tf_op jit(solution)/shard_map/ppermute | solution.py:160
  321.3 2.3 collective-permute-done.18
  326.4 2.6 spread_stripes.3
  (128 shorter events, 44.9 us)
Async XLA Ops:
  2.2 2.8 collective-permute-start
  2.7 2.3 collective-permute-start.1
  6.6 52.3 %all-to-all-start = ((bf16[16,520,128]{2,1,0:T(8,128)(2,1)}), bf16[16,520,128]{2,1,0:T(8,128)(2,1)}, u32[]{:S(2)}, u32[]{:S(2)}) async-start(bf16[16,520,128]{2,1,0:T(8,128)(2,1)} %gather_stripes.2), calls=%async_computation | async-start | bytes 4259840 | tf_op jit(solution)/shard_map/all_to_all | solution.py:127
  18.3 21.4 %collective-permute-start.2 = (bf16[8,64,1024]{2,1,0:T(8,128)(2,1)}, bf16[8,64,1024]{2,1,0:T(8,128)(2,1)S(1)}, u32[]{:S(2)}, u32[]{:S(2)}) collective-permute-start(bf16[8,64,1024]{2,1,0:T(8,128)(2,1)} %constant_dynamic-slice_fusion.11), channel_id=1, source_target_pairs={{0,1},{1,0},{2,3},{3,2},{4,5},{5,4},{6,7},{7,6},{8,9},{9,8},{10,11... | collective-permute-start | bytes 3145736 | tf_op jit(solution)/shard_map/ppermute | solution.py:146
  58.9 58.0 %all-to-all-start.1 = ((bf16[16,512,128]{2,1,0:T(8,128)(2,1)}), bf16[16,512,128]{2,1,0:T(8,128)(2,1)}, u32[]{:S(2)}, u32[]{:S(2)}) async-start(bf16[16,512,128]{2,1,0:T(8,128)(2,1)} %copy-done), calls=%async_computation.1 | async-start | bytes 4194304 | tf_op jit(solution)/shard_map/all_to_all | solution.py:127
  80.1 8.7 %collective-permute-start.3 = (bf16[1024,1024]{1,0:T(8,128)(2,1)}, bf16[1024,1024]{1,0:T(8,128)(2,1)}, u32[]{:S(2)}, u32[]{:S(2)}) collective-permute-start(bf16[1024,1024]{1,0:T(8,128)(2,1)} %get-tuple-element.61.refs_1_.refs_4_), channel_id=1, source_target_pairs={{0,1},{1,0},{2,3},{3,2},{4,5},{5,4},{6,7},{7,6},{8,9},{9,8},{10,11... | collective-permute-start | bytes 6291464 | tf_op jit(solution)/shard_map/ppermute | solution.py:146
  80.1 8.7 %collective-permute-start.4 = (bf16[1024,1024]{1,0:T(8,128)(2,1)}, bf16[1024,1024]{1,0:T(8,128)(2,1)}, u32[]{:S(2)}, u32[]{:S(2)}) collective-permute-start(bf16[1024,1024]{1,0:T(8,128)(2,1)} %get-tuple-element.62.refs_3_.refs_6_), channel_id=1, source_target_pairs={{0,1},{1,0},{2,3},{3,2},{4,5},{5,4},{6,7},{7,6},{8,9},{9,8},{10,11... | collective-permute-start | bytes 6291464 | tf_op jit(solution)/shard_map/ppermute | solution.py:146
  181.8 57.4 %all-to-all-start.2 = ((bf16[16,64,1024]{2,1,0:T(8,128)(2,1)}), bf16[16,64,1024]{2,1,0:T(8,128)(2,1)}, u32[]{:S(2)}, u32[]{:S(2)}) async-start(bf16[16,64,1024]{2,1,0:T(8,128)(2,1)} %bitcast.35), calls=%async_computation.2 | async-start | bytes 4194304 | tf_op jit(solution)/shard_map/all_to_all | solution.py:133
  239.2 7.2 %collective-permute-start.6 = (bf16[1024,1024]{1,0:T(8,128)(2,1)}, bf16[1024,1024]{1,0:T(8,128)(2,1)}, u32[]{:S(2)}, u32[]{:S(2)}) collective-permute-start(bf16[1024,1024]{1,0:T(8,128)(2,1)} %get-tuple-element.85), channel_id=1, source_target_pairs={{0,1},{1,0},{2,3},{3,2},{4,5},{5,4},{6,7},{7,6},{8,9},{9,8},{10,11... | collective-permute-start | bytes 6291464 | tf_op jit(solution)/shard_map/ppermute | solution.py:146
  239.3 7.5 %collective-permute-start.7 = (bf16[1024,1024]{1,0:T(8,128)(2,1)}, bf16[1024,1024]{1,0:T(8,128)(2,1)}, u32[]{:S(2)}, u32[]{:S(2)}) collective-permute-start(bf16[1024,1024]{1,0:T(8,128)(2,1)} %get-tuple-element.87), channel_id=1, source_target_pairs={{0,1},{1,0},{2,3},{3,2},{4,5},{5,4},{6,7},{7,6},{8,9},{9,8},{10,11... | collective-permute-start | bytes 6291464 | tf_op jit(solution)/shard_map/ppermute | solution.py:146
  259.2 56.6 %all-to-all-start.3 = ((bf16[16,64,1024]{2,1,0:T(8,128)(2,1)}), bf16[16,64,1024]{2,1,0:T(8,128)(2,1)}, u32[]{:S(2)}, u32[]{:S(2)}) async-start(bf16[16,64,1024]{2,1,0:T(8,128)(2,1)} %bitcast.34), calls=%async_computation.3 | async-start | bytes 4194304 | tf_op jit(solution)/shard_map/all_to_all | solution.py:133
  267.5 2.7 collective-permute-start.5
  281.0 44.8 %copy-start.11 = (f32[2,1024,4]{1,2,0:T(4,128)S(1)}, f32[2,1024,4]{1,2,0:T(4,128)}, u32[]{:S(2)}) copy-start(f32[2,1024,4]{1,2,0:T(4,128)} %param.43) | copy-start | bytes 98308
  282.6 1.3 collective-permute-start.8
  284.7 4.7 %collective-permute-start.10 = (f32[4,1024]{1,0:T(4,128)S(1)}, f32[4,1024]{1,0:T(4,128)S(1)}, u32[]{:S(2)}, u32[]{:S(2)}) collective-permute-start(f32[4,1024]{1,0:T(4,128)S(1)} %get-tuple-element.108), channel_id=1, source_target_pairs={{0,4},{2,6},{4,0},{6,2},{8,12},{10,14},{12,8},{14,10},{16,20},{18,... | collective-permute-start | bytes 49160 | tf_op jit(solution)/shard_map/ppermute | solution.py:160
  286.6 9.7 %collective-permute-start.11 = (f32[4,1024]{1,0:T(4,128)S(1)}, f32[4,1024]{1,0:T(4,128)S(1)}, u32[]{:S(2)}, u32[]{:S(2)}) collective-permute-start(f32[4,1024]{1,0:T(4,128)S(1)} %get-tuple-element.107), channel_id=1, source_target_pairs={{0,6},{2,4},{4,2},{6,0},{8,14},{10,12},{12,10},{14,8},{16,22},{18,... | collective-permute-start | bytes 49160 | tf_op jit(solution)/shard_map/ppermute | solution.py:160
  288.1 10.1 %collective-permute-start.9 = (f32[4,1024]{1,0:T(4,128)S(1)}, f32[4,1024]{1,0:T(4,128)S(1)}, u32[]{:S(2)}, u32[]{:S(2)}) collective-permute-start(f32[4,1024]{1,0:T(4,128)S(1)} %get-tuple-element.106), channel_id=1, source_target_pairs={{0,2},{2,0},{4,6},{6,4},{8,10},{10,8},{12,14},{14,12},{16,18},{18,... | collective-permute-start | bytes 49160 | tf_op jit(solution)/shard_map/ppermute | solution.py:160
  298.2 4.5 %collective-permute-start.12 = (f32[4,1024]{1,0:T(4,128)S(1)}, f32[4,1024]{1,0:T(4,128)S(1)}, u32[]{:S(2)}, u32[]{:S(2)}) collective-permute-start(f32[4,1024]{1,0:T(4,128)S(1)} %add_add_fusion.1), channel_id=1, source_target_pairs={{0,8},{2,10},{4,12},{6,14},{8,0},{10,2},{12,4},{14,6},{16,24},{18,... | collective-permute-start | bytes 49160 | tf_op jit(solution)/shard_map/ppermute | solution.py:160
  298.3 17.5 %collective-permute-start.13 = (f32[4,1024]{1,0:T(4,128)S(1)}, f32[4,1024]{1,0:T(4,128)S(1)}, u32[]{:S(2)}, u32[]{:S(2)}) collective-permute-start(f32[4,1024]{1,0:T(4,128)S(1)} %add_add_fusion.1), channel_id=1, source_target_pairs={{0,16},{2,18},{4,20},{6,22},{8,24},{10,26},{12,28},{14,30},{16,0},... | collective-permute-start | bytes 49160 | tf_op jit(solution)/shard_map/ppermute | solution.py:160
  298.4 17.5 %collective-permute-start.14 = (f32[4,1024]{1,0:T(4,128)S(1)}, f32[4,1024]{1,0:T(4,128)S(1)}, u32[]{:S(2)}, u32[]{:S(2)}) collective-permute-start(f32[4,1024]{1,0:T(4,128)S(1)} %add_add_fusion.1), channel_id=1, source_target_pairs={{0,24},{2,26},{4,28},{6,30},{8,16},{10,18},{12,20},{14,22},{16,8},... | collective-permute-start | bytes 49160 | tf_op jit(solution)/shard_map/ppermute | solution.py:160
  315.9 5.5 %collective-permute-start.16 = (f32[4,1024]{1,0:T(4,128)S(1)}, f32[4,1024]{1,0:T(4,128)S(1)}, u32[]{:S(2)}, u32[]{:S(2)}) collective-permute-start(f32[4,1024]{1,0:T(4,128)S(1)} %add_add_fusion), channel_id=1, source_target_pairs={{0,2},{2,0},{4,6},{6,4},{8,10},{10,8},{12,14},{14,12},{16,18},{18,... | collective-permute-start | bytes 49160 | tf_op jit(solution)/shard_map/ppermute | solution.py:160
  317.4 3.9 %collective-permute-start.17 = (f32[4,1024]{1,0:T(4,128)S(1)}, f32[4,1024]{1,0:T(4,128)S(1)}, u32[]{:S(2)}, u32[]{:S(2)}) collective-permute-start(f32[4,1024]{1,0:T(4,128)S(1)} %add_add_fusion), channel_id=1, source_target_pairs={{0,4},{2,6},{4,0},{6,2},{8,12},{10,14},{12,8},{14,10},{16,20},{18,... | collective-permute-start | bytes 49160 | tf_op jit(solution)/shard_map/ppermute | solution.py:160
  319.0 4.6 %collective-permute-start.18 = (f32[4,1024]{1,0:T(4,128)S(1)}, f32[4,1024]{1,0:T(4,128)S(1)}, u32[]{:S(2)}, u32[]{:S(2)}) collective-permute-start(f32[4,1024]{1,0:T(4,128)S(1)} %add_add_fusion), channel_id=1, source_target_pairs={{0,6},{2,4},{4,2},{6,0},{8,14},{10,12},{12,10},{14,8},{16,22},{18,... | collective-permute-start | bytes 49160 | tf_op jit(solution)/shard_map/ppermute | solution.py:160
  321.2 5.2 %collective-permute-start.15 = (bf16[8,64,1024]{2,1,0:T(8,128)(2,1)S(1)}, bf16[8,64,1024]{2,1,0:T(8,128)(2,1)S(1)}, u32[]{:S(2)}, u32[]{:S(2)}) collective-permute-start(bf16[8,64,1024]{2,1,0:T(8,128)(2,1)S(1)} %constant_dynamic-slice_fusion.4), channel_id=1, source_target_pairs={{0,1},{1,0},{2,3},{3,2},{4,5},{5,4},{6,7},{7,6},{8,9},{9,8},{10,11... | collective-permute-start | bytes 3145736 | tf_op jit(solution)/shard_map/ppermute | solution.py:146
  (19 other events, 229.0 us)

commit v4 on v3

--- a/solution.py
+++ b/solution.py
@@ -580,7 +580,7 @@
     return x, lambda tokens: pl.BlockSpec(memory_space=pl.ANY)
 
 
-def over_tokens(kernel, name, tokens, operands, outs, sums, flops, scratch=()):
+def over_tokens(kernel, name, tokens, operands, outs, sums, flops, scratch=(), room=None):
     moved = sum(x.size * x.dtype.itemsize for x in [*(x for x, _ in operands), *outs, *sums])
     return pl.pallas_call(
         kernel,
@@ -591,7 +591,7 @@
         out_shape=[*outs, *sums],
         scratch_shapes=list(scratch),
         compiler_params=pltpu.CompilerParams(
-            dimension_semantics=("arbitrary",), vmem_limit_bytes=VMEM_BYTES
+            dimension_semantics=("arbitrary",), vmem_limit_bytes=room or VMEM_BYTES
         ),
         cost_estimate=pl.CostEstimate(flops=flops, bytes_accessed=moved, transcendentals=0),
         name=name,
@@ -855,6 +855,7 @@
         [],
         sums,
         1024 * tokens * width,
+        room=32 * 1024 * 1024,
     )
     layer_out, down_sum = lax.optimization_barrier((spread_stripes(layer_out), down_sum))
     up_parts = [

time: 328 us -> 326 us (level)
  waiting for transfers between devices: 49.2 us -> 60.5 us
  other arithmetic: 20.5 us -> 11.1 us
    all_to_all x2, waiting for transfers between devices: 17.4 us -> 24.5 us  [rows_home(): return lax.all_to_all(y, 'seq', 0, 0, tiled=True)]
    reshape x7, other arithmetic: 8.95 us -> 4.18 us  [row_of(): return vector.astype(jnp.float32).reshape(1, -1)]
    ppermute x10, waiting for transfers between devices: 26.6 us -> 30.8 us  [exchanged(): return lax.ppermute(x, axis, [(i, i ^ by) for i in range(size)])]
  transfers between devices with their start and end apart: 23 -> 23, of which waited for: 10 -> 11; matrix products, arithmetic and copies ran while one was open for 11% -> 7% of each run, Pallas kernels for 34% -> 34%
where the time goes in v4:
time: 326 us; the launch traced here: 328 us
  Pallas kernels  192 us (59%)
  waiting for transfers between devices  60.5 us (19%)
  starting transfers between devices  47.1 us (14%)
  other arithmetic  11.1 us (3%)
  local copies, waits for them, and re-layouts  8.48 us (3%)
  matrix products  7.41 us (2%)
    pallas_call x6, Pallas kernels, over_tokens(): pl.pallas_call(kernel, grid=(tokens // min(TOKEN_BLOCK, tokens),), in_spe...  106 us
    pallas_call x1, Pallas kernels, body(): pull(queries, grad_attended, attended, log_total, *all_keys, *all_values,...  50.4 us
    ppermute x10, waiting for transfers between devices, exchanged(): return lax.ppermute(x, axis, [(i, i ^ by) for i in range(size)])  30.8 us
    pallas_call x1, Pallas kernels, body(): attended, log_total = attend(queries, *all_keys, *all_values, marks, causal)  28.1 us
    all_to_all x2, waiting for transfers between devices, rows_home(): return lax.all_to_all(y, 'seq', 0, 0, tiled=True)  24.5 us
    all_to_all x2, starting transfers between devices, rows_home(): return lax.all_to_all(y, 'seq', 0, 0, tiled=True)  19.2 us
    all_to_all x2, starting transfers between devices, rows_back(): return lax.all_to_all(y, 'seq', 0, 0, tiled=True)  13.9 us
    ppermute x10, starting transfers between devices, exchanged(): return lax.ppermute(x, axis, [(i, i ^ by) for i in range(size)])  12.2 us
  transfers between devices with their start and end apart: 23, of which 11 were waited for; matrix products, arithmetic and copies ran while one was open for 7% of the time, Pallas kernels for 34%

profile of v4, /device:TPU:0, one launch (start us, length us, event | category | flops | bytes accessed | tf_op | source)
XLA Modules:
  0.0 327.9 jit_solution(9381502941220166309)
XLA Ops:
  2.8 2.2 collective-permute-done.1.refs_3_
  6.6 8.4 %all-to-all-start = ((bf16[16,520,128]{2,1,0:T(8,128)(2,1)}), bf16[16,520,128]{2,1,0:T(8,128)(2,1)}, u32[]{:S(2)}, u32[]{:S(2)}) async-start(bf16[16,520,128]{2,1,0:T(8,128)(2,1)} %gather_stripes.2), calls=%async_computation | async-start | bytes 4259840 | tf_op jit(solution)/shard_map/all_to_all | solution.py:127
  15.1 2.0 multiply_convert_fusion.refs_0_
  24.0 3.7 %add_convert_fusion.value_weight_ref = bf16[1024,1024]{1,0:T(8,128)(2,1)} fusion(bf16[1024,4]{0,1:T(4,128)(2,1)S(1)} %get-tuple-element.114, bf16[1024,3072]{1,0:T(8,128)(2,1)} %key_weight_ref.3, f32[2,4,1024]{2,1,0:T(4,128)S(1)} %copy-done.7), kind=kOutput, calls=%fused_computation | convolution fusion | flops 12582912 | bytes 4210688 | tf_op jit(solution)/shard_map/dot_general | solution.py:33
  27.7 3.7 %add_convert_fusion.1.weight_ref.query_weight_ref = bf16[1024,1024]{1,0:T(8,128)(2,1)} fusion(bf16[1024,4]{0,1:T(4,128)(2,1)S(1)} %get-tuple-element.113, bf16[1024,3072]{1,0:T(8,128)(2,1)} %key_weight_ref.3, f32[2,4,1024]{2,1,0:T(4,128)S(1)} %copy-done.7), kind=kOutput, calls=%fused_computation.1 | convolution fusion | flops 12582912 | bytes 4210688 | tf_op jit(solution)/shard_map/dot_general | solution.py:33
  34.4 24.5 %all-to-all-done.x_ref = bf16[16,520,128]{2,1,0:T(8,128)(2,1)} async-done(((bf16[16,520,128]{2,1,0:T(8,128)(2,1)}), bf16[16,520,128]{2,1,0:T(8,128)(2,1)}, u32[]{:S(2)}, u32[]{:S(2)}) %all-to-all-start) | async-done | bytes 2129952 | tf_op jit(solution)/shard_map/all_to_all | solution.py:127
  58.9 10.8 %all-to-all-start.1 = ((bf16[16,512,128]{2,1,0:T(8,128)(2,1)}), bf16[16,512,128]{2,1,0:T(8,128)(2,1)}, u32[]{:S(2)}, u32[]{:S(2)}) async-start(bf16[16,512,128]{2,1,0:T(8,128)(2,1)} %copy-done), calls=%async_computation.1 | async-start | bytes 4194304 | tf_op jit(solution)/shard_map/all_to_all | solution.py:127
  70.3 9.7 %enter.1 = (bf16[1024,1024]{1,0:T(8,128)(2,1)}, bf16[1024,1024]{1,0:T(8,128)(2,1)}, bf16[1024,1024]{1,0:T(8,128)(2,1)}) custom-call(bf16[16,520,128]{2,1,0:T(8,128)(2,1)} %all-to-all-done.x_ref, f32[1,1024]{1,0:T(1,128)} %bitcast.37, f32[1,1024]{1,0:T(1,128)} %bitcast.46, f32[1,1024]{1,0:T(1,128)} %get-tuple-element.118.bias_ref, ...), custom_call_target="tpu_custom_call" | custom-call | flops 4294967296 | bytes 16822272 | tf_op jit(solution)/shard_map/enter/pallas_call | solution.py:585
  81.5 6.1 %ask.1.refs_0_ = bf16[1024,1024]{1,0:T(8,128)(2,1)} custom-call(bf16[1024,1024]{1,0:T(8,128)(2,1)} %get-tuple-element.88.normed_ref, f32[1,1024]{1,0:T(1,128)} %get-tuple-element.117.bias_ref, bf16[1024,1024]{1,0:T(8,128)(2,1)} %add_convert_fusion.1.weight_ref.query_weight_ref), custom_call_target="tpu_custom_call" | custom-call | flops 2147483648 | bytes 6295552 | tf_op jit(solution)/shard_map/ask/pallas_call | solution.py:585
  88.7 28.1 %attend.1 = (bf16[1024,1024]{1,0:T(8,128)(2,1)}, f32[64,1024]{1,0:T(8,128)}) custom-call(bf16[1024,1024]{1,0:T(8,128)(2,1)} %ask.1.refs_0_, bf16[1024,1024]{1,0:T(8,128)(2,1)} %get-tuple-element.61.refs_1_.refs_4_, bf16[1024,1024]{1,0:T(8,128)(2,1)} %collective-permute-done.3.refs_2_.refs_5_, bf16[1024,1024]{1,0:T(8,128)(2,1)} %get-tuple-element.62.refs_3_.refs_6_, ...), custom_call_target="tpu_custom_call" | custom-call | flops 4831838208 | bytes 12582912 | tf_op jit(solution)/shard_map/attend/pallas_call | solution.py:788
  116.8 64.8 %middle.1 = (bf16[1024,1024]{1,0:T(8,128)(2,1)}, bf16[1024,1024]{1,0:T(8,128)(2,1)}, bf16[1024,1024]{1,0:T(8,128)(2,1)}) custom-call(bf16[16,520,128]{2,1,0:T(8,128)(2,1)} %all-to-all-done.x_ref, bf16[1024,1024]{1,0:T(8,128)(2,1)} %get-tuple-element.64.attended_ref.refs_2_, bf16[16,512,128]{2,1,0:T(8,128)(2,1)} %all-to-all-done.1.cotangent_ref, ...), custom_call_target="tpu_custom_call" | custom-call | flops 38654705664 | bytes 31522816 | tf_op jit(solution)/shard_map/middle/pallas_call | solution.py:585
  181.7 7.1 %all-to-all-start.2 = ((bf16[16,64,1024]{2,1,0:T(8,128)(2,1)}), bf16[16,64,1024]{2,1,0:T(8,128)(2,1)}, u32[]{:S(2)}, u32[]{:S(2)}) async-start(bf16[16,64,1024]{2,1,0:T(8,128)(2,1)} %bitcast.35), calls=%async_computation.2 | async-start | bytes 4194304 | tf_op jit(solution)/shard_map/all_to_all | solution.py:133
  188.7 50.4 %pull.1 = (bf16[1024,1024]{1,0:T(8,128)(2,1)}, bf16[1024,1024]{1,0:T(8,128)(2,1)}, bf16[1024,1024]{1,0:T(8,128)(2,1)}, bf16[1024,1024]{1,0:T(8,128)(2,1)}, bf16[1024,1024]{1,0:T(8,128)(2,1)}) custom-call(bf16[1024,1024]{1,0:T(8,128)(2,1)} %ask.1.refs_0_, bf16[1024,1024]{1,0:T(8,128)(2,1)} %get-tuple-element.72.refs_1_, ...), custom_call_target="tpu_custom_call" | custom-call | flops 12079595520 | bytes 25165824 | tf_op jit(solution)/shard_map/pull/pallas_call | solution.py:806
  239.8 6.6 %return.1.from_queries_ref = f32[1024,1024]{1,0:T(8,128)} custom-call(bf16[1024,1024]{1,0:T(8,128)(2,1)} %get-tuple-element.83.grad_query_ref, bf16[1024,1024]{1,0:T(8,128)(2,1)} %add_convert_fusion.1.weight_ref.query_weight_ref), custom_call_target="tpu_custom_call" | custom-call | flops 2147483648 | bytes 8388608 | tf_op jit(solution)/shard_map/return/pallas_call | solution.py:585
  246.7 12.5 %leave.1 = bf16[1024,1024]{1,0:T(8,128)(2,1)} custom-call(bf16[16,520,128]{2,1,0:T(8,128)(2,1)} %all-to-all-done.x_ref, f32[1,1024]{1,0:T(1,128)} %bitcast.38, bf16[1024,3072]{1,0:T(8,128)(2,1)} %key_weight_ref.3, bf16[1024,1024]{1,0:T(8,128)(2,1)} %add_convert_fusion.value_weight_ref, bf16[1024,1024]{1,0:T(8,128)(2,1)} %get-tuple-element.82.grad_middle_ref, ...), custom_call_target="tpu_custom_call" | custom-call | flops 4294967296 | bytes 27299840 | tf_op jit(solution)/shard_map/leave/pallas_call | solution.py:585
  259.2 6.8 %all-to-all-start.3 = ((bf16[16,64,1024]{2,1,0:T(8,128)(2,1)}), bf16[16,64,1024]{2,1,0:T(8,128)(2,1)S(1)}, u32[]{:S(2)}, u32[]{:S(2)}) async-start(bf16[16,64,1024]{2,1,0:T(8,128)(2,1)} %bitcast.34), calls=%async_computation.3 | async-start | bytes 4194304 | tf_op jit(solution)/shard_map/all_to_all | solution.py:133
  267.7 2.6 collective-permute-done.5.refs_1_
  270.3 2.6 spread_stripes.2
  272.9 6.4 %adapt.1 = (f32[8,1024]{1,0:T(8,128)S(1)}, f32[8,2048]{1,0:T(8,128)S(1)}) custom-call(bf16[1024,128]{1,0:T(8,128)(2,1)S(1)} %pad.13.down_ref, bf16[128,2048]{1,0:T(8,128)(2,1)S(1)} %fusion.1.up_ref, bf16[1024,1024]{1,0:T(8,128)(2,1)S(1)} %copy-done.4, bf16[1024,1024]{1,0:T(8,128)(2,1)S(1)} %copy-done.2, bf16[1024,1024]{1,0:T(8,128)(2,1)S(1)} %copy-done.1, ...), custom_call_target="tpu_custom_call" | custom-call | flops 1073741824 | bytes 9273344 | tf_op jit(solution)/shard_map/adapt/pallas_call | solution.py:585
  280.8 2.0 collective-permute-start.10
  284.6 11.6 %collective-permute-done.11 = f32[4,1024]{1,0:T(4,128)S(1)} collective-permute-done((f32[4,1024]{1,0:T(4,128)S(1)}, f32[4,1024]{1,0:T(4,128)S(1)}, u32[]{:S(2)}, u32[]{:S(2)}) %collective-permute-start.11) | collective-permute-done | bytes 16416 | tf_op jit(solution)/shard_map/ppermute | solution.py:160
  296.4 4.3 %collective-permute-start.14 = (f32[4,1024]{1,0:T(4,128)S(1)}, f32[4,1024]{1,0:T(4,128)S(1)}, u32[]{:S(2)}, u32[]{:S(2)}) collective-permute-start(f32[4,1024]{1,0:T(4,128)S(1)} %add_add_fusion.1), channel_id=1, source_target_pairs={{0,24},{2,26},{4,28},{6,30},{8,16},{10,18},{12,20},{14,22},{16,8},... | collective-permute-start | bytes 49160 | tf_op jit(solution)/shard_map/ppermute | solution.py:160
  301.6 14.2 %collective-permute-done.13 = f32[4,1024]{1,0:T(4,128)S(1)} collective-permute-done((f32[4,1024]{1,0:T(4,128)S(1)}, f32[4,1024]{1,0:T(4,128)S(1)}, u32[]{:S(2)}, u32[]{:S(2)}) %collective-permute-start.13) | collective-permute-done | bytes 16416 | tf_op jit(solution)/shard_map/ppermute | solution.py:160
  321.1 2.5 collective-permute-done.18
  (140 shorter events, 32.9 us)
Async XLA Ops:
  2.2 2.8 collective-permute-start
  2.7 2.3 collective-permute-start.1
  6.6 52.3 %all-to-all-start = ((bf16[16,520,128]{2,1,0:T(8,128)(2,1)}), bf16[16,520,128]{2,1,0:T(8,128)(2,1)}, u32[]{:S(2)}, u32[]{:S(2)}) async-start(bf16[16,520,128]{2,1,0:T(8,128)(2,1)} %gather_stripes.2), calls=%async_computation | async-start | bytes 4259840 | tf_op jit(solution)/shard_map/all_to_all | solution.py:127
  18.4 13.0 %collective-permute-start.2 = (bf16[8,64,1024]{2,1,0:T(8,128)(2,1)}, bf16[8,64,1024]{2,1,0:T(8,128)(2,1)}, u32[]{:S(2)}, u32[]{:S(2)}) collective-permute-start(bf16[8,64,1024]{2,1,0:T(8,128)(2,1)} %constant_dynamic-slice_fusion.11), channel_id=1, source_target_pairs={{0,1},{1,0},{2,3},{3,2},{4,5},{5,4},{6,7},{7,6},{8,9},{9,8},{10,11... | collective-permute-start | bytes 3145736 | tf_op jit(solution)/shard_map/ppermute | solution.py:146
  58.9 57.9 %all-to-all-start.1 = ((bf16[16,512,128]{2,1,0:T(8,128)(2,1)}), bf16[16,512,128]{2,1,0:T(8,128)(2,1)}, u32[]{:S(2)}, u32[]{:S(2)}) async-start(bf16[16,512,128]{2,1,0:T(8,128)(2,1)} %copy-done), calls=%async_computation.1 | async-start | bytes 4194304 | tf_op jit(solution)/shard_map/all_to_all | solution.py:127
  80.0 8.7 %collective-permute-start.3 = (bf16[1024,1024]{1,0:T(8,128)(2,1)}, bf16[1024,1024]{1,0:T(8,128)(2,1)}, u32[]{:S(2)}, u32[]{:S(2)}) collective-permute-start(bf16[1024,1024]{1,0:T(8,128)(2,1)} %get-tuple-element.61.refs_1_.refs_4_), channel_id=1, source_target_pairs={{0,1},{1,0},{2,3},{3,2},{4,5},{5,4},{6,7},{7,6},{8,9},{9,8},{10,11... | collective-permute-start | bytes 6291464 | tf_op jit(solution)/shard_map/ppermute | solution.py:146
  80.0 8.7 %collective-permute-start.4 = (bf16[1024,1024]{1,0:T(8,128)(2,1)}, bf16[1024,1024]{1,0:T(8,128)(2,1)}, u32[]{:S(2)}, u32[]{:S(2)}) collective-permute-start(bf16[1024,1024]{1,0:T(8,128)(2,1)} %get-tuple-element.62.refs_3_.refs_6_), channel_id=1, source_target_pairs={{0,1},{1,0},{2,3},{3,2},{4,5},{5,4},{6,7},{7,6},{8,9},{9,8},{10,11... | collective-permute-start | bytes 6291464 | tf_op jit(solution)/shard_map/ppermute | solution.py:146
  181.7 57.5 %all-to-all-start.2 = ((bf16[16,64,1024]{2,1,0:T(8,128)(2,1)}), bf16[16,64,1024]{2,1,0:T(8,128)(2,1)}, u32[]{:S(2)}, u32[]{:S(2)}) async-start(bf16[16,64,1024]{2,1,0:T(8,128)(2,1)} %bitcast.35), calls=%async_computation.2 | async-start | bytes 4194304 | tf_op jit(solution)/shard_map/all_to_all | solution.py:133
  239.2 7.2 %collective-permute-start.6 = (bf16[1024,1024]{1,0:T(8,128)(2,1)}, bf16[1024,1024]{1,0:T(8,128)(2,1)}, u32[]{:S(2)}, u32[]{:S(2)}) collective-permute-start(bf16[1024,1024]{1,0:T(8,128)(2,1)} %get-tuple-element.85), channel_id=1, source_target_pairs={{0,1},{1,0},{2,3},{3,2},{4,5},{5,4},{6,7},{7,6},{8,9},{9,8},{10,11... | collective-permute-start | bytes 6291464 | tf_op jit(solution)/shard_map/ppermute | solution.py:146
  239.3 7.5 %collective-permute-start.7 = (bf16[1024,1024]{1,0:T(8,128)(2,1)}, bf16[1024,1024]{1,0:T(8,128)(2,1)}, u32[]{:S(2)}, u32[]{:S(2)}) collective-permute-start(bf16[1024,1024]{1,0:T(8,128)(2,1)} %get-tuple-element.87), channel_id=1, source_target_pairs={{0,1},{1,0},{2,3},{3,2},{4,5},{5,4},{6,7},{7,6},{8,9},{9,8},{10,11... | collective-permute-start | bytes 6291464 | tf_op jit(solution)/shard_map/ppermute | solution.py:146
  259.2 56.6 %all-to-all-start.3 = ((bf16[16,64,1024]{2,1,0:T(8,128)(2,1)}), bf16[16,64,1024]{2,1,0:T(8,128)(2,1)S(1)}, u32[]{:S(2)}, u32[]{:S(2)}) async-start(bf16[16,64,1024]{2,1,0:T(8,128)(2,1)} %bitcast.34), calls=%async_computation.3 | async-start | bytes 4194304 | tf_op jit(solution)/shard_map/all_to_all | solution.py:133
  267.6 2.7 collective-permute-start.5
  279.4 46.3 %copy-start.12 = (f32[2,1024,4]{1,2,0:T(4,128)S(1)}, f32[2,1024,4]{1,2,0:T(4,128)}, u32[]{:S(2)}) copy-start(f32[2,1024,4]{1,2,0:T(4,128)} %param.43) | copy-start | bytes 98308
  279.4 1.3 collective-permute-start.8
  280.8 3.8 %collective-permute-start.10 = (f32[4,1024]{1,0:T(4,128)S(1)}, f32[4,1024]{1,0:T(4,128)S(1)}, u32[]{:S(2)}, u32[]{:S(2)}) collective-permute-start(f32[4,1024]{1,0:T(4,128)S(1)} %get-tuple-element.108), channel_id=1, source_target_pairs={{0,4},{2,6},{4,0},{6,2},{8,12},{10,14},{12,8},{14,10},{16,20},{18,... | collective-permute-start | bytes 49160 | tf_op jit(solution)/shard_map/ppermute | solution.py:160
  282.8 13.4 %collective-permute-start.11 = (f32[4,1024]{1,0:T(4,128)S(1)}, f32[4,1024]{1,0:T(4,128)S(1)}, u32[]{:S(2)}, u32[]{:S(2)}) collective-permute-start(f32[4,1024]{1,0:T(4,128)S(1)} %get-tuple-element.107), channel_id=1, source_target_pairs={{0,6},{2,4},{4,2},{6,0},{8,14},{10,12},{12,10},{14,8},{16,22},{18,... | collective-permute-start | bytes 49160 | tf_op jit(solution)/shard_map/ppermute | solution.py:160
  284.2 12.0 %collective-permute-start.9 = (f32[4,1024]{1,0:T(4,128)S(1)}, f32[4,1024]{1,0:T(4,128)S(1)}, u32[]{:S(2)}, u32[]{:S(2)}) collective-permute-start(f32[4,1024]{1,0:T(4,128)S(1)} %get-tuple-element.106), channel_id=1, source_target_pairs={{0,2},{2,0},{4,6},{6,4},{8,10},{10,8},{12,14},{14,12},{16,18},{18,... | collective-permute-start | bytes 49160 | tf_op jit(solution)/shard_map/ppermute | solution.py:160
  296.2 5.4 %collective-permute-start.12 = (f32[4,1024]{1,0:T(4,128)S(1)}, f32[4,1024]{1,0:T(4,128)S(1)}, u32[]{:S(2)}, u32[]{:S(2)}) collective-permute-start(f32[4,1024]{1,0:T(4,128)S(1)} %add_add_fusion.1), channel_id=1, source_target_pairs={{0,8},{2,10},{4,12},{6,14},{8,0},{10,2},{12,4},{14,6},{16,24},{18,... | collective-permute-start | bytes 49160 | tf_op jit(solution)/shard_map/ppermute | solution.py:160
  296.3 19.5 %collective-permute-start.13 = (f32[4,1024]{1,0:T(4,128)S(1)}, f32[4,1024]{1,0:T(4,128)S(1)}, u32[]{:S(2)}, u32[]{:S(2)}) collective-permute-start(f32[4,1024]{1,0:T(4,128)S(1)} %add_add_fusion.1), channel_id=1, source_target_pairs={{0,16},{2,18},{4,20},{6,22},{8,24},{10,26},{12,28},{14,30},{16,0},... | collective-permute-start | bytes 49160 | tf_op jit(solution)/shard_map/ppermute | solution.py:160
  296.4 19.4 %collective-permute-start.14 = (f32[4,1024]{1,0:T(4,128)S(1)}, f32[4,1024]{1,0:T(4,128)S(1)}, u32[]{:S(2)}, u32[]{:S(2)}) collective-permute-start(f32[4,1024]{1,0:T(4,128)S(1)} %add_add_fusion.1), channel_id=1, source_target_pairs={{0,24},{2,26},{4,28},{6,30},{8,16},{10,18},{12,20},{14,22},{16,8},... | collective-permute-start | bytes 49160 | tf_op jit(solution)/shard_map/ppermute | solution.py:160
  315.8 5.1 %collective-permute-start.16 = (f32[4,1024]{1,0:T(4,128)S(1)}, f32[4,1024]{1,0:T(4,128)S(1)}, u32[]{:S(2)}, u32[]{:S(2)}) collective-permute-start(f32[4,1024]{1,0:T(4,128)S(1)} %add_add_fusion), channel_id=1, source_target_pairs={{0,2},{2,0},{4,6},{6,4},{8,10},{10,8},{12,14},{14,12},{16,18},{18,... | collective-permute-start | bytes 49160 | tf_op jit(solution)/shard_map/ppermute | solution.py:160
  317.3 3.7 %collective-permute-start.17 = (f32[4,1024]{1,0:T(4,128)S(1)}, f32[4,1024]{1,0:T(4,128)S(1)}, u32[]{:S(2)}, u32[]{:S(2)}) collective-permute-start(f32[4,1024]{1,0:T(4,128)S(1)} %add_add_fusion), channel_id=1, source_target_pairs={{0,4},{2,6},{4,0},{6,2},{8,12},{10,14},{12,8},{14,10},{16,20},{18,... | collective-permute-start | bytes 49160 | tf_op jit(solution)/shard_map/ppermute | solution.py:160
  319.0 4.6 %collective-permute-start.18 = (f32[4,1024]{1,0:T(4,128)S(1)}, f32[4,1024]{1,0:T(4,128)S(1)}, u32[]{:S(2)}, u32[]{:S(2)}) collective-permute-start(f32[4,1024]{1,0:T(4,128)S(1)} %add_add_fusion), channel_id=1, source_target_pairs={{0,6},{2,4},{4,2},{6,0},{8,14},{10,12},{12,10},{14,8},{16,22},{18,... | collective-permute-start | bytes 49160 | tf_op jit(solution)/shard_map/ppermute | solution.py:160
  320.9 5.4 %collective-permute-start.15 = (bf16[8,64,1024]{2,1,0:T(8,128)(2,1)}, bf16[8,64,1024]{2,1,0:T(8,128)(2,1)S(1)}, u32[]{:S(2)}, u32[]{:S(2)}) collective-permute-start(bf16[8,64,1024]{2,1,0:T(8,128)(2,1)} %constant_dynamic-slice_fusion.4), channel_id=1, source_target_pairs={{0,1},{1,0},{2,3},{3,2},{4,5},{5,4},{6,7},{7,6},{8,9},{9,8},{10,11... | collective-permute-start | bytes 3145736 | tf_op jit(solution)/shard_map/ppermute | solution.py:146
  (25 other events, 219.0 us)

commit v5 on v4

--- a/solution.py
+++ b/solution.py
@@ -15,7 +15,7 @@
 TOKEN_BLOCK = 256
 HIDDEN_BLOCK = 1024
 AHEAD = 2
-PER = 2
+PER = 3
 SCORES_AHEAD = 2
 DELAY = 0
 VMEM_BYTES = 63 * 1024 * 1024

time: 326 us -> 326 us (level)
  no operation moved by 1% of the time
where the time goes in v5:
time: 326 us; the launch traced here: 328 us
  Pallas kernels  192 us (59%)
  waiting for transfers between devices  60.5 us (19%)
  starting transfers between devices  47.1 us (14%)
  other arithmetic  11.1 us (3%)
  local copies, waits for them, and re-layouts  8.48 us (3%)
  matrix products  7.41 us (2%)
    pallas_call x6, Pallas kernels, over_tokens(): pl.pallas_call(kernel, grid=(tokens // min(TOKEN_BLOCK, tokens),), in_spe...  106 us
    pallas_call x1, Pallas kernels, body(): pull(queries, grad_attended, attended, log_total, *all_keys, *all_values,...  50.3 us
    ppermute x10, waiting for transfers between devices, exchanged(): return lax.ppermute(x, axis, [(i, i ^ by) for i in range(size)])  30.8 us
    pallas_call x1, Pallas kernels, body(): attended, log_total = attend(queries, *all_keys, *all_values, marks, causal)  28.1 us
    all_to_all x2, waiting for transfers between devices, rows_home(): return lax.all_to_all(y, 'seq', 0, 0, tiled=True)  24.5 us
    all_to_all x2, starting transfers between devices, rows_home(): return lax.all_to_all(y, 'seq', 0, 0, tiled=True)  19.2 us
    all_to_all x2, starting transfers between devices, rows_back(): return lax.all_to_all(y, 'seq', 0, 0, tiled=True)  13.9 us
    ppermute x10, starting transfers between devices, exchanged(): return lax.ppermute(x, axis, [(i, i ^ by) for i in range(size)])  12.2 us
  transfers between devices with their start and end apart: 23, of which 11 were waited for; matrix products, arithmetic and copies ran while one was open for 7% of the time, Pallas kernels for 34%

profile of v5, /device:TPU:0, one launch (start us, length us, event | category | flops | bytes accessed | tf_op | source)
XLA Modules:
  0.0 327.8 jit_solution(10422972520475856132)
XLA Ops:
  2.8 2.2 collective-permute-done.1.refs_3_
  6.6 8.4 %all-to-all-start = ((bf16[16,520,128]{2,1,0:T(8,128)(2,1)}), bf16[16,520,128]{2,1,0:T(8,128)(2,1)}, u32[]{:S(2)}, u32[]{:S(2)}) async-start(bf16[16,520,128]{2,1,0:T(8,128)(2,1)} %gather_stripes.2), calls=%async_computation | async-start | bytes 4259840 | tf_op jit(solution)/shard_map/all_to_all | solution.py:127
  15.1 2.0 multiply_convert_fusion.refs_0_
  24.0 3.7 %add_convert_fusion.value_weight_ref = bf16[1024,1024]{1,0:T(8,128)(2,1)} fusion(bf16[1024,4]{0,1:T(4,128)(2,1)S(1)} %get-tuple-element.114, bf16[1024,3072]{1,0:T(8,128)(2,1)} %key_weight_ref.3, f32[2,4,1024]{2,1,0:T(4,128)S(1)} %copy-done.7), kind=kOutput, calls=%fused_computation | convolution fusion | flops 12582912 | bytes 4210688 | tf_op jit(solution)/shard_map/dot_general | solution.py:33
  27.7 3.7 %add_convert_fusion.1.weight_ref.query_weight_ref = bf16[1024,1024]{1,0:T(8,128)(2,1)} fusion(bf16[1024,4]{0,1:T(4,128)(2,1)S(1)} %get-tuple-element.113, bf16[1024,3072]{1,0:T(8,128)(2,1)} %key_weight_ref.3, f32[2,4,1024]{2,1,0:T(4,128)S(1)} %copy-done.7), kind=kOutput, calls=%fused_computation.1 | convolution fusion | flops 12582912 | bytes 4210688 | tf_op jit(solution)/shard_map/dot_general | solution.py:33
  34.4 24.5 %all-to-all-done.x_ref = bf16[16,520,128]{2,1,0:T(8,128)(2,1)} async-done(((bf16[16,520,128]{2,1,0:T(8,128)(2,1)}), bf16[16,520,128]{2,1,0:T(8,128)(2,1)}, u32[]{:S(2)}, u32[]{:S(2)}) %all-to-all-start) | async-done | bytes 2129952 | tf_op jit(solution)/shard_map/all_to_all | solution.py:127
  58.9 10.8 %all-to-all-start.1 = ((bf16[16,512,128]{2,1,0:T(8,128)(2,1)}), bf16[16,512,128]{2,1,0:T(8,128)(2,1)}, u32[]{:S(2)}, u32[]{:S(2)}) async-start(bf16[16,512,128]{2,1,0:T(8,128)(2,1)} %copy-done), calls=%async_computation.1 | async-start | bytes 4194304 | tf_op jit(solution)/shard_map/all_to_all | solution.py:127
  70.3 9.7 %enter.1 = (bf16[1024,1024]{1,0:T(8,128)(2,1)}, bf16[1024,1024]{1,0:T(8,128)(2,1)}, bf16[1024,1024]{1,0:T(8,128)(2,1)}) custom-call(bf16[16,520,128]{2,1,0:T(8,128)(2,1)} %all-to-all-done.x_ref, f32[1,1024]{1,0:T(1,128)} %bitcast.37, f32[1,1024]{1,0:T(1,128)} %bitcast.46, f32[1,1024]{1,0:T(1,128)} %get-tuple-element.118.bias_ref, ...), custom_call_target="tpu_custom_call" | custom-call | flops 4294967296 | bytes 16822272 | tf_op jit(solution)/shard_map/enter/pallas_call | solution.py:585
  81.5 6.1 %ask.1.refs_0_ = bf16[1024,1024]{1,0:T(8,128)(2,1)} custom-call(bf16[1024,1024]{1,0:T(8,128)(2,1)} %get-tuple-element.88.normed_ref, f32[1,1024]{1,0:T(1,128)} %get-tuple-element.117.bias_ref, bf16[1024,1024]{1,0:T(8,128)(2,1)} %add_convert_fusion.1.weight_ref.query_weight_ref), custom_call_target="tpu_custom_call" | custom-call | flops 2147483648 | bytes 6295552 | tf_op jit(solution)/shard_map/ask/pallas_call | solution.py:585
  88.7 28.1 %attend.1 = (bf16[1024,1024]{1,0:T(8,128)(2,1)}, f32[64,1024]{1,0:T(8,128)}) custom-call(bf16[1024,1024]{1,0:T(8,128)(2,1)} %ask.1.refs_0_, bf16[1024,1024]{1,0:T(8,128)(2,1)} %get-tuple-element.61.refs_1_.refs_4_, bf16[1024,1024]{1,0:T(8,128)(2,1)} %collective-permute-done.3.refs_2_.refs_5_, bf16[1024,1024]{1,0:T(8,128)(2,1)} %get-tuple-element.62.refs_3_.refs_6_, ...), custom_call_target="tpu_custom_call" | custom-call | flops 4831838208 | bytes 12582912 | tf_op jit(solution)/shard_map/attend/pallas_call | solution.py:788
  116.8 64.8 %middle.1 = (bf16[1024,1024]{1,0:T(8,128)(2,1)}, bf16[1024,1024]{1,0:T(8,128)(2,1)}, bf16[1024,1024]{1,0:T(8,128)(2,1)}) custom-call(bf16[16,520,128]{2,1,0:T(8,128)(2,1)} %all-to-all-done.x_ref, bf16[1024,1024]{1,0:T(8,128)(2,1)} %get-tuple-element.64.attended_ref.refs_2_, bf16[16,512,128]{2,1,0:T(8,128)(2,1)} %all-to-all-done.1.cotangent_ref, ...), custom_call_target="tpu_custom_call" | custom-call | flops 38654705664 | bytes 31522816 | tf_op jit(solution)/shard_map/middle/pallas_call | solution.py:585
  181.7 7.1 %all-to-all-start.2 = ((bf16[16,64,1024]{2,1,0:T(8,128)(2,1)}), bf16[16,64,1024]{2,1,0:T(8,128)(2,1)}, u32[]{:S(2)}, u32[]{:S(2)}) async-start(bf16[16,64,1024]{2,1,0:T(8,128)(2,1)} %bitcast.35), calls=%async_computation.2 | async-start | bytes 4194304 | tf_op jit(solution)/shard_map/all_to_all | solution.py:133
  188.7 50.3 %pull.1 = (bf16[1024,1024]{1,0:T(8,128)(2,1)}, bf16[1024,1024]{1,0:T(8,128)(2,1)}, bf16[1024,1024]{1,0:T(8,128)(2,1)}, bf16[1024,1024]{1,0:T(8,128)(2,1)}, bf16[1024,1024]{1,0:T(8,128)(2,1)}) custom-call(bf16[1024,1024]{1,0:T(8,128)(2,1)} %ask.1.refs_0_, bf16[1024,1024]{1,0:T(8,128)(2,1)} %get-tuple-element.72.refs_1_, ...), custom_call_target="tpu_custom_call" | custom-call | flops 12079595520 | bytes 25165824 | tf_op jit(solution)/shard_map/pull/pallas_call | solution.py:806
  239.6 6.6 %return.1.from_queries_ref = f32[1024,1024]{1,0:T(8,128)} custom-call(bf16[1024,1024]{1,0:T(8,128)(2,1)} %get-tuple-element.83.grad_query_ref, bf16[1024,1024]{1,0:T(8,128)(2,1)} %add_convert_fusion.1.weight_ref.query_weight_ref), custom_call_target="tpu_custom_call" | custom-call | flops 2147483648 | bytes 8388608 | tf_op jit(solution)/shard_map/return/pallas_call | solution.py:585
  246.6 12.5 %leave.1 = bf16[1024,1024]{1,0:T(8,128)(2,1)} custom-call(bf16[16,520,128]{2,1,0:T(8,128)(2,1)} %all-to-all-done.x_ref, f32[1,1024]{1,0:T(1,128)} %bitcast.38, bf16[1024,3072]{1,0:T(8,128)(2,1)} %key_weight_ref.3, bf16[1024,1024]{1,0:T(8,128)(2,1)} %add_convert_fusion.value_weight_ref, bf16[1024,1024]{1,0:T(8,128)(2,1)} %get-tuple-element.82.grad_middle_ref, ...), custom_call_target="tpu_custom_call" | custom-call | flops 4294967296 | bytes 27299840 | tf_op jit(solution)/shard_map/leave/pallas_call | solution.py:585
  259.0 6.8 %all-to-all-start.3 = ((bf16[16,64,1024]{2,1,0:T(8,128)(2,1)}), bf16[16,64,1024]{2,1,0:T(8,128)(2,1)S(1)}, u32[]{:S(2)}, u32[]{:S(2)}) async-start(bf16[16,64,1024]{2,1,0:T(8,128)(2,1)} %bitcast.34), calls=%async_computation.3 | async-start | bytes 4194304 | tf_op jit(solution)/shard_map/all_to_all | solution.py:133
  267.5 2.6 collective-permute-done.5.refs_1_
  270.1 2.6 spread_stripes.2
  272.8 6.4 %adapt.1 = (f32[8,1024]{1,0:T(8,128)S(1)}, f32[8,2048]{1,0:T(8,128)S(1)}) custom-call(bf16[1024,128]{1,0:T(8,128)(2,1)S(1)} %pad.13.down_ref, bf16[128,2048]{1,0:T(8,128)(2,1)S(1)} %fusion.1.up_ref, bf16[1024,1024]{1,0:T(8,128)(2,1)S(1)} %copy-done.4, bf16[1024,1024]{1,0:T(8,128)(2,1)S(1)} %copy-done.2, bf16[1024,1024]{1,0:T(8,128)(2,1)S(1)} %copy-done.1, ...), custom_call_target="tpu_custom_call" | custom-call | flops 1073741824 | bytes 9273344 | tf_op jit(solution)/shard_map/adapt/pallas_call | solution.py:585
  280.6 2.0 collective-permute-start.10
  284.4 11.6 %collective-permute-done.11 = f32[4,1024]{1,0:T(4,128)S(1)} collective-permute-done((f32[4,1024]{1,0:T(4,128)S(1)}, f32[4,1024]{1,0:T(4,128)S(1)}, u32[]{:S(2)}, u32[]{:S(2)}) %collective-permute-start.11) | collective-permute-done | bytes 16416 | tf_op jit(solution)/shard_map/ppermute | solution.py:160
  296.2 4.3 %collective-permute-start.14 = (f32[4,1024]{1,0:T(4,128)S(1)}, f32[4,1024]{1,0:T(4,128)S(1)}, u32[]{:S(2)}, u32[]{:S(2)}) collective-permute-start(f32[4,1024]{1,0:T(4,128)S(1)} %add_add_fusion.1), channel_id=1, source_target_pairs={{0,24},{2,26},{4,28},{6,30},{8,16},{10,18},{12,20},{14,22},{16,8},... | collective-permute-start | bytes 49160 | tf_op jit(solution)/shard_map/ppermute | solution.py:160
  301.4 14.2 %collective-permute-done.13 = f32[4,1024]{1,0:T(4,128)S(1)} collective-permute-done((f32[4,1024]{1,0:T(4,128)S(1)}, f32[4,1024]{1,0:T(4,128)S(1)}, u32[]{:S(2)}, u32[]{:S(2)}) %collective-permute-start.13) | collective-permute-done | bytes 16416 | tf_op jit(solution)/shard_map/ppermute | solution.py:160
  320.9 2.5 collective-permute-done.18
  (140 shorter events, 32.9 us)
Async XLA Ops:
  2.2 2.8 collective-permute-start
  2.7 2.3 collective-permute-start.1
  6.6 52.3 %all-to-all-start = ((bf16[16,520,128]{2,1,0:T(8,128)(2,1)}), bf16[16,520,128]{2,1,0:T(8,128)(2,1)}, u32[]{:S(2)}, u32[]{:S(2)}) async-start(bf16[16,520,128]{2,1,0:T(8,128)(2,1)} %gather_stripes.2), calls=%async_computation | async-start | bytes 4259840 | tf_op jit(solution)/shard_map/all_to_all | solution.py:127
  18.4 13.0 %collective-permute-start.2 = (bf16[8,64,1024]{2,1,0:T(8,128)(2,1)}, bf16[8,64,1024]{2,1,0:T(8,128)(2,1)}, u32[]{:S(2)}, u32[]{:S(2)}) collective-permute-start(bf16[8,64,1024]{2,1,0:T(8,128)(2,1)} %constant_dynamic-slice_fusion.11), channel_id=1, source_target_pairs={{0,1},{1,0},{2,3},{3,2},{4,5},{5,4},{6,7},{7,6},{8,9},{9,8},{10,11... | collective-permute-start | bytes 3145736 | tf_op jit(solution)/shard_map/ppermute | solution.py:146
  58.9 57.9 %all-to-all-start.1 = ((bf16[16,512,128]{2,1,0:T(8,128)(2,1)}), bf16[16,512,128]{2,1,0:T(8,128)(2,1)}, u32[]{:S(2)}, u32[]{:S(2)}) async-start(bf16[16,512,128]{2,1,0:T(8,128)(2,1)} %copy-done), calls=%async_computation.1 | async-start | bytes 4194304 | tf_op jit(solution)/shard_map/all_to_all | solution.py:127
  80.0 8.7 %collective-permute-start.3 = (bf16[1024,1024]{1,0:T(8,128)(2,1)}, bf16[1024,1024]{1,0:T(8,128)(2,1)}, u32[]{:S(2)}, u32[]{:S(2)}) collective-permute-start(bf16[1024,1024]{1,0:T(8,128)(2,1)} %get-tuple-element.61.refs_1_.refs_4_), channel_id=1, source_target_pairs={{0,1},{1,0},{2,3},{3,2},{4,5},{5,4},{6,7},{7,6},{8,9},{9,8},{10,11... | collective-permute-start | bytes 6291464 | tf_op jit(solution)/shard_map/ppermute | solution.py:146
  80.0 8.7 %collective-permute-start.4 = (bf16[1024,1024]{1,0:T(8,128)(2,1)}, bf16[1024,1024]{1,0:T(8,128)(2,1)}, u32[]{:S(2)}, u32[]{:S(2)}) collective-permute-start(bf16[1024,1024]{1,0:T(8,128)(2,1)} %get-tuple-element.62.refs_3_.refs_6_), channel_id=1, source_target_pairs={{0,1},{1,0},{2,3},{3,2},{4,5},{5,4},{6,7},{7,6},{8,9},{9,8},{10,11... | collective-permute-start | bytes 6291464 | tf_op jit(solution)/shard_map/ppermute | solution.py:146
  181.7 57.3 %all-to-all-start.2 = ((bf16[16,64,1024]{2,1,0:T(8,128)(2,1)}), bf16[16,64,1024]{2,1,0:T(8,128)(2,1)}, u32[]{:S(2)}, u32[]{:S(2)}) async-start(bf16[16,64,1024]{2,1,0:T(8,128)(2,1)} %bitcast.35), calls=%async_computation.2 | async-start | bytes 4194304 | tf_op jit(solution)/shard_map/all_to_all | solution.py:133
  239.0 7.2 %collective-permute-start.6 = (bf16[1024,1024]{1,0:T(8,128)(2,1)}, bf16[1024,1024]{1,0:T(8,128)(2,1)}, u32[]{:S(2)}, u32[]{:S(2)}) collective-permute-start(bf16[1024,1024]{1,0:T(8,128)(2,1)} %get-tuple-element.85), channel_id=1, source_target_pairs={{0,1},{1,0},{2,3},{3,2},{4,5},{5,4},{6,7},{7,6},{8,9},{9,8},{10,11... | collective-permute-start | bytes 6291464 | tf_op jit(solution)/shard_map/ppermute | solution.py:146
  239.1 7.5 %collective-permute-start.7 = (bf16[1024,1024]{1,0:T(8,128)(2,1)}, bf16[1024,1024]{1,0:T(8,128)(2,1)}, u32[]{:S(2)}, u32[]{:S(2)}) collective-permute-start(bf16[1024,1024]{1,0:T(8,128)(2,1)} %get-tuple-element.87), channel_id=1, source_target_pairs={{0,1},{1,0},{2,3},{3,2},{4,5},{5,4},{6,7},{7,6},{8,9},{9,8},{10,11... | collective-permute-start | bytes 6291464 | tf_op jit(solution)/shard_map/ppermute | solution.py:146
  259.0 56.6 %all-to-all-start.3 = ((bf16[16,64,1024]{2,1,0:T(8,128)(2,1)}), bf16[16,64,1024]{2,1,0:T(8,128)(2,1)S(1)}, u32[]{:S(2)}, u32[]{:S(2)}) async-start(bf16[16,64,1024]{2,1,0:T(8,128)(2,1)} %bitcast.34), calls=%async_computation.3 | async-start | bytes 4194304 | tf_op jit(solution)/shard_map/all_to_all | solution.py:133
  267.4 2.7 collective-permute-start.5
  279.2 46.3 %copy-start.12 = (f32[2,1024,4]{1,2,0:T(4,128)S(1)}, f32[2,1024,4]{1,2,0:T(4,128)}, u32[]{:S(2)}) copy-start(f32[2,1024,4]{1,2,0:T(4,128)} %param.43) | copy-start | bytes 98308
  279.2 1.3 collective-permute-start.8
  280.6 3.8 %collective-permute-start.10 = (f32[4,1024]{1,0:T(4,128)S(1)}, f32[4,1024]{1,0:T(4,128)S(1)}, u32[]{:S(2)}, u32[]{:S(2)}) collective-permute-start(f32[4,1024]{1,0:T(4,128)S(1)} %get-tuple-element.108), channel_id=1, source_target_pairs={{0,4},{2,6},{4,0},{6,2},{8,12},{10,14},{12,8},{14,10},{16,20},{18,... | collective-permute-start | bytes 49160 | tf_op jit(solution)/shard_map/ppermute | solution.py:160
  282.6 13.4 %collective-permute-start.11 = (f32[4,1024]{1,0:T(4,128)S(1)}, f32[4,1024]{1,0:T(4,128)S(1)}, u32[]{:S(2)}, u32[]{:S(2)}) collective-permute-start(f32[4,1024]{1,0:T(4,128)S(1)} %get-tuple-element.107), channel_id=1, source_target_pairs={{0,6},{2,4},{4,2},{6,0},{8,14},{10,12},{12,10},{14,8},{16,22},{18,... | collective-permute-start | bytes 49160 | tf_op jit(solution)/shard_map/ppermute | solution.py:160
  284.1 12.0 %collective-permute-start.9 = (f32[4,1024]{1,0:T(4,128)S(1)}, f32[4,1024]{1,0:T(4,128)S(1)}, u32[]{:S(2)}, u32[]{:S(2)}) collective-permute-start(f32[4,1024]{1,0:T(4,128)S(1)} %get-tuple-element.106), channel_id=1, source_target_pairs={{0,2},{2,0},{4,6},{6,4},{8,10},{10,8},{12,14},{14,12},{16,18},{18,... | collective-permute-start | bytes 49160 | tf_op jit(solution)/shard_map/ppermute | solution.py:160
  296.1 5.4 %collective-permute-start.12 = (f32[4,1024]{1,0:T(4,128)S(1)}, f32[4,1024]{1,0:T(4,128)S(1)}, u32[]{:S(2)}, u32[]{:S(2)}) collective-permute-start(f32[4,1024]{1,0:T(4,128)S(1)} %add_add_fusion.1), channel_id=1, source_target_pairs={{0,8},{2,10},{4,12},{6,14},{8,0},{10,2},{12,4},{14,6},{16,24},{18,... | collective-permute-start | bytes 49160 | tf_op jit(solution)/shard_map/ppermute | solution.py:160
  296.1 19.5 %collective-permute-start.13 = (f32[4,1024]{1,0:T(4,128)S(1)}, f32[4,1024]{1,0:T(4,128)S(1)}, u32[]{:S(2)}, u32[]{:S(2)}) collective-permute-start(f32[4,1024]{1,0:T(4,128)S(1)} %add_add_fusion.1), channel_id=1, source_target_pairs={{0,16},{2,18},{4,20},{6,22},{8,24},{10,26},{12,28},{14,30},{16,0},... | collective-permute-start | bytes 49160 | tf_op jit(solution)/shard_map/ppermute | solution.py:160
  296.2 19.4 %collective-permute-start.14 = (f32[4,1024]{1,0:T(4,128)S(1)}, f32[4,1024]{1,0:T(4,128)S(1)}, u32[]{:S(2)}, u32[]{:S(2)}) collective-permute-start(f32[4,1024]{1,0:T(4,128)S(1)} %add_add_fusion.1), channel_id=1, source_target_pairs={{0,24},{2,26},{4,28},{6,30},{8,16},{10,18},{12,20},{14,22},{16,8},... | collective-permute-start | bytes 49160 | tf_op jit(solution)/shard_map/ppermute | solution.py:160
  315.6 5.1 %collective-permute-start.16 = (f32[4,1024]{1,0:T(4,128)S(1)}, f32[4,1024]{1,0:T(4,128)S(1)}, u32[]{:S(2)}, u32[]{:S(2)}) collective-permute-start(f32[4,1024]{1,0:T(4,128)S(1)} %add_add_fusion), channel_id=1, source_target_pairs={{0,2},{2,0},{4,6},{6,4},{8,10},{10,8},{12,14},{14,12},{16,18},{18,... | collective-permute-start | bytes 49160 | tf_op jit(solution)/shard_map/ppermute | solution.py:160
  317.2 3.7 %collective-permute-start.17 = (f32[4,1024]{1,0:T(4,128)S(1)}, f32[4,1024]{1,0:T(4,128)S(1)}, u32[]{:S(2)}, u32[]{:S(2)}) collective-permute-start(f32[4,1024]{1,0:T(4,128)S(1)} %add_add_fusion), channel_id=1, source_target_pairs={{0,4},{2,6},{4,0},{6,2},{8,12},{10,14},{12,8},{14,10},{16,20},{18,... | collective-permute-start | bytes 49160 | tf_op jit(solution)/shard_map/ppermute | solution.py:160
  318.8 4.6 %collective-permute-start.18 = (f32[4,1024]{1,0:T(4,128)S(1)}, f32[4,1024]{1,0:T(4,128)S(1)}, u32[]{:S(2)}, u32[]{:S(2)}) collective-permute-start(f32[4,1024]{1,0:T(4,128)S(1)} %add_add_fusion), channel_id=1, source_target_pairs={{0,6},{2,4},{4,2},{6,0},{8,14},{10,12},{12,10},{14,8},{16,22},{18,... | collective-permute-start | bytes 49160 | tf_op jit(solution)/shard_map/ppermute | solution.py:160
  320.8 5.4 %collective-permute-start.15 = (bf16[8,64,1024]{2,1,0:T(8,128)(2,1)}, bf16[8,64,1024]{2,1,0:T(8,128)(2,1)S(1)}, u32[]{:S(2)}, u32[]{:S(2)}) collective-permute-start(bf16[8,64,1024]{2,1,0:T(8,128)(2,1)} %constant_dynamic-slice_fusion.4), channel_id=1, source_target_pairs={{0,1},{1,0},{2,3},{3,2},{4,5},{5,4},{6,7},{7,6},{8,9},{9,8},{10,11... | collective-permute-start | bytes 3145736 | tf_op jit(solution)/shard_map/ppermute | solution.py:146
  (25 other events, 219.0 us)
